TPU v7x, 32 devices: a whole 2x2x4 slice. The times are simulated.
32 devices in a mesh: tower: 2 (over x), dp: 16 (over z, y, core).
Axes of the slice: x: 2, y: 2, z: 4, core: 2. Of those that a mesh axis runs over, the one named last changes fastest.
Arguments:
- tokens: bfloat16 [2, 256, 64, 768], P('tower', 'dp'), may hold values from -6 to 6
- segments: int32 [256, 64], P('dp'), may hold values from 0 to 3, never falling along the last dimension, each value on 1 to 32 neighbouring positions
- caption_image: int32 [256, 4], P('dp'), may hold values from 0 to 255
- logit_scale: float32 [1], replicated, may hold values from 30 to 80
- first_gain: bfloat16 [2, 768], P('tower'), may hold values from 0.5 to 1.5
- first_bias: bfloat16 [2, 768], P('tower'), may hold values from -1.1953125 to 1.1953125
- triple_weight: bfloat16 [2, 768, 2304], P('tower'), may hold values from -0.21875 to 0.21875
- query_bias: bfloat16 [2, 768], P('tower'), may hold values from -1.1953125 to 1.1953125
- value_bias: bfloat16 [2, 768], P('tower'), may hold values from -1.1953125 to 1.1953125
- output_weight: bfloat16 [2, 768, 768], P('tower'), may hold values from -0.875 to 0.875
- output_bias: bfloat16 [2, 768], P('tower'), may hold values from -1.1953125 to 1.1953125
- second_gain: bfloat16 [2, 768], P('tower'), may hold values from 0.5 to 1.5
- second_bias: bfloat16 [2, 768], P('tower'), may hold values from -1.1953125 to 1.1953125
- expand_weight: bfloat16 [2, 768, 3072], P('tower'), may hold values from -0.21875 to 0.21875
- expand_bias: bfloat16 [2, 3072], P('tower'), may hold values from -1.1953125 to 1.1953125
- shrink_weight: bfloat16 [2, 3072, 768], P('tower'), may hold values from -0.109375 to 0.109375
- shrink_bias: bfloat16 [2, 768], P('tower'), may hold values from -1.1953125 to 1.1953125
Outputs:
- loss: float32 [1], replicated
- scale_grad: float32 [1], replicated
- input_grad: float32 [2, 256, 64, 768], P('tower', 'dp')
- first_gain_grad: float32 [768], P(('tower', 'dp'))
- first_bias_grad: float32 [768], P(('tower', 'dp'))
- triple_weight_grad: float32 [768, 2304], P(('tower', 'dp'))
- query_bias_grad: float32 [768], P(('tower', 'dp'))
- value_bias_grad: float32 [768], P(('tower', 'dp'))
- output_weight_grad: float32 [768, 768], P(('tower', 'dp'))
- output_bias_grad: float32 [768], P(('tower', 'dp'))
- second_gain_grad: float32 [768], P(('tower', 'dp'))
- second_bias_grad: float32 [768], P(('tower', 'dp'))
- expand_weight_grad: float32 [768, 3072], P(('tower', 'dp'))
- expand_bias_grad: float32 [3072], P(('tower', 'dp'))
- shrink_weight_grad: float32 [3072, 768], P(('tower', 'dp'))
- shrink_bias_grad: float32 [768], P(('tower', 'dp'))
Inputs may be any that keep to these rules, and one draw needn't show every extreme that they name: `segments`: every text row holds captions 0 to 3 in order, each at 1 to 32 positions.
All inputs are finite; a program needn't handle non-finite values.
Results may differ from a plain program's by a relative error of at most 0.012.
The roundings to bfloat16 on the way count: a program that leaves them out, or rounds other values in their place, can miss the bound.
Values may be sent and summed in bfloat16 or wider, within the bound.
A program may use at most 256 MiB of HBM per device.

v0:
```python
import jax
import jax.numpy as jnp
from jax import lax
from jax.sharding import PartitionSpec as P

HEADS = 12
IMG_TOK = 50
CAPS = 4


HIGH = lax.Precision.HIGHEST


def shifted(shard, axis, by):
    peers = lax.axis_size(axis)
    pairs = [(i, i + by) for i in range(peers) if 0 <= i + by < peers]
    return lax.ppermute(shard, axis, pairs)


def layer_stats(values):
    center = values - jnp.mean(values, axis=-1, keepdims=True)
    spread = lax.rsqrt(jnp.mean(center * center, axis=-1, keepdims=True) + 1e-05)
    return (center * spread, spread)


def norm_back(grad_normed, normed, spread):
    return spread * (
        grad_normed
        - jnp.mean(grad_normed, axis=-1, keepdims=True)
        - normed * jnp.mean(grad_normed * normed, axis=-1, keepdims=True)
    )


def masked_scores(queries, key_heads, same_seg):
    raw = (
        jnp.einsum("rqhc,rkhc->rhqk", queries, key_heads, preferred_element_type=jnp.float32)
        * 0.125
    )
    return jnp.where(same_seg, raw, -1e30)


def sum_grads(grads):
    return (
        lax.psum_scatter(grads[0], ("tower", "dp"), scatter_dimension=0, tiled=True),
        lax.psum_scatter(grads[1], ("tower", "dp"), scatter_dimension=0, tiled=True),
        lax.psum_scatter(grads[2], ("tower", "dp"), scatter_dimension=0, tiled=True),
        lax.psum_scatter(grads[3], ("tower", "dp"), scatter_dimension=0, tiled=True),
        lax.psum_scatter(grads[4], ("tower", "dp"), scatter_dimension=0, tiled=True),
        lax.psum_scatter(grads[5], ("tower", "dp"), scatter_dimension=0, tiled=True),
        lax.psum_scatter(grads[6], ("tower", "dp"), scatter_dimension=0, tiled=True),
        lax.psum_scatter(grads[7], ("tower", "dp"), scatter_dimension=0, tiled=True),
        lax.psum_scatter(grads[8], ("tower", "dp"), scatter_dimension=0, tiled=True),
        lax.psum_scatter(grads[9], ("tower", "dp"), scatter_dimension=0, tiled=True),
        lax.psum_scatter(grads[10], ("tower", "dp"), scatter_dimension=0, tiled=True),
        lax.psum_scatter(grads[11], ("tower", "dp"), scatter_dimension=0, tiled=True),
        lax.psum_scatter(grads[12], ("tower", "dp"), scatter_dimension=0, tiled=True),
    )


def local(
    tokens,
    segments,
    caption_image,
    logit_scale,
    first_gain,
    first_bias,
    triple_weight,
    query_bias,
    value_bias,
    output_weight,
    output_bias,
    second_gain,
    second_bias,
    expand_weight,
    expand_bias,
    shrink_weight,
    shrink_bias,
):
    rows_here = tokens.shape[1]
    length = tokens.shape[2]
    features = tokens.shape[3]
    head_size = features // HEADS
    token_count = rows_here * length
    is_text = lax.axis_index("tower") == 1
    text_flag = is_text.astype(jnp.float32)
    position = jnp.arange(length, dtype=jnp.int32)
    image_segs = jnp.broadcast_to(
        (position >= IMG_TOK).astype(jnp.int32)[None, :], (rows_here, length)
    )
    seg_ids = jnp.where(is_text, segments, image_segs)
    same_seg = (seg_ids[:, :, None] == seg_ids[:, None, :])[:, None, :, :]
    head_shape = (rows_here, length, HEADS, head_size)
    gain_one = first_gain[0].astype(jnp.float32)
    shift_one = first_bias[0].astype(jnp.float32)
    triple_w = triple_weight[0]
    query_shift = query_bias[0].astype(jnp.float32)
    value_shift = value_bias[0].astype(jnp.float32)
    output_w = output_weight[0]
    output_shift = output_bias[0].astype(jnp.float32)
    gain_two = second_gain[0].astype(jnp.float32)
    shift_two = second_bias[0].astype(jnp.float32)
    expand_w = expand_weight[0]
    expand_shift = expand_bias[0].astype(jnp.float32)
    shrink_w = shrink_weight[0]
    shrink_shift = shrink_bias[0].astype(jnp.float32)
    inputs = tokens[0].reshape(token_count, features).astype(jnp.float32)
    normed_a, spread_a = layer_stats(inputs)
    normed_one = (normed_a * gain_one + shift_one).astype(jnp.bfloat16)
    triple = jnp.dot(normed_one, triple_w, preferred_element_type=jnp.float32)
    queries = (triple[:, :features] + query_shift).astype(jnp.bfloat16).reshape(head_shape)
    key_heads = triple[:, features : 2 * features].astype(jnp.bfloat16).reshape(head_shape)
    value_heads = (triple[:, 2 * features :] + value_shift).astype(jnp.bfloat16).reshape(head_shape)
    scores = masked_scores(queries, key_heads, same_seg)
    row_peak = jnp.max(scores, axis=-1, keepdims=True)
    log_total = row_peak + jnp.log(jnp.sum(jnp.exp(scores - row_peak), axis=-1, keepdims=True))
    attn_probs = jnp.exp(scores - log_total)
    mixed_low = (
        jnp.einsum(
            "rhqk,rkhc->rqhc",
            attn_probs.astype(jnp.bfloat16),
            value_heads,
            preferred_element_type=jnp.float32,
        )
        .reshape(token_count, features)
        .astype(jnp.bfloat16)
    )
    hidden = (
        inputs + jnp.dot(mixed_low, output_w, preferred_element_type=jnp.float32) + output_shift
    )
    normed_b, spread_b = layer_stats(hidden)
    normed_two = (normed_b * gain_two + shift_two).astype(jnp.bfloat16)
    expanded = jnp.dot(normed_two, expand_w, preferred_element_type=jnp.float32) + expand_shift
    activated, gelu_back = jax.vjp(jax.nn.gelu, expanded)
    active_low = activated.astype(jnp.bfloat16)
    block_out = (
        hidden + jnp.dot(active_low, shrink_w, preferred_element_type=jnp.float32) + shrink_shift
    )
    slot_ids = jnp.arange(CAPS, dtype=jnp.int32)
    member = (seg_ids[:, None, :] == slot_ids[None, :, None]).astype(jnp.float32)
    counts = jnp.maximum(jnp.sum(member, axis=2), 1.0)
    pooled = (
        jnp.einsum(
            "rst,rtd->rsd", member, block_out.reshape(rows_here, length, features), precision=HIGH
        )
        / counts[:, :, None]
    )
    inverse = lax.rsqrt(jnp.sum(pooled * pooled, axis=2, keepdims=True) + 1e-06)
    embedding = pooled * inverse
    first_slot = embedding[:, 0, :].astype(jnp.bfloat16)
    collected = lax.all_gather(first_slot, "dp", axis=0, tiled=True)
    image_table = shifted(collected, "tower", 1)
    text_low = embedding.reshape(rows_here * CAPS, features).astype(jnp.bfloat16)
    similar = jnp.einsum("cd,id->ci", text_low, image_table, preferred_element_type=jnp.float32)
    factor = logit_scale[0]
    logits = factor * similar
    logit_peak = jnp.max(logits, axis=1, keepdims=True)
    logit_total = logit_peak + jnp.log(jnp.sum(jnp.exp(logits - logit_peak), axis=1, keepdims=True))
    targets = caption_image.reshape(-1)
    image_ids = jnp.arange(image_table.shape[0], dtype=jnp.int32)
    target_hot = (image_ids[None, :] == targets[:, None]).astype(jnp.float32)
    picked = jnp.sum(logits * target_hot, axis=1)
    loss_here = jnp.sum(logit_total[:, 0] - picked) * text_flag
    grad_logits = (jnp.exp(logits - logit_total) - target_hot) * text_flag
    factor_here = jnp.sum(grad_logits * similar)
    loss_total, factor_total = lax.psum((loss_here, factor_here), ("tower", "dp"))
    caption_total = rows_here * CAPS * lax.axis_size("dp")
    grad_dots = (factor * grad_logits).astype(jnp.bfloat16)
    grad_emb = jnp.einsum(
        "ci,id->cd", grad_dots, image_table, preferred_element_type=jnp.float32
    ).reshape(rows_here, CAPS, features)
    grad_pooled = inverse * (
        grad_emb - embedding * jnp.sum(embedding * grad_emb, axis=2, keepdims=True)
    )
    grad_pooled = grad_pooled / counts[:, :, None]
    grad_out = jnp.einsum("rst,rsd->rtd", member, grad_pooled, precision=HIGH).reshape(
        token_count, features
    )
    shrink_bias_grad = jnp.sum(grad_out, axis=0)
    grad_out_low = grad_out.astype(jnp.bfloat16)
    shrink_weight_grad = jnp.einsum(
        "nf,nd->fd", active_low, grad_out_low, preferred_element_type=jnp.float32
    )
    grad_active = jnp.einsum(
        "nd,fd->nf", grad_out_low, shrink_w, preferred_element_type=jnp.float32
    )
    grad_expanded = gelu_back(grad_active)[0]
    expand_bias_grad = jnp.sum(grad_expanded, axis=0)
    grad_expanded_low = grad_expanded.astype(jnp.bfloat16)
    expand_weight_grad = jnp.einsum(
        "nd,nf->df", normed_two, grad_expanded_low, preferred_element_type=jnp.float32
    )
    grad_normed_two = jnp.einsum(
        "nf,df->nd", grad_expanded_low, expand_w, preferred_element_type=jnp.float32
    )
    second_gain_grad = jnp.sum(grad_normed_two * normed_b, axis=0)
    second_bias_grad = jnp.sum(grad_normed_two, axis=0)
    grad_hidden = grad_out + norm_back(grad_normed_two * gain_two, normed_b, spread_b)
    output_bias_grad = jnp.sum(grad_hidden, axis=0)
    grad_hidden_low = grad_hidden.astype(jnp.bfloat16)
    output_weight_grad = jnp.einsum(
        "nd,ne->de", mixed_low, grad_hidden_low, preferred_element_type=jnp.float32
    )
    grad_mixed = (
        jnp.einsum("ne,de->nd", grad_hidden_low, output_w, preferred_element_type=jnp.float32)
        .astype(jnp.bfloat16)
        .reshape(head_shape)
    )
    scores_again = masked_scores(queries, key_heads, same_seg)
    probs_again = jnp.exp(scores_again - log_total)
    probs_low = probs_again.astype(jnp.bfloat16)
    grad_values = jnp.einsum(
        "rhqk,rqhc->rkhc", probs_low, grad_mixed, preferred_element_type=jnp.float32
    )
    grad_probs = jnp.einsum(
        "rqhc,rkhc->rhqk", grad_mixed, value_heads, preferred_element_type=jnp.float32
    )
    grad_scores = (
        probs_again * (grad_probs - jnp.sum(probs_again * grad_probs, axis=-1, keepdims=True))
    ).astype(jnp.bfloat16)
    grad_queries = (
        jnp.einsum("rhqk,rkhc->rqhc", grad_scores, key_heads, preferred_element_type=jnp.float32)
        * 0.125
    )
    grad_keys = (
        jnp.einsum("rhqk,rqhc->rkhc", grad_scores, queries, preferred_element_type=jnp.float32)
        * 0.125
    )
    grad_queries = grad_queries.reshape(token_count, features)
    grad_keys = grad_keys.reshape(token_count, features)
    grad_values = grad_values.reshape(token_count, features)
    query_bias_grad = jnp.sum(grad_queries, axis=0)
    value_bias_grad = jnp.sum(grad_values, axis=0)
    grad_triple = jnp.concatenate([grad_queries, grad_keys, grad_values], axis=1).astype(
        jnp.bfloat16
    )
    triple_weight_grad = jnp.einsum(
        "nd,ne->de", normed_one, grad_triple, preferred_element_type=jnp.float32
    )
    grad_normed_one = jnp.einsum(
        "ne,de->nd", grad_triple, triple_w, preferred_element_type=jnp.float32
    )
    first_gain_grad = jnp.sum(grad_normed_one * normed_a, axis=0)
    first_bias_grad = jnp.sum(grad_normed_one, axis=0)
    input_grad = grad_hidden + norm_back(grad_normed_one * gain_one, normed_a, spread_a)
    shares = sum_grads(
        (
            first_gain_grad,
            first_bias_grad,
            triple_weight_grad,
            query_bias_grad,
            value_bias_grad,
            output_weight_grad,
            output_bias_grad,
            second_gain_grad,
            second_bias_grad,
            expand_weight_grad,
            expand_bias_grad,
            shrink_weight_grad,
            shrink_bias_grad,
        )
    )
    loss_out = (loss_total / caption_total).reshape(1)
    factor_out = factor_total.reshape(1)
    return (
        loss_out,
        factor_out,
        input_grad.reshape(1, rows_here, length, features),
        shares[0],
        shares[1],
        shares[2],
        shares[3],
        shares[4],
        shares[5],
        shares[6],
        shares[7],
        shares[8],
        shares[9],
        shares[10],
        shares[11],
        shares[12],
    )


def solution(mesh):
    placed = (
        P("tower", "dp", None, None),
        P("dp", None),
        P("dp", None),
        P(),
        P("tower", None),
        P("tower", None),
        P("tower", None, None),
        P("tower", None),
        P("tower", None),
        P("tower", None, None),
        P("tower", None),
        P("tower", None),
        P("tower", None),
        P("tower", None, None),
        P("tower", None),
        P("tower", None, None),
        P("tower", None),
    )
    return jax.shard_map(
        local,
        mesh=mesh,
        in_specs=placed,
        out_specs=(
            P(),
            P(),
            P("tower", "dp", None, None),
            P(("tower", "dp")),
            P(("tower", "dp")),
            P(("tower", "dp"), None),
            P(("tower", "dp")),
            P(("tower", "dp")),
            P(("tower", "dp"), None),
            P(("tower", "dp")),
            P(("tower", "dp")),
            P(("tower", "dp")),
            P(("tower", "dp"), None),
            P(("tower", "dp")),
            P(("tower", "dp"), None),
            P(("tower", "dp")),
        ),
        check_vma=False,
    )
```

profile of v0, /device:TPU:0, one launch (start us, length us, event | category | flops | bytes accessed | tf_op | source)
XLA Modules:
  0.0 729.7 jit_solution(6723709632042836295)
XLA Ops:
  24.7 6.1 reshape.236
  36.5 5.9 reshape.247
  42.4 6.5 copy.83
  48.9 5.9 reshape.246
  70.4 5.8 convert_element_type.126
  81.0 8.7 %fusion.14 = f32[1024,3072]{1,0:T(8,128)S(1)} fusion(bf16[1,768,3072]{2,1,0:T(8,128)(2,1)} %param.30, f32[1024,768]{1,0:T(8,128)S(1)} %get-tuple-element.48, f32[768]{0:T(1024)S(1)} %get-tuple-element.67, f32[768]{0:T(1024)S(1)} %get-tuple-element.68, f32[1024]{0:T(1024)S(1)} %add_rsqrt_fusion.2, f32[1024]{0:T(1024)S(1)} %broadcast_multiply_fusion.5), kind=kOutput, calls=%fused_computation.27 | convolution fusion | flops 4835770368 | bytes 20461568 | tf_op jit(solution)/shard_map/dot_general | solution.py:132
  89.7 7.8 %add_add_fusion = f32[1024,768]{1,0:T(8,128)S(1)} fusion(f32[1024,768]{1,0:T(8,128)S(1)} %get-tuple-element.48, bf16[1,3072,768]{2,1,0:T(8,128)(2,1)S(1)} %bitcast.131, f32[768]{0:T(1024)S(1)} %copy-done.42, f32[1024,3072]{1,0:T(8,128)S(1)} %fusion.14, f32[3072]{0:T(1024)S(1)} %bitcast.128), kind=kOutput, calls=%fused_computation.70 | convolution fusion | flops 4864868352 | bytes 23608320 | tf_op jit(solution)/shard_map/dot_general | solution.py:136
  100.3 25.7 %all-gather = bf16[256,1,768]{2,0,1:T(8,128)(2,1)} all-gather(bf16[16,1,768]{2,0,1:T(8,128)(2,1)S(1)} %copy.75), channel_id=2, replica_groups=mesh['tower'=2,'dp'=16] {'dp'}, dimensions={0}, use_global_device_ids=true | all-gather | bytes 417792 | tf_op jit(solution)/shard_map/all_gather | solution.py:150
  150.5 15.8 %fusion.85 = (f32[3072]{0:T(1024)}, bf16[1024,3072]{1,0:T(8,128)(2,1)S(1)}) fusion(f32[1024,3072]{1,0:T(8,128)} %copy-done.49, f32[3072]{0:T(1024)S(1)} %bitcast.129, bf16[1024,768]{1,0:T(8,128)(2,1)S(1)} %bitcast.126, bf16[1,3072,768]{2,1,0:T(8,128)(2,1)} %param.32), kind=kOutput, calls=%fused_computation.151 | convolution fusion | flops 4901041152 | bytes 25190400 | tf_op jit(solution)/shard_map/nd,fd->nf/dot_general | solution.py:183
  166.4 11.0 %multiply_reduce_fusion.1 = (f32[768]{0:T(1024)}, f32[1024]{0:T(1024)S(1)}, f32[1024]{0:T(1024)S(1)}, f32[768]{0:T(1024)}, f32[1024,768]{1,0:T(8,128)S(1)}) fusion(f32[1024,768]{1,0:T(8,128)S(1)} %copy-done.3, f32[1024]{0:T(1024)S(1)} %add_rsqrt_fusion.2, f32[1024]{0:T(1024)S(1)} %broadcast_multiply_fusion.5, f32[768]{0:T(1024)S(1)} %copy-done.25, ...), kind=kOutput, calls=%fused_computation.65 | convolution fusion | flops 4838912000 | bytes 17327104 | tf_op jit(solution)/shard_map/nf,df->nd/dot_general | solution.py:192
  188.8 6.1 reshape.237
  194.9 12.3 %multiply_reduce_fusion = (f32[16,12,64]{2,1,0:T(8,128)}, f32[16,12,64,64]{2,3,1,0:T(8,128)}) fusion(f32[16,12,64,64]{2,3,1,0:T(8,128)} %copy-done.1, f32[16,12,64]{2,1,0:T(8,128)} %copy-done.17, pred[16,64,64]{1,2,0:T(8,128)(4,1)} %broadcast_compare_fusion, bf16[16,64,12,64]{3,2,1,0:T(8,128)(2,1)} %reshape.246, bf16[16,64,12,64]{3,2,1,0:T(8,128)(2,1)} %reshape.237), kind=kOutput, calls=%fused_computation.16 | convolution fusion | flops 104583168 | bytes 9601024 | tf_op jit(solution)/shard_map/rqhc,rkhc->rhqk/dot_general | solution.py:214
  207.2 8.3 %bitcast_convert_fusion = (bf16[16,64,12,64]{3,1,2,0:T(8,128)(2,1)}, f32[16,12,64,64]{2,3,1,0:T(8,128)}) fusion(bf16[16,64,12,64]{3,2,1,0:T(8,128)(2,1)S(1)} %copy-done.5, f32[16,12,64,64]{2,3,1,0:T(8,128)} %copy-done.1, f32[16,12,64]{2,1,0:T(8,128)S(1)} %copy-done.18, pred[16,64,64]{1,2,0:T(8,128)(4,1)S(1)} %copy-done.16), kind=kOutput, calls=%fused_computation.11 | convolution fusion | flops 104595456 | bytes 9551872 | tf_op jit(solution)/shard_map/rhqk,rqhc->rkhc/dot_general | solution.py:211
  215.6 6.0 multiply_convert_fusion.2
  246.5 8.5 %bitcast_convert_fusion.1 = (bf16[16,64,12,64]{3,1,2,0:T(8,128)(2,1)}, f32[16,12,64,64]{2,3,1,0:T(8,128)}) fusion(bf16[16,12,64,64]{2,3,1,0:T(8,128)(2,1)} %copy-done.4, bf16[16,64,12,64]{3,2,1,0:T(8,128)(2,1)} %reshape.236), kind=kOutput, calls=%fused_computation.13 | convolution fusion | flops 102236160 | bytes 7864320 | tf_op jit(solution)/shard_map/rhqk,rkhc->rqhc/dot_general | solution.py:221
  260.2 5.8 reshape.221
  269.4 7.0 fusion.42
  276.4 6.0 fusion.86
  282.5 13.4 %fusion.82 = f32[3072,768]{1,0:T(8,128)} fusion(bf16[1024,768]{1,0:T(8,128)(2,1)} %get-tuple-element.41, f32[1024,3072]{1,0:T(8,128)} %copy-done.49, f32[3072]{0:T(1024)} %bitcast.127), kind=kOutput, calls=%fused_computation.148 | convolution fusion | flops 4863295488 | bytes 23605248 | tf_op jit(solution)/shard_map/nf,nd->fd/dot_general | solution.py:180
  296.5 11.2 %fusion.45 = f32[768,3072]{1,0:T(8,128)} fusion(bf16[1024,3072]{1,0:T(8,128)(2,1)} %copy-done.11, f32[1024,768]{1,0:T(8,128)} %copy-done.2, f32[768]{0:T(1024)S(1)} %copy-done.28, f32[768]{0:T(1024)S(1)} %copy-done.25, f32[1024]{0:T(1024)S(1)} %add_rsqrt_fusion.2, f32[1024]{0:T(1024)S(1)} %broadcast_multiply_fusion.5), kind=kOutput, calls=%fused_computation.67 | convolution fusion | flops 4835770368 | bytes 18888704 | tf_op jit(solution)/shard_map/nd,nf->df/dot_general | solution.py:189
  319.7 39.3 %all-reduce.9 = (f32[]{:T(128)}, f32[1]{0:T(128)}, f32[768]{0:T(1024)}, f32[768]{0:T(1024)}, f32[768]{0:T(1024)}, /*index=5*/f32[768]{0:T(1024)}, f32[768]{0:T(1...) all-reduce(f32[]{:T(128)S(6)} %mul.254, ...), channel_id=1, replica_groups=mesh['tower'=2,'dp'=16] {'tower','dp'}, use_global_device_ids=true, to_apply=%region_12.13 | all-reduce | flops 9218 | bytes 73744 | tf_op jit(solution)/shard_map/psum | solution.py:165
  376.3 62.1 %reduce-scatter.5.cloned.1.call-done = f32[24,2304]{1,0:T(8,128)} async-done(((f32[768,2304]{1,0:T(8,128)}), f32[24,2304]{1,0:T(8,128)}) %reduce-scatter.5.cloned.1.call-update) | async-done | bytes 221200 | tf_op jit(solution)/shard_map/reduce_scatter | solution.py:46
  438.4 141.5 %reduce-scatter.11.cloned.1.call-done = f32[96,768]{1,0:T(8,128)} async-done(((f32[3072,768]{1,0:T(8,128)}), f32[96,768]{1,0:T(8,128)}) %reduce-scatter.11.cloned.1.call-update) | async-done | bytes 294928 | tf_op jit(solution)/shard_map/reduce_scatter | solution.py:55
  579.9 141.9 %reduce-scatter.9.cloned.1.call-done = f32[24,3072]{1,0:T(8,128)} async-done(((f32[768,3072]{1,0:T(8,128)}), f32[24,3072]{1,0:T(8,128)}) %reduce-scatter.9.cloned.1.call-update) | async-done | bytes 294928 | tf_op jit(solution)/shard_map/reduce_scatter | solution.py:53
  (194 shorter events, 143.3 us)
Async XLA Ops:
  7.2 8.8 %copy-start = (bf16[1,768,2304]{2,1,0:T(8,128)(2,1)S(1)}, bf16[1,768,2304]{2,1,0:T(8,128)(2,1)}, u32[]{:S(2)}) copy-start(bf16[1,768,2304]{2,1,0:T(8,128)(2,1)} %param.23) | copy-start | bytes 10616836
  7.2 8.0 %copy-start.43 = (bf16[1,768]{1,0:T(2,128)(2,1)S(1)}, bf16[1,768]{1,0:T(2,128)(2,1)}, u32[]{:S(2)}) copy-start(bf16[1,768]{1,0:T(2,128)(2,1)} %param.22) | copy-start | bytes 4612
  7.2 369.1 %reduce-scatter.7.cloned.1.call-start = ((), (), s32[]{:S(2)}) async-start(), calls=%async_computation.5 | async-start | bytes 2433024 | tf_op jit(solution)/shard_map/reduce_scatter | solution.py:49
  7.3 7.9 %copy-start.44 = (bf16[1,768]{1,0:T(2,128)(2,1)S(1)}, bf16[1,768]{1,0:T(2,128)(2,1)}, u32[]{:S(2)}) copy-start(bf16[1,768]{1,0:T(2,128)(2,1)} %param.21) | copy-start | bytes 4612
  7.3 8.0 %copy-start.6 = (bf16[1,16,64,768]{3,2,1,0:T(8,128)(2,1)S(1)}, bf16[1,16,64,768]{3,2,1,0:T(8,128)(2,1)}, u32[]{:S(2)}) copy-start(bf16[1,16,64,768]{3,2,1,0:T(8,128)(2,1)} %param.17) | copy-start | bytes 4718596
  80.1 9.5 %copy-start.2 = (f32[1024,768]{1,0:T(8,128)}, f32[1024,768]{1,0:T(8,128)S(1)}, u32[]{:S(2)}) copy-start(f32[1024,768]{1,0:T(8,128)S(1)} %get-tuple-element.48) | copy-start | bytes 9437188
  80.2 9.5 %slice-start = ((s8[4718592]{0:T(1024)(128)(4,1)}), s8[4194304]{0:T(1024)(128)(4,1)S(1)}, s32[]{:S(2)}) async-start(s8[4718592]{0:T(1024)(128)(4,1)} %bitcast.130), calls=%async_computation.8 | async-start | bytes 8388608
  80.9 8.7 %copy-start.24 = (f32[768]{0:T(1024)}, f32[768]{0:T(1024)S(1)}, u32[]{:S(2)}) copy-start(f32[768]{0:T(1024)S(1)} %get-tuple-element.68) | copy-start | bytes 9220
  80.9 8.7 %copy-start.27 = (f32[768]{0:T(1024)}, f32[768]{0:T(1024)S(1)}, u32[]{:S(2)}) copy-start(f32[768]{0:T(1024)S(1)} %get-tuple-element.67) | copy-start | bytes 9220
  80.9 8.8 %copy-start.40 = (f32[1,3072]{1,0:T(1,128)S(1)}, f32[1,3072]{1,0:T(1,128)}, u32[]{:S(2)}) copy-start(f32[1,3072]{1,0:T(1,128)} %add.237) | copy-start | bytes 36868
  80.9 8.8 %copy-start.42 = (f32[768]{0:T(1024)S(1)}, f32[768]{0:T(1024)}, u32[]{:S(2)}) copy-start(f32[768]{0:T(1024)} %convert_reduce_fusion.2) | copy-start | bytes 9220
  80.9 8.8 %slice-start.1 = ((s8[4718592]{0:T(1024)(128)(4,1)}), s8[524288]{0:T(1024)(128)(4,1)S(1)}, s32[]{:S(2)}) async-start(s8[4718592]{0:T(1024)(128)(4,1)} %bitcast.130), calls=%async_computation.9 | async-start | bytes 1048576
  126.0 13.4 %collective-permute-start = (bf16[256,768]{1,0:T(8,128)(2,1)}, bf16[256,768]{1,0:T(8,128)(2,1)}, u32[]{:S(2)}, u32[]{:S(2)}) collective-permute-start(bf16[256,768]{1,0:T(8,128)(2,1)} %bitcast.10), channel_id=1, source_target_pairs={{0,16},{1,17},{2,18},{3,19},{4,20},{5,21},{6,22},{7,23},{8,24},{9,... | collective-permute-start | bytes 1179656 | tf_op jit(solution)/shard_map/ppermute | solution.py:17
  150.5 15.8 %copy-start.3 = (f32[1024,768]{1,0:T(8,128)S(1)}, f32[1024,768]{1,0:T(8,128)}, u32[]{:S(2)}) copy-start(f32[1024,768]{1,0:T(8,128)} %copy-done.2) | copy-start | bytes 9437188
  150.5 15.8 %copy-start.25 = (f32[768]{0:T(1024)S(1)}, f32[768]{0:T(1024)}, u32[]{:S(2)}) copy-start(f32[768]{0:T(1024)} %copy-done.24) | copy-start | bytes 9220
  166.4 11.0 %copy-start.11 = (bf16[1024,3072]{1,0:T(8,128)(2,1)}, bf16[1024,3072]{1,0:T(8,128)(2,1)S(1)}, u32[]{:S(2)}) copy-start(bf16[1024,3072]{1,0:T(8,128)(2,1)S(1)} %get-tuple-element.62) | copy-start | bytes 18874372
  194.9 12.3 %copy-start.5 = (bf16[16,64,12,64]{3,2,1,0:T(8,128)(2,1)S(1)}, bf16[16,64,12,64]{3,2,1,0:T(8,128)(2,1)}, u32[]{:S(2)}) copy-start(bf16[16,64,12,64]{3,2,1,0:T(8,128)(2,1)} %reshape.237) | copy-start | bytes 4718596
  194.9 12.3 %copy-start.16 = (pred[16,64,64]{1,2,0:T(8,128)(4,1)S(1)}, pred[16,64,64]{1,2,0:T(8,128)(4,1)}, u32[]{:S(2)}) copy-start(pred[16,64,64]{1,2,0:T(8,128)(4,1)} %broadcast_compare_fusion) | copy-start | bytes 196612
  194.9 12.3 %copy-start.18 = (f32[16,12,64]{2,1,0:T(8,128)S(1)}, f32[16,12,64]{2,1,0:T(8,128)}, u32[]{:S(2)}) copy-start(f32[16,12,64]{2,1,0:T(8,128)} %copy-done.17) | copy-start | bytes 147460
  215.6 222.9 %reduce-scatter.5.cloned.1.call-start = ((), (), s32[]{:S(2)}) async-start(), calls=%async_computation.4 | async-start | bytes 7299072 | tf_op jit(solution)/shard_map/reduce_scatter | solution.py:46
  282.4 297.5 %reduce-scatter.11.cloned.1.call-start = ((), (), s32[]{:S(2)}) async-start(), calls=%async_computation.7 | async-start | bytes 9732096 | tf_op jit(solution)/shard_map/reduce_scatter | solution.py:55
  295.9 426.0 %reduce-scatter.9.cloned.1.call-start = ((), (), s32[]{:S(2)}) async-start(), calls=%async_computation.6 | async-start | bytes 9732096 | tf_op jit(solution)/shard_map/reduce_scatter | solution.py:53
  312.0 59.1 %copy-start.31 = (f32[768]{0:T(1024)S(1)}, f32[768]{0:T(1024)}, u32[]{:S(2)}) copy-start(f32[768]{0:T(1024)} %copy-done.29) | copy-start | bytes 9220
  312.0 59.1 %copy-start.35 = (f32[1024]{0:T(1024)S(1)}, f32[1024]{0:T(1024)}, u32[]{:S(2)}) copy-start(f32[1024]{0:T(1024)} %div.54) | copy-start | bytes 12292
  (33 other events, 87.6 us)
Sparse Core Ops, SparseCore 0:
  215.7 97.2 reduce-scatter.6
  320.2 118.1 reduce-scatter.4
  444.9 134.9 reduce-scatter.10
  587.2 134.5 reduce-scatter.8
where the time goes:
time: 741 us; the launch traced here: 730 us
  waiting for transfers between devices  346 us (47%)
  matrix products  142 us (19%)
  local copies, waits for them, and re-layouts  108 us (15%)
  blocking collectives  65.1 us (9%)
  other arithmetic  45.7 us (6%)
  between operations  17.8 us (2%)
    reduce_scatter x1, waiting for transfers between devices, sum_grads(): lax.psum_scatter(grads[9], ('tower', 'dp'), scatter_dimension=0, tiled=True)  142 us
    reduce_scatter x1, waiting for transfers between devices, sum_grads(): lax.psum_scatter(grads[11], ('tower', 'dp'), scatter_dimension=0, tiled=T...  141 us
    reduce_scatter x1, waiting for transfers between devices, sum_grads(): lax.psum_scatter(grads[2], ('tower', 'dp'), scatter_dimension=0, tiled=True)  62.1 us
    psum x1, blocking collectives, local(): lax.psum((loss_here, factor_here), ('tower', 'dp'))  39.3 us
    all_gather x1, blocking collectives, local(): collected = lax.all_gather(first_slot, 'dp', axis=0, tiled=True)  25.7 us
    unnamed x116, local copies, waits for them, and re-layouts  24.9 us
    dot_general x1, matrix products, local(): jnp.einsum('nd,fd->nf', grad_out_low, shrink_w, preferred_element_type=jn...  15.8 us
  transfers between devices with their start and end apart: 5, of which 4 were waited for; matrix products, arithmetic and copies ran while one was open for 17% of the time, Pallas kernels for 0%

commit v1 on v0

--- a/solution.py
+++ b/solution.py
@@ -1,11 +1,806 @@
+import functools
+
 import jax
 import jax.numpy as jnp
 from jax import lax
+from jax.experimental import pallas as pl
+from jax.experimental.pallas import tpu as pltpu
 from jax.sharding import PartitionSpec as P
 
 HEADS = 12
 IMG_TOK = 50
 CAPS = 4
+
+f32, bf16 = jnp.float32, jnp.bfloat16
+GELU_C = 0.7978845608028654
+GELU_A = 0.044715
+STEP_ROWS = 4
+
+
+def mm(a, b):
+    return jnp.dot(a, b, preferred_element_type=f32)
+
+
+def mm_nt(a, b):
+    return lax.dot_general(a, b, (((1,), (1,)), ((), ())), preferred_element_type=f32)
+
+
+def mm_tn(a, b):
+    return lax.dot_general(a, b, (((0,), (0,)), ((), ())), preferred_element_type=f32)
+
+
+def stats(x):
+    center = x - jnp.mean(x, axis=-1, keepdims=True)
+    spread = lax.rsqrt(jnp.mean(center * center, axis=-1, keepdims=True) + 1e-05)
+    return center * spread, spread
+
+
+def low_pair(x):
+    high = x.astype(bf16)
+    return high, (x - high.astype(f32)).astype(bf16)
+
+
+def fwd_kernel(tok, seg, g1, b1, qb, vb, ob, g2, b2, eb, sb, w3h, woh, weh, wsh,
+               qkv, probs, mixed, hidden, act, slope, member_out, pooled_out, count_out,
+               w3, wo, we, ws, pool_acc, count_acc, sems):
+    i = pl.program_id(0)
+    steps = pl.num_programs(0)
+    rows_here, length = seg.shape
+    slots = rows_here * CAPS
+    feat = tok.shape[1]
+    block = tok.shape[0]
+    is_text = lax.axis_index("tower") == 1
+    copies = [pltpu.make_async_copy(src, dst, sems.at[n])
+              for n, (src, dst) in enumerate(((w3h, w3), (woh, wo), (weh, we), (wsh, ws)))]
+
+    @pl.when(i == 0)
+    def _():
+        for c in copies:
+            c.start()
+        pool_acc[...] = jnp.zeros_like(pool_acc)
+        count_acc[...] = jnp.zeros_like(count_acc)
+
+    def arrive(n):
+        @pl.when(i == 0)
+        def _():
+            copies[n].wait()
+
+    x = tok[...].astype(f32)
+    norm, _ = stats(x)
+    n1 = (norm * g1[...].astype(f32) + b1[...].astype(f32)).astype(bf16)
+    arrive(0)
+    qkv[:, :feat] = (mm(n1, w3[:, :feat]) + qb[...].astype(f32)).astype(bf16)
+    qkv[:, feat:2 * feat] = mm(n1, w3[:, feat:2 * feat]).astype(bf16)
+    qkv[:, 2 * feat:] = (mm(n1, w3[:, 2 * feat:]) + vb[...].astype(f32)).astype(bf16)
+
+    image_seg = (lax.broadcasted_iota(jnp.int32, (1, length), 1) >= IMG_TOK).astype(jnp.int32)
+    row_segs = []
+    for r in range(STEP_ROWS):
+        s = seg[pl.ds(STEP_ROWS * i + r, 1), :]
+        row_segs.append(jnp.where(is_text, s, image_seg))
+    lane = lax.broadcasted_iota(jnp.int32, (128, 128), 1)
+    first_half = lane < 64
+    slot_lanes = []
+    for pair in range(STEP_ROWS // 2):
+        base = STEP_ROWS * i + 2 * pair
+        keyed = jnp.concatenate(
+            [row_segs[2 * pair] * rows_here + base, row_segs[2 * pair + 1] * rows_here + (base + 1)], axis=1)
+        slot_lanes.append(keyed)
+        across = jnp.broadcast_to(keyed.astype(f32), (128, 128))
+        bias = jnp.where(across == across.T, 0.0, -1e30)
+        bias = jnp.concatenate([bias, bias], axis=0)
+        t0 = pair * 128
+        for hp in range(HEADS // 2):
+            c0 = hp * 128
+            q = qkv[t0:t0 + 128, c0:c0 + 128] * jnp.asarray(0.125, bf16)
+            k = qkv[t0:t0 + 128, feat + c0:feat + c0 + 128]
+            v = qkv[t0:t0 + 128, 2 * feat + c0:2 * feat + c0 + 128]
+            zero = jnp.zeros_like(q)
+            q2 = jnp.concatenate([jnp.where(first_half, q, zero), jnp.where(first_half, zero, q)], axis=0)
+            s = mm_nt(q2, k) + bias
+            e = jnp.exp(s - jnp.max(s, axis=-1, keepdims=True))
+            p = (e * (1.0 / jnp.sum(e, axis=-1, keepdims=True))).astype(bf16)
+            probs[256 * pair:256 * (pair + 1), c0:c0 + 128] = p
+            o = mm(p, v)
+            mixed[t0:t0 + 128, c0:c0 + 128] = jnp.where(first_half, o[:128], o[128:]).astype(bf16)
+
+    arrive(1)
+    hid = x + mm(mixed[...], wo[...]) + ob[...].astype(f32)
+    hidden[...] = hid
+    norm2, _ = stats(hid)
+    n2 = (norm2 * g2[...].astype(f32) + b2[...].astype(f32)).astype(bf16)
+    arrive(2)
+    arrive(3)
+    out = hid + sb[...].astype(f32)
+    tile = 768
+    for f in range(0, we.shape[1], tile):
+        v = mm(n2, we[:, f:f + tile]) + eb[:, f:f + tile].astype(f32)
+        v2 = v * v
+        cv = v * GELU_C
+        t = jnp.tanh(cv * (1.0 + GELU_A * v2))
+        h = 0.5 + 0.5 * t
+        a = (v * h).astype(bf16)
+        act[:, f:f + tile] = a
+        slope[:, f:f + tile] = (h + h * (1.0 - h) * ((2.0 * cv) * (1.0 + (3.0 * GELU_A) * v2))).astype(bf16)
+        out = out + mm(a, ws[f:f + tile, :])
+    slot_row = jnp.concatenate(slot_lanes, axis=1)
+    hot = (lax.broadcasted_iota(jnp.int32, (slots, block), 0) == slot_row)
+    member = hot.astype(f32).astype(bf16)
+    member_out[...] = member
+    out_hi, out_lo = low_pair(out)
+    pool_acc[...] += mm(member, out_hi) + mm(member, out_lo)
+    count_acc[...] += jnp.broadcast_to(jnp.sum(hot.astype(f32), axis=1, keepdims=True), count_acc.shape)
+
+    @pl.when(i == steps - 1)
+    def _():
+        counts = jnp.maximum(count_acc[...], 1.0)
+        count_out[...] = counts
+        pooled_out[...] = pool_acc[...] / counts[:, :1]
+
+
+def forward(tokens, segments, g1, b1, w3, qb, vb, wo, ob, g2, b2, we, eb, ws, sb):
+    count, feat = tokens.shape
+    rows_here, length = segments.shape
+    slots = rows_here * CAPS
+    ff = we.shape[1]
+    block = STEP_ROWS * length
+    steps = count // block
+    pairs = STEP_ROWS // 2
+    whole = lambda a: pl.BlockSpec(a.shape, lambda i: (0,) * a.ndim)
+    rows = lambda width: pl.BlockSpec((block, width), lambda i: (i, 0))
+    anyw = pl.BlockSpec(memory_space=pl.ANY)
+    smalls = (g1, b1, qb, vb, ob, g2, b2, eb, sb)
+    return pl.pallas_call(
+        fwd_kernel,
+        grid=(steps,),
+        in_specs=[rows(feat), whole(segments)] + [whole(a) for a in smalls] + [anyw] * 4,
+        out_specs=[rows(3 * feat),
+                   pl.BlockSpec((256 * pairs, feat), lambda i: (i, 0)),
+                   rows(feat), rows(feat), rows(ff), rows(ff),
+                   pl.BlockSpec((slots, block), lambda i: (0, i)),
+                   pl.BlockSpec((slots, feat), lambda i: (0, 0)),
+                   pl.BlockSpec((slots, 128), lambda i: (0, 0))],
+        out_shape=[jax.ShapeDtypeStruct((count, 3 * feat), bf16),
+                   jax.ShapeDtypeStruct((steps * pairs * 256, feat), bf16),
+                   jax.ShapeDtypeStruct((count, feat), bf16),
+                   jax.ShapeDtypeStruct((count, feat), f32),
+                   jax.ShapeDtypeStruct((count, ff), bf16),
+                   jax.ShapeDtypeStruct((count, ff), bf16),
+                   jax.ShapeDtypeStruct((slots, count), bf16),
+                   jax.ShapeDtypeStruct((slots, feat), f32),
+                   jax.ShapeDtypeStruct((slots, 128), f32)],
+        scratch_shapes=[pltpu.VMEM(w3.shape, bf16), pltpu.VMEM(wo.shape, bf16), pltpu.VMEM(we.shape, bf16),
+                        pltpu.VMEM(ws.shape, bf16), pltpu.VMEM((slots, feat), f32), pltpu.VMEM((slots, 128), f32),
+                        pltpu.SemaphoreType.DMA((4,))],
+        compiler_params=pltpu.CompilerParams(vmem_limit_bytes=56 << 20, dimension_semantics=("arbitrary",)),
+        name="fwd",
+    )(tokens, segments, *smalls, w3, wo, we, ws)
+
+
+MESH = pl.DeviceIdType.MESH
+PLANE = 8
+BLK = 256
+CH = 768
+HALF = CH // 2
+ROWS = HALF // PLANE
+N_CH = 12
+
+
+def fold(x):
+    return jnp.sum(x.reshape(x.shape[0] // 8, 8, x.shape[1]), axis=0)
+
+
+def bwd_kernel(member, pooled, count, caption, scale, g1, b1, g2, b2,
+               qkv_h, probs_h, mixed_h, hidden_h, act_h, slope_h, tok_h, w3_h, wo_h, we_h, ws_h,
+               tw_out, ow_out, ew_out, sw_out, in_out, vec_out,
+               cs, snd, prv, own, prcv, swrcv, fin, swfin,
+               gol, gn2, hid, spread2, n2b, n1b, tok, act, slope, ws, we, ge, qkv, w3, wo, inbuf,
+               imgs, elow, ebsum, attn_sum, vec, vecrcv, vecall,
+               ld, psend, precv, xsend, xrecv, plsend, plrecv, swsend, swrecv, fsend, frecv, fout,
+               gsend, grecv, esend, erecv, vsend, vrecv, outsem):
+    t = lax.axis_index("tower")
+    d = lax.axis_index("dp")
+    p = d // 2
+    c = lax.rem(d, 2)
+    is_text = t == 1
+    count_t = gol.shape[0]
+    blocks = count_t // BLK
+    feat = CH
+    rows_here = caption.shape[0]
+    other = 1 - c
+
+    def peer(k):
+        return lax.rem(p + k, PLANE)
+
+    def at_core(tt, pp):
+        return (tt, pp * 2 + c)
+
+    partner = (t, p * 2 + other)
+
+    def remote(src, dst, ssem, rsem, dev):
+        return pltpu.make_async_remote_copy(src_ref=src, dst_ref=dst, send_sem=ssem, recv_sem=rsem,
+                                            device_id=dev, device_id_type=MESH)
+
+    barrier = pltpu.get_barrier_semaphore()
+    pl.semaphore_signal(barrier, inc=1, device_id=partner, device_id_type=MESH)
+    pl.semaphore_signal(barrier, inc=1, device_id=at_core(1 - t, p), device_id_type=MESH)
+    for k in range(1, PLANE):
+        pl.semaphore_signal(barrier, inc=1, device_id=at_core(t, peer(k)), device_id_type=MESH)
+        pl.semaphore_signal(barrier, inc=1, device_id=at_core(1 - t, peer(k)), device_id_type=MESH)
+
+    pooled_v = pooled[...]
+    inverse = lax.rsqrt(jnp.sum(pooled_v * pooled_v, axis=1, keepdims=True) + 1e-06)
+    emb = pooled_v * inverse
+    emb_low = emb.astype(bf16)
+
+    def lane(q):
+        return jnp.where(q < 8, q // 2, q - 4)
+
+    def pair_copy(q):
+        return remote(snd.at[lax.rem(q, 2)], prv.at[q], psend.at[q], precv.at[q], partner)
+
+    def x_copy(q):
+        return remote(cs.at[q, 0:HALF], cs.at[q, 0:HALF], xsend.at[q], xrecv.at[q], at_core(1 - t, p))
+
+    def plane_copy(q, k):
+        row = pl.multiple_of(HALF * t + ROWS * peer(k), 16)
+        return remote(cs.at[q, pl.ds(row, ROWS)], prcv.at[lane(q), k], plsend.at[q, k], plrecv.at[q, k],
+                      at_core(t, peer(k)))
+
+    def sw_copy(q, zz, y):
+        to = 2 * zz + y
+        k = lax.rem(to - p + PLANE, PLANE)
+        row = pl.multiple_of(HALF * t + 4 * ROWS * y, 16)
+        return remote(cs.at[q, pl.ds(row, 4 * ROWS)], swrcv.at[k], swsend.at[zz, y], swrecv.at[k], at_core(t, to))
+
+    def plane_send(q):
+        for k in range(1, PLANE):
+            plane_copy(q, k).start()
+
+    def sw_send(q, zz):
+        for y in range(2):
+            @pl.when(p != 2 * zz + y)
+            def _():
+                sw_copy(q, zz, y).start()
+
+    def sw_sent(q, zz):
+        for y in range(2):
+            @pl.when(p != 2 * zz + y)
+            def _():
+                sw_copy(q, zz, y).wait_send()
+
+    def chip_sum(q):
+        pair_copy(q).wait_recv()
+        slot = lax.rem(q, 2)
+        for r in range(0, CH, 128):
+            cs[q, r:r + 128, :] = (own[slot, r:r + 128, :] + prv[q, r:r + 128, :].astype(f32)).astype(bf16)
+        x_copy(q).start()
+
+    def chunk(q, left, right_of):
+        slot = lax.rem(q, 2)
+
+        @pl.when(q >= 2)
+        def _():
+            pair_copy(q - 2).wait_send()
+        for mine in (False, True):
+            right = right_of(c if mine else other)
+            for r in range(0, CH, 256):
+                part = mm_tn(left[:, r:r + 256], right)
+                if mine:
+                    own[slot, r:r + 256, :] = part
+                else:
+                    snd[slot, r:r + 256, :] = part.astype(bf16)
+            if not mine:
+                pair_copy(q).start()
+
+    def gather_copy(k):
+        return remote(elow, imgs.at[c, p], gsend.at[k], grecv.at[k], at_core(1 - t, peer(k)))
+
+    def share_copy():
+        return remote(imgs.at[c], imgs.at[c], esend, erecv, partner)
+
+    def load(n, src, dst):
+        return pltpu.make_async_copy(src, dst, ld.at[n])
+
+    def tile_loads(i):
+        s = lax.rem(i, 2)
+        out = []
+        ff = act_h.shape[1]
+        for h in range(2):
+            col = pl.multiple_of((ff // 2) * h + HALF * i, 128)
+            here = pl.ds(HALF * h, HALF)
+            out.append(load(8 * s + 4 * h, act_h.at[:, pl.ds(col, HALF)], act.at[s, :, here]))
+            out.append(load(8 * s + 4 * h + 1, slope_h.at[:, pl.ds(col, HALF)], slope.at[s, :, here]))
+            out.append(load(8 * s + 4 * h + 2, ws_h.at[pl.ds(col, HALF)], ws.at[s, here]))
+            out.append(load(8 * s + 4 * h + 3, we_h.at[:, pl.ds(col, HALF)], we.at[s, :, here]))
+        return out
+
+    hid_load = load(16, hidden_h, hid)
+    tok_load = load(17, tok_h, tok)
+    qkv_load = load(18, qkv_h, qkv)
+    w3_load = load(19, w3_h, w3)
+    wo_load = load(20, wo_h, wo)
+    mixed_load = load(21, mixed_h, slope.at[0])
+    probs_loads = [load(22 + h, probs_h.at[pl.ds(count_t * h, count_t)], act.at[h]) for h in range(2)]
+
+    @pl.when(t == 0)
+    def _():
+        elow[...] = emb_low[:rows_here]
+        pl.semaphore_wait(barrier, 2 * PLANE)
+        for k in range(PLANE):
+            gather_copy(k).start()
+        inbuf[0] = jnp.zeros_like(inbuf[0])
+        for m in range(blocks):
+            pltpu.make_async_copy(inbuf.at[0], in_out.at[pl.ds(BLK * m, BLK)], outsem.at[m]).start()
+
+        @pl.loop(0, 4)
+        def _(i):
+            x_copy(2 * i).wait_recv()
+            sw_send(2 * i, i)
+            x_copy(2 * i + 1).wait_recv()
+            plane_send(2 * i + 1)
+
+        @pl.loop(8, N_CH)
+        def _(q):
+            x_copy(q).wait_recv()
+            plane_send(q)
+        for k in range(PLANE):
+            gather_copy(k).wait_send()
+        for m in range(blocks):
+            pltpu.make_async_copy(inbuf.at[0], in_out.at[pl.ds(BLK * m, BLK)], outsem.at[m]).wait()
+
+    @pl.when(is_text)
+    def _():
+        hid_load.start()
+        tok_load.start()
+        for cp in tile_loads(0):
+            cp.start()
+        for cp in tile_loads(1):
+            cp.start()
+        qkv_load.start()
+        w3_load.start()
+        wo_load.start()
+        gain2, shift2 = g2[...].astype(f32), b2[...].astype(f32)
+        gain1, shift1 = g1[...].astype(f32), b1[...].astype(f32)
+        hid_load.wait()
+
+        @pl.loop(0, blocks)
+        def _(m):
+            here = pl.ds(pl.multiple_of(m * BLK, BLK), BLK)
+            norm, spread = stats(hid[here, :])
+            n2b[here, :] = (norm * gain2 + shift2).astype(bf16)
+            hid[here, :] = norm
+            spread2[here, :] = spread
+        tok_load.wait()
+
+        @pl.loop(0, blocks)
+        def _(m):
+            here = pl.ds(pl.multiple_of(m * BLK, BLK), BLK)
+            norm, _s = stats(tok[here, :].astype(f32))
+            n1b[here, :] = (norm * gain1 + shift1).astype(bf16)
+        gn2[...] = jnp.zeros_like(gn2)
+        attn_sum[...] = jnp.zeros_like(attn_sum)
+        vec[...] = jnp.zeros_like(vec)
+        pl.semaphore_wait(barrier, 2 * PLANE)
+        for k in range(PLANE):
+            gather_copy(k).wait_recv()
+        share_copy().start()
+        share_copy().wait_send()
+        remote(imgs.at[other], imgs.at[other], esend, erecv, partner).wait_recv()
+
+        table = imgs[...].reshape(2 * PLANE * rows_here, feat)
+        dots = mm_nt(emb_low, table)
+        factor = scale[0]
+        logits = factor * dots
+        peak = jnp.max(logits, axis=1, keepdims=True)
+        weight = jnp.exp(logits - peak)
+        total = jnp.sum(weight, axis=1, keepdims=True)
+        wanted = jnp.concatenate([caption[:, s:s + 1] for s in range(CAPS)], axis=0)
+        span = 2 * rows_here
+        inside = lax.rem(wanted, span)
+        wanted = (inside // rows_here) * (PLANE * rows_here) + (wanted // span) * rows_here + lax.rem(inside, rows_here)
+        hot = (lax.broadcasted_iota(jnp.int32, dots.shape, 1) == wanted).astype(f32)
+        picked = jnp.sum(logits * hot, axis=1, keepdims=True)
+        loss_here = jnp.sum(peak + jnp.log(total) - picked, axis=0, keepdims=True)
+        grad_logits = weight / total - hot
+        factor_here = jnp.sum(jnp.sum(grad_logits * dots, axis=1, keepdims=True), axis=0, keepdims=True)
+        grad_emb = mm((factor * grad_logits).astype(bf16), table)
+        counts = count[:, :1]
+        grad_pool = inverse * (grad_emb - emb * jnp.sum(emb * grad_emb, axis=1, keepdims=True))
+        vec[7:8, :] = jnp.sum(grad_pool, axis=0, keepdims=True)
+        column = lax.broadcasted_iota(jnp.int32, (1, feat), 1)
+        vec[12:13, :] = jnp.where(column == 0, loss_here, jnp.where(column == 1, factor_here, 0.0))
+        gp_hi, gp_lo = low_pair(grad_pool / counts)
+        for m in range(blocks):
+            gol[BLK * m:BLK * (m + 1), :] = mm_tn(member[:, BLK * m:BLK * (m + 1)], gp_hi).astype(bf16)
+
+        @pl.loop(0, 4)
+        def _(i):
+            s = lax.rem(i, 2)
+            for cp in tile_loads(i):
+                cp.wait()
+            chunk(2 * i, act.at[s], lambda h: gol[:, pl.ds(pl.multiple_of(HALF * h, 128), HALF)])
+
+            @pl.when(i > 0)
+            def _():
+                chip_sum(2 * i - 1)
+                plane_send(2 * i - 1)
+            sums = jnp.zeros((8, feat), f32)
+            for m in range(blocks):
+                here = slice(BLK * m, BLK * (m + 1))
+                grad = mm_nt(gol[here, :], ws[s]) * slope[s, here, :].astype(f32)
+                sums = sums + fold(grad)
+                ge[here, :] = grad.astype(bf16)
+            sums = jnp.sum(sums, axis=0, keepdims=True)
+            for h in range(2):
+                ebsum[:, pl.ds(pl.multiple_of(4 * HALF * h + HALF * i, 128), HALF)] = sums[:, HALF * h:HALF * (h + 1)]
+            chunk(2 * i + 1, n2b, lambda h: ge[:, pl.ds(pl.multiple_of(HALF * h, 128), HALF)])
+            chip_sum(2 * i)
+            sw_send(2 * i, i)
+            for m in range(blocks):
+                here = slice(BLK * m, BLK * (m + 1))
+                gn2[here, :] += mm_nt(ge[here, :], we[s])
+
+            @pl.when(i < 2)
+            def _():
+                for cp in tile_loads(i + 2):
+                    cp.start()
+
+            @pl.when(i == 2)
+            def _():
+                mixed_load.start()
+                probs_loads[0].start()
+        probs_loads[1].start()
+        chip_sum(7)
+        plane_send(7)
+
+        zeros8 = jnp.zeros((8, feat), f32)
+
+        def norm2_back(m, sums):
+            here = pl.ds(pl.multiple_of(m * BLK, BLK), BLK)
+            norm, g_in = hid[here, :], gn2[here, :]
+            hot_m = member[:, here]
+            grad_out = mm_tn(hot_m, gp_hi) + mm_tn(hot_m, gp_lo)
+            g = g_in * gain2
+            back = spread2[here, :] * (g - jnp.mean(g, axis=1, keepdims=True)
+                                       - norm * jnp.mean(g * norm, axis=1, keepdims=True))
+            gh = grad_out + back
+            gn2[here, :] = gh
+            gol[here, :] = gh.astype(bf16)
+            return (sums[0] + fold(g_in * norm), sums[1] + fold(g_in), sums[2] + fold(gh))
+        sums = lax.fori_loop(0, blocks, norm2_back, (zeros8, zeros8, zeros8))
+        for row, x in ((5, sums[0]), (6, sums[1]), (4, sums[2])):
+            vec[row:row + 1, :] = jnp.sum(x, axis=0, keepdims=True)
+        for n in range(4):
+            vec[8 + n:9 + n, :] = ebsum[:, feat * n:feat * (n + 1)]
+
+        mixed_load.wait()
+        chunk(8, slope.at[0], lambda h: gol[:, pl.ds(pl.multiple_of(HALF * h, 128), HALF)])
+        wo_load.wait()
+        for m in range(blocks):
+            here = slice(BLK * m, BLK * (m + 1))
+            ge[here, :] = mm_nt(gol[here, :], wo[...]).astype(bf16)
+        chip_sum(8)
+        plane_send(8)
+
+        qkv_load.wait()
+        for cp in probs_loads:
+            cp.wait()
+        first_half = lax.broadcasted_iota(jnp.int32, (128, 128), 1) < 64
+
+        def split(x):
+            zero = jnp.zeros_like(x)
+            return jnp.concatenate([jnp.where(first_half, x, zero), jnp.where(first_half, zero, x)], axis=0)
+
+        @pl.loop(0, count_t // 128)
+        def _(rp):
+            here = pl.ds(pl.multiple_of(rp * 128, 128), 128)
+            half = rp // (count_t // 256)
+            prow = pl.ds(pl.multiple_of(lax.rem(rp, count_t // 256) * 256, 256), 256)
+            for hp in range(HEADS // 2):
+                c0 = hp * 128
+                q, k, v = (qkv[here, feat * n + c0:feat * n + c0 + 128] for n in range(3))
+                gm2 = split(ge[here, c0:c0 + 128])
+                probs = act[half, prow, c0:c0 + 128]
+                probs_f = probs.astype(f32)
+                gp = mm_nt(gm2, v)
+                weighted = probs_f * gp
+                gs = (weighted - probs_f * jnp.sum(weighted, axis=1, keepdims=True)).astype(bf16)
+                gv = mm_tn(probs, gm2)
+                gk = mm_tn(gs, split(q)) * 0.125
+                gq2 = mm(gs, k)
+                gq = jnp.where(first_half, gq2[:128], gq2[128:]) * 0.125
+                for n, x in ((0, gq), (1, gk), (2, gv)):
+                    qkv[here, feat * n + c0:feat * n + c0 + 128] = x.astype(bf16)
+                    if n != 1:
+                        at = slice((feat if n else 0) + c0, (feat if n else 0) + c0 + 128)
+                        attn_sum[:, at] += fold(x)
+        vec[2:3, :] = jnp.sum(attn_sum[:, :feat], axis=0, keepdims=True)
+        vec[3:4, :] = jnp.sum(attn_sum[:, feat:], axis=0, keepdims=True)
+
+        @pl.loop(0, 3)
+        def _(j):
+            chunk(9 + j, n1b, lambda h: qkv[:, pl.ds(pl.multiple_of(CH * j + HALF * h, 128), HALF)])
+
+            @pl.when(j > 0)
+            def _():
+                chip_sum(8 + j)
+                plane_send(8 + j)
+        w3_load.wait()
+
+        def norm1_back(m, sums):
+            here = pl.ds(pl.multiple_of(m * BLK, BLK), BLK)
+            slot = lax.rem(m, 2)
+
+            def out_copy(mm_):
+                return pltpu.make_async_copy(inbuf.at[lax.rem(mm_, 2)],
+                                             in_out.at[pl.ds(pl.multiple_of(mm_ * BLK, BLK), BLK)], outsem.at[mm_])
+
+            g_in = mm_nt(qkv[here, :], w3[...])
+
+            @pl.when(m == 0)
+            def _():
+                chip_sum(11)
+                plane_send(11)
+
+            @pl.when(m >= 2)
+            def _():
+                out_copy(m - 2).wait()
+            norm, spread = stats(tok[here, :].astype(f32))
+            g = g_in * gain1
+            back = spread * (g - jnp.mean(g, axis=1, keepdims=True)
+                             - norm * jnp.mean(g * norm, axis=1, keepdims=True))
+            inbuf[slot] = gn2[here, :] + back
+            out_copy(m).start()
+            return (sums[0] + fold(g_in * norm), sums[1] + fold(g_in))
+        sums = lax.fori_loop(0, blocks, norm1_back, (zeros8, zeros8))
+        for row, x in ((0, sums[0]), (1, sums[1])):
+            vec[row:row + 1, :] = jnp.sum(x, axis=0, keepdims=True)
+        for m in (blocks - 2, blocks - 1):
+            pltpu.make_async_copy(inbuf.at[m % 2], in_out.at[pl.ds(BLK * m, BLK)], outsem.at[m]).wait()
+
+    mine8 = pl.ds(pl.multiple_of(8 * c, 8), 8)
+    their8 = pl.ds(pl.multiple_of(8 * other, 8), 8)
+
+    def v_pair():
+        return remote(vec.at[their8], vecrcv.at[0], vsend.at[0], vrecv.at[0], partner)
+
+    def v_plane(k):
+        return remote(vec.at[mine8], vecrcv.at[k], vsend.at[k], vrecv.at[k], at_core(t, peer(k)))
+
+    def v_share(half):
+        return remote(vecall.at[half], vecall.at[half], vsend.at[8], vrecv.at[8], partner)
+
+    def v_across():
+        return remote(vecall, vecall, vsend.at[9], vrecv.at[9], at_core(1 - t, p))
+
+    @pl.when(is_text)
+    def _():
+        v_pair().start()
+        v_pair().wait_recv()
+        vec[mine8, :] += vecrcv[0]
+        for k in range(1, PLANE):
+            v_plane(k).start()
+
+    def total_of(block, get):
+        out = block
+        for k in range(1, PLANE):
+            out = out + get(k).astype(f32)
+        return out
+
+    def finish(q, out, col, base):
+        for k in range(1, PLANE):
+            plane_copy(q, k).wait_recv()
+        row = pl.multiple_of(HALF * t + ROWS * p, 16)
+        fin[lane(q)] = total_of(cs[q, pl.ds(row, ROWS), :].astype(f32), lambda k: prcv[lane(q), k])
+        keep_copy(q, out, col).start()
+        give_copy(q, out, col).start()
+
+    def keep_copy(q, out, col):
+        n = ROWS // 2
+        return pltpu.make_async_copy(fin.at[lane(q), pl.ds(pl.multiple_of(n * c, 8), n)], out.at[:, pl.ds(col, HALF)],
+                                     fout.at[q])
+
+    def give_copy(q, out, col):
+        n = ROWS // 2
+        return remote(fin.at[lane(q), pl.ds(pl.multiple_of(n * other, 8), n)], out.at[:, pl.ds(col, HALF)],
+                      fsend.at[q], frecv.at[q], partner)
+
+    def sw_keep():
+        n = 2 * ROWS
+        return pltpu.make_async_copy(swfin.at[pl.ds(pl.multiple_of(n * c, 8), n)],
+                                     sw_out.at[:, pl.ds(pl.multiple_of(HALF * c, 128), HALF)], fout.at[0])
+
+    def sw_give():
+        n = 2 * ROWS
+        return remote(swfin.at[pl.ds(pl.multiple_of(n * other, 8), n)],
+                      sw_out.at[:, pl.ds(pl.multiple_of(HALF * c, 128), HALF)], fsend.at[0], frecv.at[0], partner)
+
+    def wait_frecv(q, out, col_other):
+        n = ROWS // 2
+        remote(fin.at[lane(q), pl.ds(pl.multiple_of(n * other, 8), n)], out.at[:, pl.ds(col_other, HALF)],
+               fsend.at[q], frecv.at[q], partner).wait_recv()
+
+    for k in range(1, PLANE):
+        remote(cs.at[0, 0:4 * ROWS], swrcv.at[k], swsend.at[0, 0], swrecv.at[k], partner).wait_recv()
+    sw_q = 2 * (p // 2)
+    sw_row = pl.multiple_of(HALF * t + 4 * ROWS * lax.rem(p, 2), 16)
+    swfin[...] = total_of(cs[sw_q, pl.ds(sw_row, 4 * ROWS), :].astype(f32), lambda k: swrcv[k])
+    sw_keep().start()
+    sw_give().start()
+
+    def ew_col(i, h):
+        return pl.multiple_of(4 * HALF * h + HALF * i, 128)
+
+    def tw_col(j, h):
+        return pl.multiple_of(CH * j + HALF * h, 128)
+
+    def ow_col(h):
+        return pl.multiple_of(HALF * h, 128)
+
+    @pl.loop(0, 4)
+    def _(i):
+        finish(2 * i + 1, ew_out, ew_col(i, c), None)
+    finish(8, ow_out, ow_col(c), None)
+
+    @pl.loop(0, 3)
+    def _(j):
+        finish(9 + j, tw_out, tw_col(j, c), None)
+
+    @pl.when(is_text)
+    def _():
+        for k in range(1, PLANE):
+            v_plane(k).wait_recv()
+        vecall[c] = total_of(vec[mine8, :], lambda k: vecrcv[k])
+        v_share(c).start()
+        v_share(other).wait_recv()
+        v_across().start()
+        v_across().wait_send()
+        v_share(c).wait_send()
+        v_pair().wait_send()
+        for k in range(1, PLANE):
+            v_plane(k).wait_send()
+        for q in (N_CH - 2, N_CH - 1):
+            pair_copy(q).wait_send()
+
+        @pl.loop(0, N_CH)
+        def _(q):
+            x_copy(q).wait_send()
+
+    @pl.when(t == 0)
+    def _():
+        v_across().wait_recv()
+    vec_out[...] = vecall[...]
+
+    @pl.loop(0, 4)
+    def _(i):
+        sw_sent(2 * i, i)
+        for k in range(1, PLANE):
+            plane_copy(2 * i + 1, k).wait_send()
+        keep_copy(2 * i + 1, ew_out, ew_col(i, c)).wait()
+        give_copy(2 * i + 1, ew_out, ew_col(i, c)).wait_send()
+        wait_frecv(2 * i + 1, ew_out, ew_col(i, other))
+
+    @pl.loop(8, N_CH)
+    def _(q):
+        for k in range(1, PLANE):
+            plane_copy(q, k).wait_send()
+    keep_copy(8, ow_out, ow_col(c)).wait()
+    give_copy(8, ow_out, ow_col(c)).wait_send()
+    wait_frecv(8, ow_out, ow_col(other))
+
+    @pl.loop(0, 3)
+    def _(j):
+        keep_copy(9 + j, tw_out, tw_col(j, c)).wait()
+        give_copy(9 + j, tw_out, tw_col(j, c)).wait_send()
+        wait_frecv(9 + j, tw_out, tw_col(j, other))
+    sw_keep().wait()
+    sw_give().wait_send()
+    remote(swfin.at[pl.ds(0, 2 * ROWS)], sw_out.at[:, pl.ds(pl.multiple_of(HALF * other, 128), HALF)],
+           fsend.at[0], frecv.at[0], partner).wait_recv()
+
+    @pl.when(is_text)
+    def _():
+        pass
+
+
+def backward(member, pooled, count, caption, scale, g1, b1, g2, b2,
+             qkv, probs, mixed, hidden, act, slope, tokens, w3, wo, we, ws):
+    n_tok, feat = tokens.shape
+    rows_here = caption.shape[0]
+    ff = we.shape[1]
+    dma = pltpu.SemaphoreType.DMA
+    vm = pltpu.VMEM
+    vspec = pl.BlockSpec(memory_space=pltpu.VMEM)
+    sspec = pl.BlockSpec(memory_space=pltpu.SMEM)
+    anyw = pl.BlockSpec(memory_space=pl.ANY)
+    shape = jax.ShapeDtypeStruct
+    scratch = [
+        vm((N_CH, CH, HALF), bf16), vm((2, CH, HALF), bf16), vm((N_CH, CH, HALF), bf16), vm((2, CH, HALF), f32),
+        vm((N_CH - 4, PLANE, ROWS, HALF), bf16), vm((PLANE, 4 * ROWS, HALF), bf16),
+        vm((N_CH - 4, ROWS, HALF), f32), vm((4 * ROWS, HALF), f32),
+        vm((n_tok, feat), bf16), vm((n_tok, feat), f32), vm((n_tok, feat), f32), vm((n_tok, 1), f32),
+        vm((n_tok, feat), bf16), vm((n_tok, feat), bf16), vm((n_tok, feat), bf16),
+        vm((2, n_tok, CH), bf16), vm((2, n_tok, CH), bf16), vm((2, CH, feat), bf16), vm((2, feat, CH), bf16),
+        vm((n_tok, feat), bf16), vm((n_tok, 3 * feat), bf16), vm(w3.shape, bf16), vm(wo.shape, bf16),
+        vm((2, BLK, feat), f32),
+        vm((2, PLANE, rows_here, feat), bf16), vm((rows_here, feat), bf16), vm((1, ff), f32), vm((8, 2 * feat), f32),
+        vm((16, feat), f32), vm((PLANE, 8, feat), f32), vm((2, 8, feat), f32),
+        dma((24,)), dma((N_CH,)), dma((N_CH,)), dma((N_CH,)), dma((N_CH,)), dma((N_CH, PLANE)), dma((N_CH, PLANE)),
+        dma((4, 2)), dma((PLANE,)), dma((N_CH,)), dma((N_CH,)), dma((N_CH,)),
+        dma((PLANE,)), dma((PLANE,)), dma, dma, dma((10,)), dma((10,)), dma((n_tok // BLK,)),
+    ]
+    return pl.pallas_call(
+        bwd_kernel,
+        in_specs=[vspec] * 4 + [sspec] + [vspec] * 4 + [anyw] * 11,
+        out_specs=[anyw] * 5 + [vspec],
+        out_shape=[shape((ROWS // 2, 3 * feat), f32), shape((ROWS // 2, feat), f32), shape((ROWS // 2, ff), f32),
+                   shape((2 * ROWS, feat), f32), shape((n_tok, feat), f32), shape((2, 8, feat), f32)],
+        scratch_shapes=scratch,
+        compiler_params=pltpu.CompilerParams(vmem_limit_bytes=61 << 20, collective_id=0, has_side_effects=True),
+        name="bwd",
+    )(member, pooled, count, caption, scale, g1, b1, g2, b2,
+      qkv, probs, mixed, hidden, act, slope, tokens, w3, wo, we, ws)
+
+
+def hand_out_kernel(scale_by, vec, tw, ow, ew, sw, inp, loss, factor, *rest):
+    smalls, bigs, sems = rest[:9], rest[9:14], rest[14]
+    moves = [pltpu.make_async_copy(src, dst, sems.at[n]) for n, (src, dst) in enumerate(zip((tw, ow, ew, sw, inp), bigs))]
+    for move in moves:
+        move.start()
+    feat = vec.shape[2]
+    width = smalls[0].shape[1]
+    wide = smalls[8].shape[1]
+    g = lax.axis_index("tower") * lax.axis_size("dp") + lax.axis_index("dp")
+    turned = pltpu.roll(vec[0], lax.rem(feat - width * g, feat), axis=1)
+    for n in range(8):
+        smalls[n][...] = turned[n:n + 1, :width]
+    per_row = feat // wide
+    row = vec[1, pl.ds(g // per_row, 1), :]
+    rows = jnp.broadcast_to(row, (8, feat))
+    smalls[8][...] = pltpu.roll(rows, lax.rem(feat - wide * lax.rem(g, per_row), feat), axis=1)[:1, :wide]
+    loss[...] = vec[1, 4:5, 0:1] * scale_by
+    factor[...] = vec[1, 4:5, 1:2]
+    for move in moves:
+        move.wait()
+
+
+def hand_out(vec, tw, ow, ew, sw, inp, captions):
+    devices = lax.axis_size("tower") * lax.axis_size("dp")
+    feat = vec.shape[2]
+    shape = jax.ShapeDtypeStruct
+    bigs = (tw, ow, ew, sw, inp)
+    vspec = pl.BlockSpec(memory_space=pltpu.VMEM)
+    anyw = pl.BlockSpec(memory_space=pl.ANY)
+    return pl.pallas_call(
+        functools.partial(hand_out_kernel, 1.0 / captions),
+        in_specs=[vspec] + [anyw] * 5,
+        out_specs=[vspec] * 11 + [anyw] * 5,
+        out_shape=[shape((1, 1), f32)] * 2 + [shape((1, feat // devices), f32)] * 8
+        + [shape((1, ew.shape[1] // devices), f32)] + [shape(a.shape, f32) for a in bigs],
+        scratch_shapes=[pltpu.SemaphoreType.DMA((5,))],
+        name="hand_out",
+    )(vec, *bigs)
+
+
+def local_fast(tokens, segments, caption_image, logit_scale, first_gain, first_bias, triple_weight, query_bias,
+               value_bias, output_weight, output_bias, second_gain, second_bias, expand_weight, expand_bias,
+               shrink_weight, shrink_bias):
+    rows_here, length, feat = tokens.shape[1:]
+    flat = tokens[0].reshape(rows_here * length, feat)
+    w3, wo, we, ws = triple_weight[0], output_weight[0], expand_weight[0], shrink_weight[0]
+    qkv, probs, mixed, hidden, act, slope, member, pooled, count = forward(
+        flat, segments, first_gain, first_bias, w3, query_bias, value_bias, wo, output_bias,
+        second_gain, second_bias, we, expand_bias, ws, shrink_bias)
+    tw, ow, ew, sw, inp, vec = backward(member, pooled, count, caption_image, logit_scale, first_gain, first_bias,
+                                        second_gain, second_bias, qkv, probs, mixed, hidden, act, slope, flat,
+                                        w3, wo, we, ws)
+    captions = rows_here * CAPS * lax.axis_size("dp")
+    outs = hand_out(vec, tw, ow, ew, sw, inp, captions)
+    loss, factor = outs[0].reshape(1), outs[1].reshape(1)
+    g1, b1, qb, vb, ob, g2, b2, sb, eb = (a.reshape(-1) for a in outs[2:11])
+    tw, ow, ew, sw, inp = outs[11:]
+    return (loss, factor, inp.reshape(1, rows_here, length, feat), g1, b1, tw, qb, vb, ow, ob, g2, b2, ew, eb, sw, sb)
 
 
 HIGH = lax.Precision.HIGHEST
@@ -301,8 +1096,9 @@
         P("tower", None, None),
         P("tower", None),
     )
+    fits = mesh.shape["tower"] == 2 and mesh.shape["dp"] == 2 * PLANE
     return jax.shard_map(
-        local,
+        local_fast if fits else local,
         mesh=mesh,
         in_specs=placed,
         out_specs=(

time: 741 us -> 288 us (0.39)
  the two profiles are of different devices: /device:TPU:0 before, /device:TPU:25 now
where the time goes in v1:
time: 288 us
  Pallas kernels  285 us (99%)
    pallas_call x1, Pallas kernels, hand_out(): pl.pallas_call(functools.partial(hand_out_kernel, 1.0 / captions), in_spe...  125 us
    pallas_call x1, Pallas kernels, backward(): pl.pallas_call(bwd_kernel, in_specs=[vspec] * 4 + [sspec] + [vspec] * 4 +...  125 us
    pallas_call x1, Pallas kernels, forward(): pl.pallas_call(fwd_kernel, grid=(steps,), in_specs=[rows(feat), whole(seg...  35.6 us

profile of v1, /device:TPU:25, one launch (start us, length us, event | category | flops | bytes accessed | tf_op | source)
XLA Modules:
  0.0 287.6 jit_solution(16466655573044771477)
XLA Ops:
  1.3 1.4 copy.33.caption
  2.6 35.6 %fwd.1 = (bf16[1024,2304]{1,0:T(8,128)(2,1)}, bf16[2048,768]{1,0:T(8,128)(2,1)}, bf16[1024,768]{1,0:T(8,128)(2,1)}, f32[1024,768]{1,0:T(8,128)}, bf16[1024,3072]...) custom-call(bf16[1024,768]{1,0:T(8,128)(2,1)} %bitcast.23, ...), custom_call_target="tpu_custom_call" | custom-call | tf_op jit(solution)/shard_map/fwd/pallas_call | solution.py:153
  38.3 124.5 %bwd.1 = (f32[24,2304]{1,0:T(8,128)}, f32[24,768]{1,0:T(8,128)}, f32[24,3072]{1,0:T(8,128)}, f32[96,768]{1,0:T(8,128)}, f32[1024,768]{1,0:T(8,128)}, /*index=5*/f32[2,8,768]{2,1,0:T(8,128)}) custom-call(bf16[64,1024]{1,0:T(8,128)(2,1)} %get-tuple-element.47.member, f32[64,768]{1,0:T(8,128)} %get-tuple-element.48.pooled, f32[64,128]{1,0:T(8,128)} %get-tuple-element.49.count, ...), custom_call_target="tpu_custom_call" | custom-call | tf_op jit(solution)/shard_map/bwd/pallas_call | solution.py:733
  162.8 124.6 %hand_out.1 = (f32[1,1]{1,0:T(1,128)}, f32[1,1]{1,0:T(1,128)}, f32[1,24]{1,0:T(1,128)}, f32[1,24]{1,0:T(1,128)}, f32[1,24]{1,0:T(1,128)}, /*index=5*/f32[1,24]{1...) custom-call(f32[2,8,768]{2,1,0:T(8,128)} %get-tuple-element.56.vec, ...), custom_call_target="tpu_custom_call" | custom-call | tf_op jit(solution)/shard_map/hand_out/pallas_call | solution.py:775

commit v2 on v1

--- a/solution.py
+++ b/solution.py
@@ -744,43 +744,43 @@
 
 
 def hand_out_kernel(scale_by, vec, tw, ow, ew, sw, inp, loss, factor, *rest):
-    smalls, bigs, sems = rest[:9], rest[9:14], rest[14]
-    moves = [pltpu.make_async_copy(src, dst, sems.at[n]) for n, (src, dst) in enumerate(zip((tw, ow, ew, sw, inp), bigs))]
-    for move in moves:
-        move.start()
-    feat = vec.shape[2]
-    width = smalls[0].shape[1]
-    wide = smalls[8].shape[1]
-    g = lax.axis_index("tower") * lax.axis_size("dp") + lax.axis_index("dp")
-    turned = pltpu.roll(vec[0], lax.rem(feat - width * g, feat), axis=1)
-    for n in range(8):
-        smalls[n][...] = turned[n:n + 1, :width]
-    per_row = feat // wide
-    row = vec[1, pl.ds(g // per_row, 1), :]
-    rows = jnp.broadcast_to(row, (8, feat))
-    smalls[8][...] = pltpu.roll(rows, lax.rem(feat - wide * lax.rem(g, per_row), feat), axis=1)[:1, :wide]
-    loss[...] = vec[1, 4:5, 0:1] * scale_by
-    factor[...] = vec[1, 4:5, 1:2]
-    for move in moves:
-        move.wait()
+    smalls, bigs = rest[:9], rest[9:]
+    bigs[4][...] = inp[...]
+
+    @pl.when(pl.program_id(0) == 0)
+    def _():
+        for src, dst in zip((tw, ow, ew, sw), bigs):
+            dst[...] = src[...]
+        feat = vec.shape[2]
+        width = smalls[0].shape[1]
+        wide = smalls[8].shape[1]
+        g = lax.axis_index("tower") * lax.axis_size("dp") + lax.axis_index("dp")
+        turned = pltpu.roll(vec[0], lax.rem(feat - width * g, feat), axis=1)
+        for n in range(8):
+            smalls[n][...] = turned[n:n + 1, :width]
+        per_row = feat // wide
+        rows = jnp.broadcast_to(vec[1, pl.ds(g // per_row, 1), :], (8, feat))
+        smalls[8][...] = pltpu.roll(rows, lax.rem(feat - wide * lax.rem(g, per_row), feat), axis=1)[:1, :wide]
+        loss[...] = vec[1, 4:5, 0:1] * scale_by
+        factor[...] = vec[1, 4:5, 1:2]
 
 
 def hand_out(vec, tw, ow, ew, sw, inp, captions):
     devices = lax.axis_size("tower") * lax.axis_size("dp")
     feat = vec.shape[2]
-    shape = jax.ShapeDtypeStruct
-    bigs = (tw, ow, ew, sw, inp)
-    vspec = pl.BlockSpec(memory_space=pltpu.VMEM)
-    anyw = pl.BlockSpec(memory_space=pl.ANY)
+    bigs = (tw, ow, ew, sw)
+    outs = ([(1, 1)] * 2 + [(1, feat // devices)] * 8 + [(1, ew.shape[1] // devices)]
+            + [a.shape for a in bigs])
+    whole = lambda dims: pl.BlockSpec(dims, lambda i: (0,) * len(dims))
+    moving = pl.BlockSpec((BLK, feat), lambda i: (i, 0))
     return pl.pallas_call(
         functools.partial(hand_out_kernel, 1.0 / captions),
-        in_specs=[vspec] + [anyw] * 5,
-        out_specs=[vspec] * 11 + [anyw] * 5,
-        out_shape=[shape((1, 1), f32)] * 2 + [shape((1, feat // devices), f32)] * 8
-        + [shape((1, ew.shape[1] // devices), f32)] + [shape(a.shape, f32) for a in bigs],
-        scratch_shapes=[pltpu.SemaphoreType.DMA((5,))],
+        grid=(inp.shape[0] // BLK,),
+        in_specs=[whole(vec.shape)] + [whole(a.shape) for a in bigs] + [moving],
+        out_specs=[whole(dims) for dims in outs] + [moving],
+        out_shape=[jax.ShapeDtypeStruct(dims, f32) for dims in outs + [inp.shape]],
         name="hand_out",
-    )(vec, *bigs)
+    )(vec, *bigs, inp)
 
 
 def local_fast(tokens, segments, caption_image, logit_scale, first_gain, first_bias, triple_weight, query_bias,

time: 288 us -> 168 us (0.58)
  Pallas kernels: 285 us -> 165 us
    pallas_call x1, Pallas kernels: 125 us -> 4.93 us  [hand_out(): pl.pallas_call(functools.partial(hand_out_kernel, 1.0 / captions), grid=(...]
where the time goes in v2:
time: 168 us
  Pallas kernels  165 us (98%)
    pallas_call x1, Pallas kernels, backward(): pl.pallas_call(bwd_kernel, in_specs=[vspec] * 4 + [sspec] + [vspec] * 4 +...  125 us
    pallas_call x1, Pallas kernels, forward(): pl.pallas_call(fwd_kernel, grid=(steps,), in_specs=[rows(feat), whole(seg...  35.6 us
    pallas_call x1, Pallas kernels, hand_out(): pl.pallas_call(functools.partial(hand_out_kernel, 1.0 / captions), grid=(...  4.93 us

profile of v2, /device:TPU:25, one launch (start us, length us, event | category | flops | bytes accessed | tf_op | source)
XLA Modules:
  0.0 167.8 jit_solution(7398622580064928418)
XLA Ops:
  1.3 1.4 copy.33.caption
  2.6 35.6 %fwd.1 = (bf16[1024,2304]{1,0:T(8,128)(2,1)}, bf16[2048,768]{1,0:T(8,128)(2,1)}, bf16[1024,768]{1,0:T(8,128)(2,1)}, f32[1024,768]{1,0:T(8,128)}, bf16[1024,3072]...) custom-call(bf16[1024,768]{1,0:T(8,128)(2,1)} %bitcast.23, ...), custom_call_target="tpu_custom_call" | custom-call | tf_op jit(solution)/shard_map/fwd/pallas_call | solution.py:153
  38.3 124.5 %bwd.1 = (f32[24,2304]{1,0:T(8,128)}, f32[24,768]{1,0:T(8,128)}, f32[24,3072]{1,0:T(8,128)}, f32[96,768]{1,0:T(8,128)}, f32[1024,768]{1,0:T(8,128)}, /*index=5*/f32[2,8,768]{2,1,0:T(8,128)}) custom-call(bf16[64,1024]{1,0:T(8,128)(2,1)} %get-tuple-element.47.member, f32[64,768]{1,0:T(8,128)} %get-tuple-element.48.pooled, f32[64,128]{1,0:T(8,128)} %get-tuple-element.49.count, ...), custom_call_target="tpu_custom_call" | custom-call | tf_op jit(solution)/shard_map/bwd/pallas_call | solution.py:733
  162.8 4.9 %hand_out.1 = (f32[1,1]{1,0:T(1,128)}, f32[1,1]{1,0:T(1,128)}, f32[1,24]{1,0:T(1,128)}, f32[1,24]{1,0:T(1,128)}, f32[1,24]{1,0:T(1,128)}, /*index=5*/f32[1,24]{1...) custom-call(f32[2,8,768]{2,1,0:T(8,128)} %get-tuple-element.56.vec, ...), custom_call_target="tpu_custom_call" | custom-call | tf_op jit(solution)/shard_map/hand_out/pallas_call | solution.py:776

commit v3 on v2

--- a/solution.py
+++ b/solution.py
@@ -33,6 +33,11 @@
     center = x - jnp.mean(x, axis=-1, keepdims=True)
     spread = lax.rsqrt(jnp.mean(center * center, axis=-1, keepdims=True) + 1e-05)
     return center * spread, spread
+
+
+def split(x, first):
+    zero = jnp.zeros_like(x)
+    return jnp.concatenate([jnp.where(first, x, zero), jnp.where(first, zero, x)], axis=0)
 
 
 def low_pair(x):
@@ -88,21 +93,21 @@
         slot_lanes.append(keyed)
         across = jnp.broadcast_to(keyed.astype(f32), (128, 128))
         bias = jnp.where(across == across.T, 0.0, -1e30)
-        bias = jnp.concatenate([bias, bias], axis=0)
-        t0 = pair * 128
-        for hp in range(HEADS // 2):
-            c0 = hp * 128
-            q = qkv[t0:t0 + 128, c0:c0 + 128] * jnp.asarray(0.125, bf16)
-            k = qkv[t0:t0 + 128, feat + c0:feat + c0 + 128]
-            v = qkv[t0:t0 + 128, 2 * feat + c0:2 * feat + c0 + 128]
-            zero = jnp.zeros_like(q)
-            q2 = jnp.concatenate([jnp.where(first_half, q, zero), jnp.where(first_half, zero, q)], axis=0)
-            s = mm_nt(q2, k) + bias
-            e = jnp.exp(s - jnp.max(s, axis=-1, keepdims=True))
-            p = (e * (1.0 / jnp.sum(e, axis=-1, keepdims=True))).astype(bf16)
-            probs[256 * pair:256 * (pair + 1), c0:c0 + 128] = p
-            o = mm(p, v)
-            mixed[t0:t0 + 128, c0:c0 + 128] = jnp.where(first_half, o[:128], o[128:]).astype(bf16)
+        bias = jnp.concatenate([bias, bias], axis=1)
+        here = slice(pair * 128, pair * 128 + 128)
+        hps = range(HEADS // 2)
+        scores = [mm_nt(qkv[here, feat + 128 * h:feat + 128 * h + 128],
+                        split(qkv[here, 128 * h:128 * h + 128] * jnp.asarray(0.125, bf16), first_half)) + bias
+                  for h in hps]
+        lows = []
+        for h in hps:
+            e = jnp.exp(scores[h] - jnp.max(scores[h], axis=0, keepdims=True))
+            p = (e * (1.0 / jnp.sum(e, axis=0, keepdims=True))).astype(bf16)
+            probs[here, 256 * h:256 * h + 256] = p
+            lows.append(p)
+        for h in hps:
+            o = mm_tn(lows[h], qkv[here, 2 * feat + 128 * h:2 * feat + 128 * h + 128])
+            mixed[here, 128 * h:128 * h + 128] = jnp.where(first_half, o[:128], o[128:]).astype(bf16)
 
     arrive(1)
     hid = x + mm(mixed[...], wo[...]) + ob[...].astype(f32)
@@ -113,8 +118,12 @@
     arrive(3)
     out = hid + sb[...].astype(f32)
     tile = 768
-    for f in range(0, we.shape[1], tile):
-        v = mm(n2, we[:, f:f + tile]) + eb[:, f:f + tile].astype(f32)
+    starts = range(0, we.shape[1], tile)
+    ahead = mm(n2, we[:, :tile])
+    for f in starts:
+        v = ahead + eb[:, f:f + tile].astype(f32)
+        if f + tile < we.shape[1]:
+            ahead = mm(n2, we[:, f + tile:f + 2 * tile])
         v2 = v * v
         cv = v * GELU_C
         t = jnp.tanh(cv * (1.0 + GELU_A * v2))
@@ -145,7 +154,6 @@
     ff = we.shape[1]
     block = STEP_ROWS * length
     steps = count // block
-    pairs = STEP_ROWS // 2
     whole = lambda a: pl.BlockSpec(a.shape, lambda i: (0,) * a.ndim)
     rows = lambda width: pl.BlockSpec((block, width), lambda i: (i, 0))
     anyw = pl.BlockSpec(memory_space=pl.ANY)
@@ -155,13 +163,13 @@
         grid=(steps,),
         in_specs=[rows(feat), whole(segments)] + [whole(a) for a in smalls] + [anyw] * 4,
         out_specs=[rows(3 * feat),
-                   pl.BlockSpec((256 * pairs, feat), lambda i: (i, 0)),
+                   rows(2 * feat),
                    rows(feat), rows(feat), rows(ff), rows(ff),
                    pl.BlockSpec((slots, block), lambda i: (0, i)),
                    pl.BlockSpec((slots, feat), lambda i: (0, 0)),
                    pl.BlockSpec((slots, 128), lambda i: (0, 0))],
         out_shape=[jax.ShapeDtypeStruct((count, 3 * feat), bf16),
-                   jax.ShapeDtypeStruct((steps * pairs * 256, feat), bf16),
+                   jax.ShapeDtypeStruct((count, 2 * feat), bf16),
                    jax.ShapeDtypeStruct((count, feat), bf16),
                    jax.ShapeDtypeStruct((count, feat), f32),
                    jax.ShapeDtypeStruct((count, ff), bf16),
@@ -179,11 +187,14 @@
 
 MESH = pl.DeviceIdType.MESH
 PLANE = 8
+LINE = 4
 BLK = 256
 CH = 768
 HALF = CH // 2
 ROWS = HALF // PLANE
 N_CH = 12
+LONG = (1, 3, 5, 7, 8, 10)
+SHORT = (9, 11)
 
 
 def fold(x):
@@ -193,15 +204,17 @@
 def bwd_kernel(member, pooled, count, caption, scale, g1, b1, g2, b2,
                qkv_h, probs_h, mixed_h, hidden_h, act_h, slope_h, tok_h, w3_h, wo_h, we_h, ws_h,
                tw_out, ow_out, ew_out, sw_out, in_out, vec_out,
-               cs, snd, prv, own, prcv, swrcv, fin, swfin,
-               gol, gn2, hid, spread2, n2b, n1b, tok, act, slope, ws, we, ge, qkv, w3, wo, inbuf,
-               imgs, elow, ebsum, attn_sum, vec, vecrcv, vecall,
-               ld, psend, precv, xsend, xrecv, plsend, plrecv, swsend, swrecv, fsend, frecv, fout,
-               gsend, grecv, esend, erecv, vsend, vrecv, outsem):
+               cs, snd, prv, own, yrcv, ysw, zrcv, arcv, swrcv, fin, swfin,
+               gol, gn2, hid, spread2, n2b, tok, act, slope, ws, we, ge, qkv, w3, wo,
+               imgs, elow, ebsum, attn_sum, vec, vown, vpair, vrcv,
+               ld, psend, precv, xsend, xrecv, ysend, yrecv, yswsend, yswrecv, zsend, zrecv, asend, arecv,
+               swsend, swrecv, fsem, swfsem, gsem, esem, vpsem, vsem, outsem):
     t = lax.axis_index("tower")
     d = lax.axis_index("dp")
     p = d // 2
     c = lax.rem(d, 2)
+    z = p // 2
+    y = lax.rem(p, 2)
     is_text = t == 1
     count_t = gol.shape[0]
     blocks = count_t // BLK
@@ -216,6 +229,8 @@
         return (tt, pp * 2 + c)
 
     partner = (t, p * 2 + other)
+    beside = at_core(t, 2 * z + (1 - y))
+    across = at_core(1 - t, p)
 
     def remote(src, dst, ssem, rsem, dev):
         return pltpu.make_async_remote_copy(src_ref=src, dst_ref=dst, send_sem=ssem, recv_sem=rsem,
@@ -223,7 +238,7 @@
 
     barrier = pltpu.get_barrier_semaphore()
     pl.semaphore_signal(barrier, inc=1, device_id=partner, device_id_type=MESH)
-    pl.semaphore_signal(barrier, inc=1, device_id=at_core(1 - t, p), device_id_type=MESH)
+    pl.semaphore_signal(barrier, inc=1, device_id=across, device_id_type=MESH)
     for k in range(1, PLANE):
         pl.semaphore_signal(barrier, inc=1, device_id=at_core(t, peer(k)), device_id_type=MESH)
         pl.semaphore_signal(barrier, inc=1, device_id=at_core(1 - t, peer(k)), device_id_type=MESH)
@@ -233,71 +248,96 @@
     emb = pooled_v * inverse
     emb_low = emb.astype(bf16)
 
-    def lane(q):
-        return jnp.where(q < 8, q // 2, q - 4)
-
     def pair_copy(q):
-        return remote(snd.at[lax.rem(q, 2)], prv.at[q], psend.at[q], precv.at[q], partner)
-
-    def x_copy(q):
-        return remote(cs.at[q, 0:HALF], cs.at[q, 0:HALF], xsend.at[q], xrecv.at[q], at_core(1 - t, p))
-
-    def plane_copy(q, k):
-        row = pl.multiple_of(HALF * t + ROWS * peer(k), 16)
-        return remote(cs.at[q, pl.ds(row, ROWS)], prcv.at[lane(q), k], plsend.at[q, k], plrecv.at[q, k],
-                      at_core(t, peer(k)))
-
-    def sw_copy(q, zz, y):
-        to = 2 * zz + y
-        k = lax.rem(to - p + PLANE, PLANE)
-        row = pl.multiple_of(HALF * t + 4 * ROWS * y, 16)
-        return remote(cs.at[q, pl.ds(row, 4 * ROWS)], swrcv.at[k], swsend.at[zz, y], swrecv.at[k], at_core(t, to))
-
-    def plane_send(q):
+        slot = lax.rem(q, 2)
+        return remote(snd.at[slot], prv.at[q], psend.at[slot], precv.at[q], partner)
+
+    def x_all(q):
+        return remote(cs.at[q, 0:LINE], cs.at[q, 0:LINE], xsend.at[q], xrecv.at[q], across)
+
+    def x_line(q):
+        return remote(cs.at[q, 0:LINE, y], cs.at[q, 0:LINE, y], xsend.at[q], xrecv.at[q], across)
+
+    def y_copy(q):
+        return remote(cs.at[q, :, 1 - y], yrcv.at[q // 2], ysend.at[q // 2], yrecv.at[q // 2], beside)
+
+    def z_start(q):
+        for k in range(1, LINE):
+            to = lax.rem(z + k, LINE)
+            remote(cs.at[q, LINE * t + to, y], zrcv.at[q // 2, k - 1], zsend.at[q // 2], zrecv.at[q // 2],
+                   at_core(t, 2 * to + y)).start()
+
+    def z_all(q):
+        return remote(zrcv.at[q // 2], zrcv.at[q // 2], zsend.at[q // 2], zrecv.at[q // 2], partner)
+
+    def a_start(q):
         for k in range(1, PLANE):
-            plane_copy(q, k).start()
-
-    def sw_send(q, zz):
-        for y in range(2):
-            @pl.when(p != 2 * zz + y)
-            def _():
-                sw_copy(q, zz, y).start()
-
-    def sw_sent(q, zz):
-        for y in range(2):
-            @pl.when(p != 2 * zz + y)
-            def _():
-                sw_copy(q, zz, y).wait_send()
+            to = peer(k)
+            remote(cs.at[q, LINE * t + to // 2, lax.rem(to, 2)], arcv.at[(q - 9) // 2, k - 1],
+                   asend.at[(q - 9) // 2], arecv.at[(q - 9) // 2], at_core(t, to)).start()
+
+    def a_all(q):
+        a = (q - 9) // 2
+        return remote(arcv.at[a], arcv.at[a], asend.at[a], arecv.at[a], partner)
+
+    def ysw_copy(i):
+        return remote(cs.at[2 * i, pl.ds(LINE * t + 2 * (1 - y), 2)], ysw.at[i], yswsend.at[i], yswrecv.at[i], beside)
+
+    def sw_z(i):
+        k = lax.rem(i - z + LINE, LINE)
+        return remote(cs.at[2 * i, pl.ds(LINE * t + 2 * y, 2)], swrcv.at[jnp.maximum(k, 1) - 1], swsend,
+                      swrecv, at_core(t, 2 * i + y))
+
+    def sw_mid(i):
+        ysw_copy(i).wait_recv()
+        for a in range(2):
+            at = LINE * t + 2 * y + a
+            cs[2 * i, at] = (cs[2 * i, at].astype(f32) + ysw[i, a].astype(f32)).astype(bf16)
+
+        @pl.when(z != i)
+        def _():
+            sw_z(i).start()
+
+    def long_mid(q):
+        y_copy(q).wait_recv()
+        for a in range(PLANE):
+            cs[q, a, y] = (cs[q, a, y].astype(f32) + yrcv[q // 2, a].astype(f32)).astype(bf16)
+        x_line(q).start()
+        z_start(q)
 
     def chip_sum(q):
         pair_copy(q).wait_recv()
         slot = lax.rem(q, 2)
-        for r in range(0, CH, 128):
-            cs[q, r:r + 128, :] = (own[slot, r:r + 128, :] + prv[q, r:r + 128, :].astype(f32)).astype(bf16)
-        x_copy(q).start()
-
-    def chunk(q, left, right_of):
+        n = 2 * ROWS
+        for a in range(PLANE):
+            total = own[slot, n * a:n * (a + 1), :] + prv[q, n * a:n * (a + 1), :].astype(f32)
+            cs[q, a] = total.reshape(2, ROWS, HALF).astype(bf16)
+
+    def chunk(q, left, right):
         slot = lax.rem(q, 2)
 
         @pl.when(q >= 2)
         def _():
             pair_copy(q - 2).wait_send()
-        for mine in (False, True):
-            right = right_of(c if mine else other)
-            for r in range(0, CH, 256):
-                part = mm_tn(left[:, r:r + 256], right)
-                if mine:
-                    own[slot, r:r + 256, :] = part
-                else:
-                    snd[slot, r:r + 256, :] = part.astype(bf16)
-            if not mine:
-                pair_copy(q).start()
-
-    def gather_copy(k):
-        return remote(elow, imgs.at[c, p], gsend.at[k], grecv.at[k], at_core(1 - t, peer(k)))
-
-    def share_copy():
-        return remote(imgs.at[c], imgs.at[c], esend, erecv, partner)
+        for r in range(0, CH, 256):
+            part = mm_tn(left[:, r:r + 256], right)
+            low, high = part[:, :HALF], part[:, HALF:]
+            own[slot, r:r + 256, :] = jnp.where(c == 0, low, high)
+            snd[slot, r:r + 256, :] = jnp.where(c == 0, high, low).astype(bf16)
+        pair_copy(q).start()
+
+    def gather_start():
+        for k in range(PLANE):
+            remote(elow, imgs.at[c, p], gsem.at[0], gsem.at[1], at_core(1 - t, peer(k))).start()
+
+    def gather_all():
+        return remote(imgs.at[c], imgs.at[c], gsem.at[0], gsem.at[1], partner)
+
+    def share_copy(h):
+        return remote(imgs.at[h], imgs.at[h], esem.at[0], esem.at[1], partner)
+
+    def v_pair():
+        return remote(vown.at[other], vpair, vpsem.at[0], vpsem.at[1], partner)
 
     def load(n, src, dst):
         return pltpu.make_async_copy(src, dst, ld.at[n])
@@ -321,33 +361,42 @@
     w3_load = load(19, w3_h, w3)
     wo_load = load(20, wo_h, wo)
     mixed_load = load(21, mixed_h, slope.at[0])
-    probs_loads = [load(22 + h, probs_h.at[pl.ds(count_t * h, count_t)], act.at[h]) for h in range(2)]
+    probs_loads = [load(22 + h, probs_h.at[:, pl.ds(feat * h, feat)], act.at[h]) for h in range(2)]
 
     @pl.when(t == 0)
     def _():
         elow[...] = emb_low[:rows_here]
         pl.semaphore_wait(barrier, 2 * PLANE)
-        for k in range(PLANE):
-            gather_copy(k).start()
-        inbuf[0] = jnp.zeros_like(inbuf[0])
+        gather_start()
+        gn2[:BLK, :] = jnp.zeros((BLK, feat), f32)
         for m in range(blocks):
-            pltpu.make_async_copy(inbuf.at[0], in_out.at[pl.ds(BLK * m, BLK)], outsem.at[m]).start()
-
-        @pl.loop(0, 4)
+            pltpu.make_async_copy(gn2.at[0:BLK], in_out.at[pl.ds(BLK * m, BLK)], outsem.at[m]).start()
+
+        @pl.loop(0, 6)
         def _(i):
-            x_copy(2 * i).wait_recv()
-            sw_send(2 * i, i)
-            x_copy(2 * i + 1).wait_recv()
-            plane_send(2 * i + 1)
-
-        @pl.loop(8, N_CH)
-        def _(q):
-            x_copy(q).wait_recv()
-            plane_send(q)
-        for k in range(PLANE):
-            gather_copy(k).wait_send()
+            @pl.when(i < 4)
+            def _():
+                x_all(2 * i).wait_recv()
+                ysw_copy(i).start()
+
+            @pl.when((i >= 1) & (i <= 4))
+            def _():
+                sw_mid(i - 1)
+
+            @pl.when(i >= 2)
+            def _():
+                x_line(2 * i - 3).wait_recv()
+                z_start(2 * i - 3)
+        for q in (9, 8, 11, 10):
+            if q in SHORT:
+                x_all(q).wait_recv()
+                a_start(q)
+            else:
+                x_line(q).wait_recv()
+                z_start(q)
+        gather_all().wait_send()
         for m in range(blocks):
-            pltpu.make_async_copy(inbuf.at[0], in_out.at[pl.ds(BLK * m, BLK)], outsem.at[m]).wait()
+            pltpu.make_async_copy(gn2.at[0:BLK], in_out.at[pl.ds(BLK * m, BLK)], outsem.at[m]).wait()
 
     @pl.when(is_text)
     def _():
@@ -371,22 +420,14 @@
             n2b[here, :] = (norm * gain2 + shift2).astype(bf16)
             hid[here, :] = norm
             spread2[here, :] = spread
-        tok_load.wait()
-
-        @pl.loop(0, blocks)
-        def _(m):
-            here = pl.ds(pl.multiple_of(m * BLK, BLK), BLK)
-            norm, _s = stats(tok[here, :].astype(f32))
-            n1b[here, :] = (norm * gain1 + shift1).astype(bf16)
         gn2[...] = jnp.zeros_like(gn2)
         attn_sum[...] = jnp.zeros_like(attn_sum)
         vec[...] = jnp.zeros_like(vec)
         pl.semaphore_wait(barrier, 2 * PLANE)
-        for k in range(PLANE):
-            gather_copy(k).wait_recv()
-        share_copy().start()
-        share_copy().wait_send()
-        remote(imgs.at[other], imgs.at[other], esend, erecv, partner).wait_recv()
+        gather_all().wait_recv()
+        share_copy(c).start()
+        share_copy(c).wait_send()
+        share_copy(other).wait_recv()
 
         table = imgs[...].reshape(2 * PLANE * rows_here, feat)
         dots = mm_nt(emb_low, table)
@@ -419,12 +460,12 @@
             s = lax.rem(i, 2)
             for cp in tile_loads(i):
                 cp.wait()
-            chunk(2 * i, act.at[s], lambda h: gol[:, pl.ds(pl.multiple_of(HALF * h, 128), HALF)])
+            chunk(2 * i, act.at[s], gol[...])
 
             @pl.when(i > 0)
             def _():
                 chip_sum(2 * i - 1)
-                plane_send(2 * i - 1)
+                y_copy(2 * i - 1).start()
             sums = jnp.zeros((8, feat), f32)
             for m in range(blocks):
                 here = slice(BLK * m, BLK * (m + 1))
@@ -434,12 +475,21 @@
             sums = jnp.sum(sums, axis=0, keepdims=True)
             for h in range(2):
                 ebsum[:, pl.ds(pl.multiple_of(4 * HALF * h + HALF * i, 128), HALF)] = sums[:, HALF * h:HALF * (h + 1)]
-            chunk(2 * i + 1, n2b, lambda h: ge[:, pl.ds(pl.multiple_of(HALF * h, 128), HALF)])
+            chunk(2 * i + 1, n2b, ge[...])
             chip_sum(2 * i)
-            sw_send(2 * i, i)
+            x_all(2 * i).start()
+            ysw_copy(i).start()
+
+            @pl.when(i > 0)
+            def _():
+                sw_mid(i - 1)
             for m in range(blocks):
                 here = slice(BLK * m, BLK * (m + 1))
                 gn2[here, :] += mm_nt(ge[here, :], we[s])
+
+            @pl.when(i >= 2)
+            def _():
+                long_mid(2 * i - 3)
 
             @pl.when(i < 2)
             def _():
@@ -452,7 +502,7 @@
                 probs_loads[0].start()
         probs_loads[1].start()
         chip_sum(7)
-        plane_send(7)
+        y_copy(7).start()
 
         zeros8 = jnp.zeros((8, feat), f32)
 
@@ -473,235 +523,231 @@
             vec[row:row + 1, :] = jnp.sum(x, axis=0, keepdims=True)
         for n in range(4):
             vec[8 + n:9 + n, :] = ebsum[:, feat * n:feat * (n + 1)]
+        sw_mid(3)
 
         mixed_load.wait()
-        chunk(8, slope.at[0], lambda h: gol[:, pl.ds(pl.multiple_of(HALF * h, 128), HALF)])
+        chunk(8, slope.at[0], gol[...])
         wo_load.wait()
         for m in range(blocks):
             here = slice(BLK * m, BLK * (m + 1))
             ge[here, :] = mm_nt(gol[here, :], wo[...]).astype(bf16)
         chip_sum(8)
-        plane_send(8)
+        y_copy(8).start()
+        long_mid(5)
 
         qkv_load.wait()
         for cp in probs_loads:
             cp.wait()
         first_half = lax.broadcasted_iota(jnp.int32, (128, 128), 1) < 64
-
-        def split(x):
-            zero = jnp.zeros_like(x)
-            return jnp.concatenate([jnp.where(first_half, x, zero), jnp.where(first_half, zero, x)], axis=0)
+        hps = range(HEADS // 2)
 
         @pl.loop(0, count_t // 128)
         def _(rp):
             here = pl.ds(pl.multiple_of(rp * 128, 128), 128)
-            half = rp // (count_t // 256)
-            prow = pl.ds(pl.multiple_of(lax.rem(rp, count_t // 256) * 256, 256), 256)
-            for hp in range(HEADS // 2):
-                c0 = hp * 128
-                q, k, v = (qkv[here, feat * n + c0:feat * n + c0 + 128] for n in range(3))
-                gm2 = split(ge[here, c0:c0 + 128])
-                probs = act[half, prow, c0:c0 + 128]
-                probs_f = probs.astype(f32)
-                gp = mm_nt(gm2, v)
-                weighted = probs_f * gp
-                gs = (weighted - probs_f * jnp.sum(weighted, axis=1, keepdims=True)).astype(bf16)
-                gv = mm_tn(probs, gm2)
-                gk = mm_tn(gs, split(q)) * 0.125
-                gq2 = mm(gs, k)
-                gq = jnp.where(first_half, gq2[:128], gq2[128:]) * 0.125
-                for n, x in ((0, gq), (1, gk), (2, gv)):
-                    qkv[here, feat * n + c0:feat * n + c0 + 128] = x.astype(bf16)
-                    if n != 1:
-                        at = slice((feat if n else 0) + c0, (feat if n else 0) + c0 + 128)
-                        attn_sum[:, at] += fold(x)
+
+            def probs_of(h):
+                return act[h // 3, here, 256 * (h % 3):256 * (h % 3) + 256]
+
+            def part(n, h):
+                return qkv[here, feat * n + 128 * h:feat * n + 128 * h + 128]
+            gm = [split(ge[here, 128 * h:128 * h + 128], first_half) for h in hps]
+            gp = [mm_nt(part(2, h), gm[h]) for h in hps]
+            gv = [mm(probs_of(h), gm[h]) for h in hps]
+            gs = []
+            for h in hps:
+                probs_f = probs_of(h).astype(f32)
+                weighted = probs_f * gp[h]
+                gs.append((weighted - probs_f * jnp.sum(weighted, axis=0, keepdims=True)).astype(bf16))
+            gk = [mm(gs[h], split(part(0, h), first_half)) * 0.125 for h in hps]
+            gq = []
+            for h in hps:
+                both = mm_tn(gs[h], part(1, h))
+                gq.append(jnp.where(first_half, both[:128], both[128:]) * 0.125)
+            for h in hps:
+                for n, x in ((0, gq[h]), (1, gk[h]), (2, gv[h])):
+                    qkv[here, feat * n + 128 * h:feat * n + 128 * h + 128] = x.astype(bf16)
+                for n, x in ((0, gq[h]), (1, gv[h])):
+                    attn_sum[:, feat * n + 128 * h:feat * n + 128 * h + 128] += fold(x)
         vec[2:3, :] = jnp.sum(attn_sum[:, :feat], axis=0, keepdims=True)
         vec[3:4, :] = jnp.sum(attn_sum[:, feat:], axis=0, keepdims=True)
 
+        tok_load.wait()
+
+        @pl.loop(0, blocks)
+        def _(m):
+            here = pl.ds(pl.multiple_of(m * BLK, BLK), BLK)
+            norm, _s = stats(tok[here, :].astype(f32))
+            slope[1, here, :] = (norm * gain1 + shift1).astype(bf16)
+
         @pl.loop(0, 3)
         def _(j):
-            chunk(9 + j, n1b, lambda h: qkv[:, pl.ds(pl.multiple_of(CH * j + HALF * h, 128), HALF)])
-
-            @pl.when(j > 0)
+            chunk(9 + j, slope.at[1], qkv[:, pl.ds(pl.multiple_of(CH * j, 128), CH)])
+
+            @pl.when(j == 1)
             def _():
-                chip_sum(8 + j)
-                plane_send(8 + j)
+                chip_sum(9)
+                x_all(9).start()
+                a_start(9)
+                long_mid(7)
+        chip_sum(10)
+        y_copy(10).start()
+        long_mid(8)
         w3_load.wait()
 
         def norm1_back(m, sums):
             here = pl.ds(pl.multiple_of(m * BLK, BLK), BLK)
-            slot = lax.rem(m, 2)
-
-            def out_copy(mm_):
-                return pltpu.make_async_copy(inbuf.at[lax.rem(mm_, 2)],
-                                             in_out.at[pl.ds(pl.multiple_of(mm_ * BLK, BLK), BLK)], outsem.at[mm_])
-
             g_in = mm_nt(qkv[here, :], w3[...])
 
             @pl.when(m == 0)
             def _():
                 chip_sum(11)
-                plane_send(11)
-
-            @pl.when(m >= 2)
-            def _():
-                out_copy(m - 2).wait()
+                x_all(11).start()
+                a_start(11)
+
             norm, spread = stats(tok[here, :].astype(f32))
             g = g_in * gain1
             back = spread * (g - jnp.mean(g, axis=1, keepdims=True)
                              - norm * jnp.mean(g * norm, axis=1, keepdims=True))
-            inbuf[slot] = gn2[here, :] + back
-            out_copy(m).start()
+            gn2[here, :] += back
+            pltpu.make_async_copy(gn2.at[here], in_out.at[here], outsem.at[m]).start()
             return (sums[0] + fold(g_in * norm), sums[1] + fold(g_in))
         sums = lax.fori_loop(0, blocks, norm1_back, (zeros8, zeros8))
         for row, x in ((0, sums[0]), (1, sums[1])):
             vec[row:row + 1, :] = jnp.sum(x, axis=0, keepdims=True)
-        for m in (blocks - 2, blocks - 1):
-            pltpu.make_async_copy(inbuf.at[m % 2], in_out.at[pl.ds(BLK * m, BLK)], outsem.at[m]).wait()
-
-    mine8 = pl.ds(pl.multiple_of(8 * c, 8), 8)
-    their8 = pl.ds(pl.multiple_of(8 * other, 8), 8)
-
-    def v_pair():
-        return remote(vec.at[their8], vecrcv.at[0], vsend.at[0], vrecv.at[0], partner)
-
-    def v_plane(k):
-        return remote(vec.at[mine8], vecrcv.at[k], vsend.at[k], vrecv.at[k], at_core(t, peer(k)))
-
-    def v_share(half):
-        return remote(vecall.at[half], vecall.at[half], vsend.at[8], vrecv.at[8], partner)
-
-    def v_across():
-        return remote(vecall, vecall, vsend.at[9], vrecv.at[9], at_core(1 - t, p))
-
-    @pl.when(is_text)
-    def _():
+
+        width, wide = feat // (4 * PLANE), 4 * feat // (4 * PLANE)
+        narrow = vec[0:8, :]
+        broad = vec[8:16, :]
+        scalars = vec[12:13, :128]
+        turned = [broad] + [pltpu.roll(broad, feat - wide * j, axis=1) for j in range(1, feat // wide)]
+        for g in range(4 * PLANE):
+            one = narrow if g == 0 else pltpu.roll(narrow, feat - width * g, axis=1)
+            row = g // (feat // wide)
+            tail = turned[g % (feat // wide)][row:row + 1, :128]
+            vown[g % 2, g // 2, 0:8, :] = one[:, :128]
+            vown[g % 2, g // 2, 8:9, :] = tail
+            vown[g % 2, g // 2, 9:10, :] = scalars
         v_pair().start()
+        for m in range(blocks):
+            here = pl.ds(BLK * m, BLK)
+            pltpu.make_async_copy(gn2.at[here], in_out.at[here], outsem.at[m]).wait()
         v_pair().wait_recv()
-        vec[mine8, :] += vecrcv[0]
-        for k in range(1, PLANE):
-            v_plane(k).start()
-
-    def total_of(block, get):
-        out = block
-        for k in range(1, PLANE):
-            out = out + get(k).astype(f32)
-        return out
-
-    def finish(q, out, col, base):
-        for k in range(1, PLANE):
-            plane_copy(q, k).wait_recv()
-        row = pl.multiple_of(HALF * t + ROWS * p, 16)
-        fin[lane(q)] = total_of(cs[q, pl.ds(row, ROWS), :].astype(f32), lambda k: prcv[lane(q), k])
-        keep_copy(q, out, col).start()
-        give_copy(q, out, col).start()
-
-    def keep_copy(q, out, col):
-        n = ROWS // 2
-        return pltpu.make_async_copy(fin.at[lane(q), pl.ds(pl.multiple_of(n * c, 8), n)], out.at[:, pl.ds(col, HALF)],
-                                     fout.at[q])
-
-    def give_copy(q, out, col):
-        n = ROWS // 2
-        return remote(fin.at[lane(q), pl.ds(pl.multiple_of(n * other, 8), n)], out.at[:, pl.ds(col, HALF)],
-                      fsend.at[q], frecv.at[q], partner)
+        vown[c] += vpair[...]
+        for k in range(PLANE):
+            for tt in range(2):
+                if tt == 0 or k:
+                    remote(vown.at[c, PLANE * tt + peer(k)], vrcv.at[k], vsem.at[0], vsem.at[1],
+                           at_core(tt, peer(k))).start()
+        long_mid(10)
+
+    half_rows = ROWS // 2
+
+    def keep(n, out, col):
+        return pltpu.make_async_copy(fin.at[n, pl.ds(pl.multiple_of(half_rows * c, 8), half_rows)],
+                                     out.at[:, pl.ds(col, HALF)], fsem.at[0])
+
+    def give(n, out, col):
+        return remote(fin.at[n, pl.ds(pl.multiple_of(half_rows * other, 8), half_rows)],
+                      out.at[:, pl.ds(col, HALF)], fsem.at[1], fsem.at[2], partner)
+
+    def hand_over(n, total, out, col):
+        fin[n] = total
+        keep(n, out, col).start()
+        give(n, out, col).start()
+
+    def finish_long(q, out, col):
+        z_all(q).wait_recv()
+        total = cs[q, LINE * t + z, y].astype(f32)
+        for k in range(LINE - 1):
+            total = total + zrcv[q // 2, k].astype(f32)
+        hand_over(q // 2, total, out, col)
+
+    def finish_short(q, out, col):
+        a_all(q).wait_recv()
+        total = cs[q, LINE * t + z, y].astype(f32)
+        for k in range(PLANE - 1):
+            total = total + arcv[(q - 9) // 2, k].astype(f32)
+        hand_over(len(LONG) + (q - 9) // 2, total, out, col)
+
+    def sw_all():
+        return remote(swrcv, swrcv, swsend, swrecv, partner)
 
     def sw_keep():
         n = 2 * ROWS
         return pltpu.make_async_copy(swfin.at[pl.ds(pl.multiple_of(n * c, 8), n)],
-                                     sw_out.at[:, pl.ds(pl.multiple_of(HALF * c, 128), HALF)], fout.at[0])
+                                     sw_out.at[:, pl.ds(pl.multiple_of(HALF * c, 128), HALF)], swfsem.at[0])
 
     def sw_give():
         n = 2 * ROWS
         return remote(swfin.at[pl.ds(pl.multiple_of(n * other, 8), n)],
-                      sw_out.at[:, pl.ds(pl.multiple_of(HALF * c, 128), HALF)], fsend.at[0], frecv.at[0], partner)
-
-    def wait_frecv(q, out, col_other):
-        n = ROWS // 2
-        remote(fin.at[lane(q), pl.ds(pl.multiple_of(n * other, 8), n)], out.at[:, pl.ds(col_other, HALF)],
-               fsend.at[q], frecv.at[q], partner).wait_recv()
-
-    for k in range(1, PLANE):
-        remote(cs.at[0, 0:4 * ROWS], swrcv.at[k], swsend.at[0, 0], swrecv.at[k], partner).wait_recv()
-    sw_q = 2 * (p // 2)
-    sw_row = pl.multiple_of(HALF * t + 4 * ROWS * lax.rem(p, 2), 16)
-    swfin[...] = total_of(cs[sw_q, pl.ds(sw_row, 4 * ROWS), :].astype(f32), lambda k: swrcv[k])
+                      sw_out.at[:, pl.ds(pl.multiple_of(HALF * c, 128), HALF)], swfsem.at[1], swfsem.at[2], partner)
+
+    sw_all().wait_recv()
+    for a in range(2):
+        total = cs[2 * z, LINE * t + 2 * y + a].astype(f32)
+        for k in range(LINE - 1):
+            total = total + swrcv[k, a].astype(f32)
+        swfin[2 * ROWS * a:2 * ROWS * (a + 1), :] = total.reshape(2 * ROWS, HALF)
     sw_keep().start()
     sw_give().start()
 
-    def ew_col(i, h):
-        return pl.multiple_of(4 * HALF * h + HALF * i, 128)
-
-    def tw_col(j, h):
-        return pl.multiple_of(CH * j + HALF * h, 128)
-
-    def ow_col(h):
-        return pl.multiple_of(HALF * h, 128)
-
     @pl.loop(0, 4)
     def _(i):
-        finish(2 * i + 1, ew_out, ew_col(i, c), None)
-    finish(8, ow_out, ow_col(c), None)
-
-    @pl.loop(0, 3)
-    def _(j):
-        finish(9 + j, tw_out, tw_col(j, c), None)
+        finish_long(2 * i + 1, ew_out, pl.multiple_of(4 * HALF * c + HALF * i, 128))
+    finish_short(9, tw_out, pl.multiple_of(HALF * c, 128))
+    finish_long(8, ow_out, pl.multiple_of(HALF * c, 128))
+    finish_short(11, tw_out, pl.multiple_of(2 * CH + HALF * c, 128))
+    finish_long(10, tw_out, pl.multiple_of(CH + HALF * c, 128))
 
     @pl.when(is_text)
     def _():
+        remote(vrcv.at[1:PLANE], vrcv.at[1:PLANE], vsem.at[0], vsem.at[1], partner).wait_recv()
+        total = vown[c, PLANE + p]
         for k in range(1, PLANE):
-            v_plane(k).wait_recv()
-        vecall[c] = total_of(vec[mine8, :], lambda k: vecrcv[k])
-        v_share(c).start()
-        v_share(other).wait_recv()
-        v_across().start()
-        v_across().wait_send()
-        v_share(c).wait_send()
+            total = total + vrcv[k]
+        vec_out[...] = total
+
+    @pl.when(t == 0)
+    def _():
+        remote(vrcv, vrcv, vsem.at[0], vsem.at[1], partner).wait_recv()
+        total = vrcv[0]
+        for k in range(1, PLANE):
+            total = total + vrcv[k]
+        vec_out[...] = total
+
+    @pl.when(is_text)
+    def _():
+        everything = vown.at[0, 0:2 * PLANE - 1]
+        remote(everything, everything, vsem.at[0], vsem.at[1], partner).wait_send()
         v_pair().wait_send()
-        for k in range(1, PLANE):
-            v_plane(k).wait_send()
         for q in (N_CH - 2, N_CH - 1):
             pair_copy(q).wait_send()
 
-        @pl.loop(0, N_CH)
-        def _(q):
-            x_copy(q).wait_send()
-
-    @pl.when(t == 0)
-    def _():
-        v_across().wait_recv()
-    vec_out[...] = vecall[...]
+        @pl.loop(0, 4)
+        def _(i):
+            x_all(2 * i).wait_send()
+            x_line(2 * i + 1).wait_send()
+            y_copy(2 * i + 1).wait_send()
+        for q in (8, 10):
+            x_line(q).wait_send()
+            y_copy(q).wait_send()
+        for q in SHORT:
+            x_all(q).wait_send()
 
     @pl.loop(0, 4)
     def _(i):
-        sw_sent(2 * i, i)
-        for k in range(1, PLANE):
-            plane_copy(2 * i + 1, k).wait_send()
-        keep_copy(2 * i + 1, ew_out, ew_col(i, c)).wait()
-        give_copy(2 * i + 1, ew_out, ew_col(i, c)).wait_send()
-        wait_frecv(2 * i + 1, ew_out, ew_col(i, other))
-
-    @pl.loop(8, N_CH)
-    def _(q):
-        for k in range(1, PLANE):
-            plane_copy(q, k).wait_send()
-    keep_copy(8, ow_out, ow_col(c)).wait()
-    give_copy(8, ow_out, ow_col(c)).wait_send()
-    wait_frecv(8, ow_out, ow_col(other))
-
-    @pl.loop(0, 3)
-    def _(j):
-        keep_copy(9 + j, tw_out, tw_col(j, c)).wait()
-        give_copy(9 + j, tw_out, tw_col(j, c)).wait_send()
-        wait_frecv(9 + j, tw_out, tw_col(j, other))
+        ysw_copy(i).wait_send()
+        z_all(2 * i + 1).wait_send()
+    for q in (8, 10):
+        z_all(q).wait_send()
+    for q in SHORT:
+        a_all(q).wait_send()
+    sw_all().wait_send()
     sw_keep().wait()
-    sw_give().wait_send()
-    remote(swfin.at[pl.ds(0, 2 * ROWS)], sw_out.at[:, pl.ds(pl.multiple_of(HALF * other, 128), HALF)],
-           fsend.at[0], frecv.at[0], partner).wait_recv()
-
-    @pl.when(is_text)
-    def _():
-        pass
+    sw_give().wait()
+    lower = fin.at[:, 0:half_rows]
+    pltpu.make_async_copy(lower, lower, fsem.at[0]).wait()
+    remote(lower, lower, fsem.at[1], fsem.at[2], partner).wait()
 
 
 def backward(member, pooled, count, caption, scale, g1, b1, g2, b2,
@@ -715,27 +761,29 @@
     sspec = pl.BlockSpec(memory_space=pltpu.SMEM)
     anyw = pl.BlockSpec(memory_space=pl.ANY)
     shape = jax.ShapeDtypeStruct
+    longs, shorts = len(LONG), len(SHORT)
     scratch = [
-        vm((N_CH, CH, HALF), bf16), vm((2, CH, HALF), bf16), vm((N_CH, CH, HALF), bf16), vm((2, CH, HALF), f32),
-        vm((N_CH - 4, PLANE, ROWS, HALF), bf16), vm((PLANE, 4 * ROWS, HALF), bf16),
-        vm((N_CH - 4, ROWS, HALF), f32), vm((4 * ROWS, HALF), f32),
+        vm((N_CH, PLANE, 2, ROWS, HALF), bf16), vm((2, CH, HALF), bf16), vm((N_CH, CH, HALF), bf16),
+        vm((2, CH, HALF), f32),
+        vm((longs, PLANE, ROWS, HALF), bf16), vm((4, 2, 2, ROWS, HALF), bf16), vm((longs, LINE - 1, ROWS, HALF), bf16),
+        vm((shorts, PLANE - 1, ROWS, HALF), bf16), vm((LINE - 1, 2, 2, ROWS, HALF), bf16),
+        vm((longs + shorts, ROWS, HALF), f32), vm((4 * ROWS, HALF), f32),
         vm((n_tok, feat), bf16), vm((n_tok, feat), f32), vm((n_tok, feat), f32), vm((n_tok, 1), f32),
-        vm((n_tok, feat), bf16), vm((n_tok, feat), bf16), vm((n_tok, feat), bf16),
+        vm((n_tok, feat), bf16), vm((n_tok, feat), bf16),
         vm((2, n_tok, CH), bf16), vm((2, n_tok, CH), bf16), vm((2, CH, feat), bf16), vm((2, feat, CH), bf16),
         vm((n_tok, feat), bf16), vm((n_tok, 3 * feat), bf16), vm(w3.shape, bf16), vm(wo.shape, bf16),
-        vm((2, BLK, feat), f32),
         vm((2, PLANE, rows_here, feat), bf16), vm((rows_here, feat), bf16), vm((1, ff), f32), vm((8, 2 * feat), f32),
-        vm((16, feat), f32), vm((PLANE, 8, feat), f32), vm((2, 8, feat), f32),
-        dma((24,)), dma((N_CH,)), dma((N_CH,)), dma((N_CH,)), dma((N_CH,)), dma((N_CH, PLANE)), dma((N_CH, PLANE)),
-        dma((4, 2)), dma((PLANE,)), dma((N_CH,)), dma((N_CH,)), dma((N_CH,)),
-        dma((PLANE,)), dma((PLANE,)), dma, dma, dma((10,)), dma((10,)), dma((n_tok // BLK,)),
+        vm((16, feat), f32), vm((2, 2 * PLANE, 16, 128), f32), vm((2 * PLANE, 16, 128), f32), vm((PLANE, 16, 128), f32),
+        dma((24,)), dma((2,)), dma((N_CH,)), dma((N_CH,)), dma((N_CH,)), dma((longs,)), dma((longs,)),
+        dma((4,)), dma((4,)), dma((longs,)), dma((longs,)), dma((shorts,)), dma((shorts,)),
+        dma, dma, dma((3,)), dma((3,)), dma((2,)), dma((2,)), dma((2,)), dma((2,)), dma((n_tok // BLK,)),
     ]
     return pl.pallas_call(
         bwd_kernel,
         in_specs=[vspec] * 4 + [sspec] + [vspec] * 4 + [anyw] * 11,
         out_specs=[anyw] * 5 + [vspec],
         out_shape=[shape((ROWS // 2, 3 * feat), f32), shape((ROWS // 2, feat), f32), shape((ROWS // 2, ff), f32),
-                   shape((2 * ROWS, feat), f32), shape((n_tok, feat), f32), shape((2, 8, feat), f32)],
+                   shape((2 * ROWS, feat), f32), shape((n_tok, feat), f32), shape((16, 128), f32)],
         scratch_shapes=scratch,
         compiler_params=pltpu.CompilerParams(vmem_limit_bytes=61 << 20, collective_id=0, has_side_effects=True),
         name="bwd",
@@ -751,23 +799,17 @@
     def _():
         for src, dst in zip((tw, ow, ew, sw), bigs):
             dst[...] = src[...]
-        feat = vec.shape[2]
-        width = smalls[0].shape[1]
-        wide = smalls[8].shape[1]
-        g = lax.axis_index("tower") * lax.axis_size("dp") + lax.axis_index("dp")
-        turned = pltpu.roll(vec[0], lax.rem(feat - width * g, feat), axis=1)
+        width, wide = smalls[0].shape[1], smalls[8].shape[1]
         for n in range(8):
-            smalls[n][...] = turned[n:n + 1, :width]
-        per_row = feat // wide
-        rows = jnp.broadcast_to(vec[1, pl.ds(g // per_row, 1), :], (8, feat))
-        smalls[8][...] = pltpu.roll(rows, lax.rem(feat - wide * lax.rem(g, per_row), feat), axis=1)[:1, :wide]
-        loss[...] = vec[1, 4:5, 0:1] * scale_by
-        factor[...] = vec[1, 4:5, 1:2]
+            smalls[n][...] = vec[n:n + 1, :width]
+        smalls[8][...] = vec[8:9, :wide]
+        loss[...] = vec[9:10, 0:1] * scale_by
+        factor[...] = vec[9:10, 1:2]
 
 
 def hand_out(vec, tw, ow, ew, sw, inp, captions):
     devices = lax.axis_size("tower") * lax.axis_size("dp")
-    feat = vec.shape[2]
+    feat = tw.shape[1] // 3
     bigs = (tw, ow, ew, sw)
     outs = ([(1, 1)] * 2 + [(1, feat // devices)] * 8 + [(1, ew.shape[1] // devices)]
             + [a.shape for a in bigs])

time: 168 us -> 149 us (0.89); the launches traced: 168 us -> 147 us
  Pallas kernels: 165 us -> 144 us
    pallas_call x1, Pallas kernels: 125 us -> 105 us  [backward(): pl.pallas_call(bwd_kernel, in_specs=[vspec] * 4 + [sspec] + [vspec] * 4 +...]
    pallas_call x1, Pallas kernels: 35.6 us -> 33.9 us  [forward(): pl.pallas_call(fwd_kernel, grid=(steps,), in_specs=[rows(feat), whole(seg...]
where the time goes in v3:
time: 149 us; the launch traced here: 147 us
  Pallas kernels  144 us (97%)
    pallas_call x1, Pallas kernels, backward(): pl.pallas_call(bwd_kernel, in_specs=[vspec] * 4 + [sspec] + [vspec] * 4 +...  105 us
    pallas_call x1, Pallas kernels, forward(): pl.pallas_call(fwd_kernel, grid=(steps,), in_specs=[rows(feat), whole(seg...  33.9 us
    pallas_call x1, Pallas kernels, hand_out(): pl.pallas_call(functools.partial(hand_out_kernel, 1.0 / captions), grid=(...  4.95 us

profile of v3, /device:TPU:25, one launch (start us, length us, event | category | flops | bytes accessed | tf_op | source)
XLA Modules:
  0.0 146.6 jit_solution(10866234205421927884)
XLA Ops:
  1.3 1.4 copy.33.caption
  2.6 33.9 %fwd.1 = (bf16[1024,2304]{1,0:T(8,128)(2,1)}, bf16[1024,1536]{1,0:T(8,128)(2,1)}, bf16[1024,768]{1,0:T(8,128)(2,1)}, f32[1024,768]{1,0:T(8,128)}, bf16[1024,3072...) custom-call(bf16[1024,768]{1,0:T(8,128)(2,1)} %bitcast.23, ...), custom_call_target="tpu_custom_call" | custom-call | tf_op jit(solution)/shard_map/fwd/pallas_call | solution.py:161
  36.6 105.0 %bwd.1 = (f32[24,2304]{1,0:T(8,128)}, f32[24,768]{1,0:T(8,128)}, f32[24,3072]{1,0:T(8,128)}, f32[96,768]{1,0:T(8,128)}, f32[1024,768]{1,0:T(8,128)}, /*index=5*/f32[16,128]{1,0:T(8,128)}) custom-call(bf16[64,1024]{1,0:T(8,128)(2,1)} %get-tuple-element.47.member, f32[64,768]{1,0:T(8,128)} %get-tuple-element.48.pooled, f32[64,128]{1,0:T(8,128)} %get-tuple-element.49.count, ...), custom_call_target="tpu_custom_call" | custom-call | tf_op jit(solution)/shard_map/bwd/pallas_call | solution.py:781
  141.7 4.9 %hand_out.1 = (f32[1,1]{1,0:T(1,128)}, f32[1,1]{1,0:T(1,128)}, f32[1,24]{1,0:T(1,128)}, f32[1,24]{1,0:T(1,128)}, f32[1,24]{1,0:T(1,128)}, /*index=5*/f32[1,24]{1...) custom-call(f32[16,128]{1,0:T(8,128)} %get-tuple-element.56.vec, ...), custom_call_target="tpu_custom_call" | custom-call | tf_op jit(solution)/shard_map/hand_out/pallas_call | solution.py:818

commit v4 on v3

--- a/solution.py
+++ b/solution.py
@@ -15,6 +15,7 @@
 GELU_C = 0.7978845608028654
 GELU_A = 0.044715
 STEP_ROWS = 4
+MESH = pl.DeviceIdType.MESH
 
 
 def mm(a, b):
@@ -46,8 +47,8 @@
 
 
 def fwd_kernel(tok, seg, g1, b1, qb, vb, ob, g2, b2, eb, sb, w3h, woh, weh, wsh,
-               qkv, probs, mixed, hidden, act, slope, member_out, pooled_out, count_out,
-               w3, wo, we, ws, pool_acc, count_acc, sems):
+               qkv, probs, mixed, normed_out, sums_out, slope, n1_out, n2_out, spread_out, member_out, pooled_out, count_out, table_out,
+               w3, wo, we, ws, pool_acc, count_acc, act_sum, imgs, elow, sems, gsem, esem):
     i = pl.program_id(0)
     steps = pl.num_programs(0)
     rows_here, length = seg.shape
@@ -58,12 +59,28 @@
     copies = [pltpu.make_async_copy(src, dst, sems.at[n])
               for n, (src, dst) in enumerate(((w3h, w3), (woh, wo), (weh, we), (wsh, ws)))]
 
+    tower, d = lax.axis_index("tower"), lax.axis_index("dp")
+    chip, core = d // 2, lax.rem(d, 2)
+    other = 1 - core
+    partner = (tower, chip * 2 + other)
+    chips = imgs.shape[1]
+    facing = [(1 - tower, lax.rem(chip + k, chips) * 2 + core) for k in range(chips)]
+
+    def remote(src, dst, sem, dev):
+        return pltpu.make_async_remote_copy(src_ref=src, dst_ref=dst, send_sem=sem.at[0], recv_sem=sem.at[1],
+                                            device_id=dev, device_id_type=MESH)
+
+    barrier = pltpu.get_barrier_semaphore()
+
     @pl.when(i == 0)
     def _():
         for c in copies:
             c.start()
+        for dev in facing + [partner]:
+            pl.semaphore_signal(barrier, inc=1, device_id=dev, device_id_type=MESH)
         pool_acc[...] = jnp.zeros_like(pool_acc)
         count_acc[...] = jnp.zeros_like(count_acc)
+        act_sum[...] = jnp.zeros_like(act_sum)
 
     def arrive(n):
         @pl.when(i == 0)
@@ -73,6 +90,7 @@
     x = tok[...].astype(f32)
     norm, _ = stats(x)
     n1 = (norm * g1[...].astype(f32) + b1[...].astype(f32)).astype(bf16)
+    n1_out[...] = n1
     arrive(0)
     qkv[:, :feat] = (mm(n1, w3[:, :feat]) + qb[...].astype(f32)).astype(bf16)
     qkv[:, feat:2 * feat] = mm(n1, w3[:, feat:2 * feat]).astype(bf16)
@@ -111,9 +129,16 @@
 
     arrive(1)
     hid = x + mm(mixed[...], wo[...]) + ob[...].astype(f32)
-    hidden[...] = hid
-    norm2, _ = stats(hid)
+    norm2, spread2 = stats(hid)
+    normed_out[...] = norm2
+    spread_out[...] = spread2
     n2 = (norm2 * g2[...].astype(f32) + b2[...].astype(f32)).astype(bf16)
+    n2_out[...] = n2
+    slot_row = jnp.concatenate(slot_lanes, axis=1)
+    hot = (lax.broadcasted_iota(jnp.int32, (slots, block), 0) == slot_row)
+    member = hot.astype(f32).astype(bf16)
+    placed = (lax.broadcasted_iota(jnp.int32, (2 * slots, block), 0) == slot_row + slots * core)
+    placed = placed.astype(f32).astype(bf16)
     arrive(2)
     arrive(3)
     out = hid + sb[...].astype(f32)
@@ -129,12 +154,9 @@
         t = jnp.tanh(cv * (1.0 + GELU_A * v2))
         h = 0.5 + 0.5 * t
         a = (v * h).astype(bf16)
-        act[:, f:f + tile] = a
+        act_sum[:, f:f + tile] += mm(placed, a)
         slope[:, f:f + tile] = (h + h * (1.0 - h) * ((2.0 * cv) * (1.0 + (3.0 * GELU_A) * v2))).astype(bf16)
         out = out + mm(a, ws[f:f + tile, :])
-    slot_row = jnp.concatenate(slot_lanes, axis=1)
-    hot = (lax.broadcasted_iota(jnp.int32, (slots, block), 0) == slot_row)
-    member = hot.astype(f32).astype(bf16)
     member_out[...] = member
     out_hi, out_lo = low_pair(out)
     pool_acc[...] += mm(member, out_hi) + mm(member, out_lo)
@@ -143,8 +165,27 @@
     @pl.when(i == steps - 1)
     def _():
         counts = jnp.maximum(count_acc[...], 1.0)
+        pooled = pool_acc[...] / counts[:, :1]
         count_out[...] = counts
-        pooled_out[...] = pool_acc[...] / counts[:, :1]
+        for f in range(0, we.shape[1], tile):
+            sums_out[f:f + tile, :] = act_sum[:, f:f + tile].astype(bf16).T
+        pooled_out[...] = pooled
+        pl.semaphore_wait(barrier, chips + 1)
+
+        @pl.when(tower == 0)
+        def _():
+            first = pooled[:rows_here]
+            elow[...] = (first * lax.rsqrt(jnp.sum(first * first, axis=1, keepdims=True) + 1e-06)).astype(bf16)
+            for dev in facing:
+                remote(elow, imgs.at[core, chip], gsem, dev).start()
+            remote(imgs.at[0], imgs.at[0], gsem, partner).wait_send()
+
+        @pl.when(tower == 1)
+        def _():
+            remote(imgs.at[core], imgs.at[core], gsem, partner).wait_recv()
+            remote(imgs.at[core], imgs.at[core], esem, partner).start()
+            remote(imgs.at[other], imgs.at[other], esem, partner).wait()
+            table_out[...] = imgs[...]
 
 
 def forward(tokens, segments, g1, b1, w3, qb, vb, wo, ob, g2, b2, we, eb, ws, sb):
@@ -154,6 +195,7 @@
     ff = we.shape[1]
     block = STEP_ROWS * length
     steps = count // block
+    table = (2, lax.axis_size("dp") // 2, rows_here, feat)
     whole = lambda a: pl.BlockSpec(a.shape, lambda i: (0,) * a.ndim)
     rows = lambda width: pl.BlockSpec((block, width), lambda i: (i, 0))
     anyw = pl.BlockSpec(memory_space=pl.ANY)
@@ -164,51 +206,59 @@
         in_specs=[rows(feat), whole(segments)] + [whole(a) for a in smalls] + [anyw] * 4,
         out_specs=[rows(3 * feat),
                    rows(2 * feat),
-                   rows(feat), rows(feat), rows(ff), rows(ff),
+                   rows(feat), rows(feat), pl.BlockSpec((ff, 2 * slots), lambda i: (0, 0)), rows(ff), rows(feat), rows(feat), rows(1),
                    pl.BlockSpec((slots, block), lambda i: (0, i)),
                    pl.BlockSpec((slots, feat), lambda i: (0, 0)),
-                   pl.BlockSpec((slots, 128), lambda i: (0, 0))],
+                   pl.BlockSpec((slots, 128), lambda i: (0, 0)),
+                   pl.BlockSpec(table, lambda i: (0,) * 4)],
         out_shape=[jax.ShapeDtypeStruct((count, 3 * feat), bf16),
                    jax.ShapeDtypeStruct((count, 2 * feat), bf16),
                    jax.ShapeDtypeStruct((count, feat), bf16),
                    jax.ShapeDtypeStruct((count, feat), f32),
+                   jax.ShapeDtypeStruct((ff, 2 * slots), bf16),
                    jax.ShapeDtypeStruct((count, ff), bf16),
-                   jax.ShapeDtypeStruct((count, ff), bf16),
+                   jax.ShapeDtypeStruct((count, feat), bf16),
+                   jax.ShapeDtypeStruct((count, feat), bf16),
+                   jax.ShapeDtypeStruct((count, 1), f32),
                    jax.ShapeDtypeStruct((slots, count), bf16),
                    jax.ShapeDtypeStruct((slots, feat), f32),
-                   jax.ShapeDtypeStruct((slots, 128), f32)],
+                   jax.ShapeDtypeStruct((slots, 128), f32),
+                   jax.ShapeDtypeStruct(table, bf16)],
         scratch_shapes=[pltpu.VMEM(w3.shape, bf16), pltpu.VMEM(wo.shape, bf16), pltpu.VMEM(we.shape, bf16),
-                        pltpu.VMEM(ws.shape, bf16), pltpu.VMEM((slots, feat), f32), pltpu.VMEM((slots, 128), f32),
-                        pltpu.SemaphoreType.DMA((4,))],
-        compiler_params=pltpu.CompilerParams(vmem_limit_bytes=56 << 20, dimension_semantics=("arbitrary",)),
+                        pltpu.VMEM(ws.shape, bf16), pltpu.VMEM((slots, feat), f32), pltpu.VMEM((slots, 128), f32), pltpu.VMEM((2 * slots, ff), f32),
+                        pltpu.VMEM(table, bf16), pltpu.VMEM((rows_here, feat), bf16),
+                        pltpu.SemaphoreType.DMA((4,)), pltpu.SemaphoreType.DMA((2,)), pltpu.SemaphoreType.DMA((2,))],
+        compiler_params=pltpu.CompilerParams(vmem_limit_bytes=56 << 20, dimension_semantics=("arbitrary",),
+                                             collective_id=1, has_side_effects=True),
         name="fwd",
     )(tokens, segments, *smalls, w3, wo, we, ws)
 
 
-MESH = pl.DeviceIdType.MESH
 PLANE = 8
 LINE = 4
 BLK = 256
 CH = 768
 HALF = CH // 2
 ROWS = HALF // PLANE
-N_CH = 12
-LONG = (1, 3, 5, 7, 8, 10)
-SHORT = (9, 11)
+N_CH = 8
+WIDE = (0, 1, 3, 6)
+LONG = (2, 4, 5, 7)
+WIDE_AT = {q: n for n, q in enumerate(WIDE)}
+LONG_AT = {q: n for n, q in enumerate(LONG)}
 
 
 def fold(x):
     return jnp.sum(x.reshape(x.shape[0] // 8, 8, x.shape[1]), axis=0)
 
 
-def bwd_kernel(member, pooled, count, caption, scale, g1, b1, g2, b2,
-               qkv_h, probs_h, mixed_h, hidden_h, act_h, slope_h, tok_h, w3_h, wo_h, we_h, ws_h,
+def bwd_kernel(member, pooled, count, imgs, act_sums, caption, scale, g1, b1, g2, b2,
+               qkv_h, probs_h, mixed_h, normed_h, slope_h, n1_h, n2_h, spread_h, tok_h, w3_h, wo_h, we_h, ws_h,
                tw_out, ow_out, ew_out, sw_out, in_out, vec_out,
-               cs, snd, prv, own, yrcv, ysw, zrcv, arcv, swrcv, fin, swfin,
-               gol, gn2, hid, spread2, n2b, tok, act, slope, ws, we, ge, qkv, w3, wo,
-               imgs, elow, ebsum, attn_sum, vec, vown, vpair, vrcv,
-               ld, psend, precv, xsend, xrecv, ysend, yrecv, yswsend, yswrecv, zsend, zrecv, asend, arecv,
-               swsend, swrecv, fsem, swfsem, gsem, esem, vpsem, vsem, outsem):
+               cs, snd, prv, own, ylong, ywide, zrcv, fin, apair, asum, aall, gpall, swfin, xsw,
+               gol, gn2, hid, spread2, n2b, tok, mixed, probs, slope, ws, we, ge, qkv, w3, wo,
+               ebsum, attn_sum, vec, vown, vpair, vrcv,
+               ld, psend, precv, xsend, xrecv, ysend, yrecv, zsend, zrecv,
+               fsem, asem, gsem, swsem, vpsem, vsem, outsem):
     t = lax.axis_index("tower")
     d = lax.axis_index("dp")
     p = d // 2
@@ -219,7 +269,7 @@
     count_t = gol.shape[0]
     blocks = count_t // BLK
     feat = CH
-    rows_here = caption.shape[0]
+    rows_here = caption.shape[1]
     other = 1 - c
 
     def peer(k):
@@ -258,52 +308,117 @@
     def x_line(q):
         return remote(cs.at[q, 0:LINE, y], cs.at[q, 0:LINE, y], xsend.at[q], xrecv.at[q], across)
 
+    def x_copy(q):
+        return x_all(q) if q in WIDE else x_line(q)
+
     def y_copy(q):
-        return remote(cs.at[q, :, 1 - y], yrcv.at[q // 2], ysend.at[q // 2], yrecv.at[q // 2], beside)
+        if q in LONG:
+            src, dst = cs.at[q, :, 1 - y], ylong.at[LONG_AT[q]]
+        else:
+            src, dst = cs.at[q, pl.ds(LINE * t, LINE), 1 - y], ywide.at[WIDE_AT[q]]
+        return remote(src, dst, ysend.at[q], yrecv.at[q], beside)
 
     def z_start(q):
         for k in range(1, LINE):
             to = lax.rem(z + k, LINE)
-            remote(cs.at[q, LINE * t + to, y], zrcv.at[q // 2, k - 1], zsend.at[q // 2], zrecv.at[q // 2],
+            remote(cs.at[q, LINE * t + to, y], zrcv.at[q, k - 1], zsend.at[q], zrecv.at[q],
                    at_core(t, 2 * to + y)).start()
 
     def z_all(q):
-        return remote(zrcv.at[q // 2], zrcv.at[q // 2], zsend.at[q // 2], zrecv.at[q // 2], partner)
-
-    def a_start(q):
+        return remote(zrcv.at[q], zrcv.at[q], zsend.at[q], zrecv.at[q], partner)
+
+    def mid(q):
+        y_copy(q).wait_recv()
+        if q in LONG:
+            for a in range(PLANE):
+                cs[q, a, y] = (cs[q, a, y].astype(f32) + ylong[LONG_AT[q], a].astype(f32)).astype(bf16)
+            x_line(q).start()
+        else:
+            for a in range(LINE):
+                at = LINE * t + a
+                cs[q, at, y] = (cs[q, at, y].astype(f32) + ywide[WIDE_AT[q], a].astype(f32)).astype(bf16)
+        z_start(q)
+
+    def a_pair():
+        return remote(act_sums.at[:, :, other], apair, asem.at[0], asem.at[1], partner)
+
+    def a_start():
         for k in range(1, PLANE):
-            to = peer(k)
-            remote(cs.at[q, LINE * t + to // 2, lax.rem(to, 2)], arcv.at[(q - 9) // 2, k - 1],
-                   asend.at[(q - 9) // 2], arecv.at[(q - 9) // 2], at_core(t, to)).start()
-
-    def a_all(q):
-        a = (q - 9) // 2
-        return remote(arcv.at[a], arcv.at[a], asend.at[a], arecv.at[a], partner)
-
-    def ysw_copy(i):
-        return remote(cs.at[2 * i, pl.ds(LINE * t + 2 * (1 - y), 2)], ysw.at[i], yswsend.at[i], yswrecv.at[i], beside)
-
-    def sw_z(i):
-        k = lax.rem(i - z + LINE, LINE)
-        return remote(cs.at[2 * i, pl.ds(LINE * t + 2 * y, 2)], swrcv.at[jnp.maximum(k, 1) - 1], swsend,
-                      swrecv, at_core(t, 2 * i + y))
-
-    def sw_mid(i):
-        ysw_copy(i).wait_recv()
-        for a in range(2):
-            at = LINE * t + 2 * y + a
-            cs[2 * i, at] = (cs[2 * i, at].astype(f32) + ysw[i, a].astype(f32)).astype(bf16)
-
-        @pl.when(z != i)
-        def _():
-            sw_z(i).start()
-
-    def long_mid(q):
-        y_copy(q).wait_recv()
-        for a in range(PLANE):
-            cs[q, a, y] = (cs[q, a, y].astype(f32) + yrcv[q // 2, a].astype(f32)).astype(bf16)
-        x_line(q).start()
-        z_start(q)
+            remote(asum.at[:, peer(k)], aall.at[:, :, pl.ds(pl.multiple_of(128 * p, 128), 128)],
+                   asem.at[2], asem.at[3], at_core(t, peer(k))).start()
+
+    def a_all():
+        every = asum.at[:, 0:PLANE - 1]
+        return remote(every, every, asem.at[2], asem.at[3], partner)
+
+    def gp_beside():
+        return remote(gpall.at[p, c], gpall.at[p, c], gsem.at[0], gsem.at[1], beside)
+
+    def gp_line():
+        gp_beside().wait_recv()
+        for k in range(1, LINE):
+            mine = gpall.at[pl.ds(2 * z, 2), c]
+            remote(mine, mine, gsem.at[2], gsem.at[3], at_core(t, 2 * lax.rem(z + k, LINE) + y)).start()
+
+    def gp_line_all():
+        every = gpall.at[0:2 * (LINE - 1), 0]
+        return remote(every, every, gsem.at[2], gsem.at[3], partner)
+
+    def gp_share_copy():
+        return remote(gpall.at[:, c], gpall.at[:, c], gsem.at[4], gsem.at[5], partner)
+
+    def gp_share():
+        gp_line_all().wait_recv()
+        gp_share_copy().start()
+
+    def sw_across():
+        return remote(xsw, xsw, swsem.at[0], swsem.at[1], across)
+
+    def sw_keep():
+        return pltpu.make_async_copy(swfin, sw_out, swsem.at[2])
+
+    def shrink():
+        gp_share_copy().wait_recv()
+        a_all().wait_recv()
+        rows = gpall[...].reshape(-1, feat)
+        xsw[...] = mm(aall[0], rows).astype(bf16)
+        sw_across().start()
+        swfin[...] = mm(aall[1], rows)
+        sw_keep().start()
+
+    half_rows = ROWS // 2
+
+    def place(q):
+        if q < 4:
+            return ew_out, 4 * HALF * c + HALF * q
+        if q == 4:
+            return ow_out, HALF * c
+        return tw_out, CH * (q - 5) + HALF * c
+
+    def keep(q):
+        out, col = place(q)
+        return pltpu.make_async_copy(fin.at[q, pl.ds(pl.multiple_of(half_rows * c, 8), half_rows)],
+                                     out.at[:, pl.ds(pl.multiple_of(col, 128), HALF)], fsem.at[0])
+
+    def give(q):
+        out, col = place(q)
+        return remote(fin.at[q, pl.ds(pl.multiple_of(half_rows * other, 8), half_rows)],
+                      out.at[:, pl.ds(pl.multiple_of(col, 128), HALF)], fsem.at[1], fsem.at[2], partner)
+
+    def finish(q):
+        z_all(q).wait_recv()
+        total = cs[q, LINE * t + z, y].astype(f32)
+        for k in range(LINE - 1):
+            total = total + zrcv[q, k].astype(f32)
+        fin[q] = total
+        keep(q).start()
+        give(q).start()
+
+    def leave(q):
+        chip_sum(q)
+        if q in WIDE:
+            x_all(q).start()
+        y_copy(q).start()
 
     def chip_sum(q):
         pair_copy(q).wait_recv()
@@ -326,16 +441,6 @@
             snd[slot, r:r + 256, :] = jnp.where(c == 0, high, low).astype(bf16)
         pair_copy(q).start()
 
-    def gather_start():
-        for k in range(PLANE):
-            remote(elow, imgs.at[c, p], gsem.at[0], gsem.at[1], at_core(1 - t, peer(k))).start()
-
-    def gather_all():
-        return remote(imgs.at[c], imgs.at[c], gsem.at[0], gsem.at[1], partner)
-
-    def share_copy(h):
-        return remote(imgs.at[h], imgs.at[h], esem.at[0], esem.at[1], partner)
-
     def v_pair():
         return remote(vown.at[other], vpair, vpsem.at[0], vpsem.at[1], partner)
 
@@ -345,89 +450,80 @@
     def tile_loads(i):
         s = lax.rem(i, 2)
         out = []
-        ff = act_h.shape[1]
+        ff = slope_h.shape[1]
         for h in range(2):
             col = pl.multiple_of((ff // 2) * h + HALF * i, 128)
             here = pl.ds(HALF * h, HALF)
-            out.append(load(8 * s + 4 * h, act_h.at[:, pl.ds(col, HALF)], act.at[s, :, here]))
-            out.append(load(8 * s + 4 * h + 1, slope_h.at[:, pl.ds(col, HALF)], slope.at[s, :, here]))
-            out.append(load(8 * s + 4 * h + 2, ws_h.at[pl.ds(col, HALF)], ws.at[s, here]))
-            out.append(load(8 * s + 4 * h + 3, we_h.at[:, pl.ds(col, HALF)], we.at[s, :, here]))
+            out.append(load(6 * s + 3 * h, slope_h.at[:, pl.ds(col, HALF)], slope.at[s, :, here]))
+            out.append(load(6 * s + 3 * h + 1, ws_h.at[pl.ds(col, HALF)], ws.at[s, here]))
+            out.append(load(6 * s + 3 * h + 2, we_h.at[:, pl.ds(col, HALF)], we.at[s, :, here]))
         return out
 
-    hid_load = load(16, hidden_h, hid)
+    hid_load = load(16, normed_h, hid)
     tok_load = load(17, tok_h, tok)
     qkv_load = load(18, qkv_h, qkv)
     w3_load = load(19, w3_h, w3)
     wo_load = load(20, wo_h, wo)
-    mixed_load = load(21, mixed_h, slope.at[0])
-    probs_loads = [load(22 + h, probs_h.at[:, pl.ds(feat * h, feat)], act.at[h]) for h in range(2)]
+    n2_load = load(24, n2_h, n2b)
+    spread_load = load(25, spread_h, spread2)
+    n1_load = load(26, n1_h, slope.at[1])
+    mixed_load = load(21, mixed_h, mixed)
+    probs_load = load(22, probs_h, probs)
 
     @pl.when(t == 0)
     def _():
-        elow[...] = emb_low[:rows_here]
         pl.semaphore_wait(barrier, 2 * PLANE)
-        gather_start()
         gn2[:BLK, :] = jnp.zeros((BLK, feat), f32)
         for m in range(blocks):
             pltpu.make_async_copy(gn2.at[0:BLK], in_out.at[pl.ds(BLK * m, BLK)], outsem.at[m]).start()
 
-        @pl.loop(0, 6)
-        def _(i):
-            @pl.when(i < 4)
-            def _():
-                x_all(2 * i).wait_recv()
-                ysw_copy(i).start()
-
-            @pl.when((i >= 1) & (i <= 4))
-            def _():
-                sw_mid(i - 1)
-
-            @pl.when(i >= 2)
-            def _():
-                x_line(2 * i - 3).wait_recv()
-                z_start(2 * i - 3)
-        for q in (9, 8, 11, 10):
-            if q in SHORT:
-                x_all(q).wait_recv()
-                a_start(q)
+        def over(q):
+            x_copy(q).wait_recv()
+            if q in WIDE:
+                y_copy(q).start()
             else:
-                x_line(q).wait_recv()
                 z_start(q)
-        gather_all().wait_send()
+        over(0)
+        mid(0)
+        over(1)
+        finish(0)
+        mid(1)
+        over(3)
+        finish(1)
+        over(2)
+        mid(3)
+        sw_across().wait_recv()
+        swfin[...] = xsw[...].astype(f32)
+        sw_keep().start()
+        finish(2)
+        over(4)
+        finish(3)
+        finish(4)
+        over(6)
+        over(5)
+        mid(6)
+        finish(5)
+        over(7)
+        finish(6)
+        finish(7)
         for m in range(blocks):
             pltpu.make_async_copy(gn2.at[0:BLK], in_out.at[pl.ds(BLK * m, BLK)], outsem.at[m]).wait()
 
     @pl.when(is_text)
     def _():
-        hid_load.start()
-        tok_load.start()
         for cp in tile_loads(0):
             cp.start()
+        n2_load.start()
         for cp in tile_loads(1):
             cp.start()
-        qkv_load.start()
-        w3_load.start()
-        wo_load.start()
-        gain2, shift2 = g2[...].astype(f32), b2[...].astype(f32)
-        gain1, shift1 = g1[...].astype(f32), b1[...].astype(f32)
-        hid_load.wait()
-
-        @pl.loop(0, blocks)
-        def _(m):
-            here = pl.ds(pl.multiple_of(m * BLK, BLK), BLK)
-            norm, spread = stats(hid[here, :])
-            n2b[here, :] = (norm * gain2 + shift2).astype(bf16)
-            hid[here, :] = norm
-            spread2[here, :] = spread
+        for cp in (hid_load, spread_load, mixed_load, wo_load, qkv_load, probs_load, w3_load, tok_load):
+            cp.start()
+        gain2, gain1 = g2[...].astype(f32), g1[...].astype(f32)
         gn2[...] = jnp.zeros_like(gn2)
         attn_sum[...] = jnp.zeros_like(attn_sum)
         vec[...] = jnp.zeros_like(vec)
         pl.semaphore_wait(barrier, 2 * PLANE)
-        gather_all().wait_recv()
-        share_copy(c).start()
-        share_copy(c).wait_send()
-        share_copy(other).wait_recv()
+        a_pair().start()
 
         table = imgs[...].reshape(2 * PLANE * rows_here, feat)
         dots = mm_nt(emb_low, table)
@@ -436,13 +532,20 @@
         peak = jnp.max(logits, axis=1, keepdims=True)
         weight = jnp.exp(logits - peak)
         total = jnp.sum(weight, axis=1, keepdims=True)
-        wanted = jnp.concatenate([caption[:, s:s + 1] for s in range(CAPS)], axis=0)
+        eye = (lax.broadcasted_iota(jnp.int32, (rows_here, rows_here), 0)
+               == lax.broadcasted_iota(jnp.int32, (rows_here, rows_here), 1))
+        wanted = jnp.concatenate([jnp.sum(jnp.where(eye, caption[s:s + 1, :], 0), axis=1, keepdims=True)
+                                  for s in range(CAPS)], axis=0)
         span = 2 * rows_here
         inside = lax.rem(wanted, span)
         wanted = (inside // rows_here) * (PLANE * rows_here) + (wanted // span) * rows_here + lax.rem(inside, rows_here)
         hot = (lax.broadcasted_iota(jnp.int32, dots.shape, 1) == wanted).astype(f32)
         picked = jnp.sum(logits * hot, axis=1, keepdims=True)
         loss_here = jnp.sum(peak + jnp.log(total) - picked, axis=0, keepdims=True)
+        a_pair().wait_recv()
+        asum[...] = act_sums[:, :, c] + apair[...]
+        aall[:, :, pl.ds(pl.multiple_of(128 * p, 128), 128)] = asum[:, p]
+        a_start()
         grad_logits = weight / total - hot
         factor_here = jnp.sum(jnp.sum(grad_logits * dots, axis=1, keepdims=True), axis=0, keepdims=True)
         grad_emb = mm((factor * grad_logits).astype(bf16), table)
@@ -452,6 +555,8 @@
         column = lax.broadcasted_iota(jnp.int32, (1, feat), 1)
         vec[12:13, :] = jnp.where(column == 0, loss_here, jnp.where(column == 1, factor_here, 0.0))
         gp_hi, gp_lo = low_pair(grad_pool / counts)
+        gpall[p, c] = gp_hi
+        gp_beside().start()
         for m in range(blocks):
             gol[BLK * m:BLK * (m + 1), :] = mm_tn(member[:, BLK * m:BLK * (m + 1)], gp_hi).astype(bf16)
 
@@ -460,12 +565,11 @@
             s = lax.rem(i, 2)
             for cp in tile_loads(i):
                 cp.wait()
-            chunk(2 * i, act.at[s], gol[...])
-
-            @pl.when(i > 0)
-            def _():
-                chip_sum(2 * i - 1)
-                y_copy(2 * i - 1).start()
+
+            def at(n, what, *of):
+                @pl.when(i == n)
+                def _():
+                    what(*of)
             sums = jnp.zeros((8, feat), f32)
             for m in range(blocks):
                 here = slice(BLK * m, BLK * (m + 1))
@@ -475,34 +579,28 @@
             sums = jnp.sum(sums, axis=0, keepdims=True)
             for h in range(2):
                 ebsum[:, pl.ds(pl.multiple_of(4 * HALF * h + HALF * i, 128), HALF)] = sums[:, HALF * h:HALF * (h + 1)]
-            chunk(2 * i + 1, n2b, ge[...])
-            chip_sum(2 * i)
-            x_all(2 * i).start()
-            ysw_copy(i).start()
-
-            @pl.when(i > 0)
+            at(1, gp_line)
+            at(1, leave, 0)
+            at(2, leave, 1)
+            at(3, leave, 2)
+
+            @pl.when(i == 0)
             def _():
-                sw_mid(i - 1)
+                n2_load.wait()
+            chunk(i, n2b, ge[...])
+            at(2, mid, 0)
+            at(3, mid, 1)
             for m in range(blocks):
                 here = slice(BLK * m, BLK * (m + 1))
                 gn2[here, :] += mm_nt(ge[here, :], we[s])
-
-            @pl.when(i >= 2)
-            def _():
-                long_mid(2 * i - 3)
 
             @pl.when(i < 2)
             def _():
                 for cp in tile_loads(i + 2):
                     cp.start()
-
-            @pl.when(i == 2)
-            def _():
-                mixed_load.start()
-                probs_loads[0].start()
-        probs_loads[1].start()
-        chip_sum(7)
-        y_copy(7).start()
+        n1_load.start()
+        hid_load.wait()
+        spread_load.wait()
 
         zeros8 = jnp.zeros((8, feat), f32)
 
@@ -523,21 +621,17 @@
             vec[row:row + 1, :] = jnp.sum(x, axis=0, keepdims=True)
         for n in range(4):
             vec[8 + n:9 + n, :] = ebsum[:, feat * n:feat * (n + 1)]
-        sw_mid(3)
+        leave(3)
 
         mixed_load.wait()
-        chunk(8, slope.at[0], gol[...])
+        chunk(4, mixed, gol[...])
         wo_load.wait()
         for m in range(blocks):
             here = slice(BLK * m, BLK * (m + 1))
             ge[here, :] = mm_nt(gol[here, :], wo[...]).astype(bf16)
-        chip_sum(8)
-        y_copy(8).start()
-        long_mid(5)
 
         qkv_load.wait()
-        for cp in probs_loads:
-            cp.wait()
+        probs_load.wait()
         first_half = lax.broadcasted_iota(jnp.int32, (128, 128), 1) < 64
         hps = range(HEADS // 2)
 
@@ -546,7 +640,7 @@
             here = pl.ds(pl.multiple_of(rp * 128, 128), 128)
 
             def probs_of(h):
-                return act[h // 3, here, 256 * (h % 3):256 * (h % 3) + 256]
+                return probs[here, 256 * h:256 * h + 256]
 
             def part(n, h):
                 return qkv[here, feat * n + 128 * h:feat * n + 128 * h + 128]
@@ -568,30 +662,39 @@
                     qkv[here, feat * n + 128 * h:feat * n + 128 * h + 128] = x.astype(bf16)
                 for n, x in ((0, gq[h]), (1, gv[h])):
                     attn_sum[:, feat * n + 128 * h:feat * n + 128 * h + 128] += fold(x)
+
+            @pl.when(rp == 1)
+            def _():
+                leave(4)
+                mid(2)
+
+            @pl.when(rp == 4)
+            def _():
+                gp_share()
+
+            @pl.when(rp == 5)
+            def _():
+                mid(3)
         vec[2:3, :] = jnp.sum(attn_sum[:, :feat], axis=0, keepdims=True)
         vec[3:4, :] = jnp.sum(attn_sum[:, feat:], axis=0, keepdims=True)
 
-        tok_load.wait()
-
-        @pl.loop(0, blocks)
-        def _(m):
-            here = pl.ds(pl.multiple_of(m * BLK, BLK), BLK)
-            norm, _s = stats(tok[here, :].astype(f32))
-            slope[1, here, :] = (norm * gain1 + shift1).astype(bf16)
+        n1_load.wait()
 
         @pl.loop(0, 3)
         def _(j):
-            chunk(9 + j, slope.at[1], qkv[:, pl.ds(pl.multiple_of(CH * j, 128), CH)])
+            chunk(5 + j, slope.at[1], qkv[:, pl.ds(pl.multiple_of(CH * j, 128), CH)])
+
+            @pl.when(j == 0)
+            def _():
+                shrink()
+                finish(0)
 
             @pl.when(j == 1)
             def _():
-                chip_sum(9)
-                x_all(9).start()
-                a_start(9)
-                long_mid(7)
-        chip_sum(10)
-        y_copy(10).start()
-        long_mid(8)
+                leave(5)
+        finish(1)
+        mid(4)
+        tok_load.wait()
         w3_load.wait()
 
         def norm1_back(m, sums):
@@ -600,10 +703,20 @@
 
             @pl.when(m == 0)
             def _():
-                chip_sum(11)
-                x_all(11).start()
-                a_start(11)
-
+                leave(6)
+                finish(2)
+
+            @pl.when(m == 1)
+            def _():
+                leave(7)
+
+            @pl.when(m == 2)
+            def _():
+                finish(3)
+
+            @pl.when(m == 3)
+            def _():
+                mid(5)
             norm, spread = stats(tok[here, :].astype(f32))
             g = g_in * gain1
             back = spread * (g - jnp.mean(g, axis=1, keepdims=True)
@@ -628,6 +741,8 @@
             vown[g % 2, g // 2, 8:9, :] = tail
             vown[g % 2, g // 2, 9:10, :] = scalars
         v_pair().start()
+        finish(4)
+        mid(6)
         for m in range(blocks):
             here = pl.ds(BLK * m, BLK)
             pltpu.make_async_copy(gn2.at[here], in_out.at[here], outsem.at[m]).wait()
@@ -638,66 +753,10 @@
                 if tt == 0 or k:
                     remote(vown.at[c, PLANE * tt + peer(k)], vrcv.at[k], vsem.at[0], vsem.at[1],
                            at_core(tt, peer(k))).start()
-        long_mid(10)
-
-    half_rows = ROWS // 2
-
-    def keep(n, out, col):
-        return pltpu.make_async_copy(fin.at[n, pl.ds(pl.multiple_of(half_rows * c, 8), half_rows)],
-                                     out.at[:, pl.ds(col, HALF)], fsem.at[0])
-
-    def give(n, out, col):
-        return remote(fin.at[n, pl.ds(pl.multiple_of(half_rows * other, 8), half_rows)],
-                      out.at[:, pl.ds(col, HALF)], fsem.at[1], fsem.at[2], partner)
-
-    def hand_over(n, total, out, col):
-        fin[n] = total
-        keep(n, out, col).start()
-        give(n, out, col).start()
-
-    def finish_long(q, out, col):
-        z_all(q).wait_recv()
-        total = cs[q, LINE * t + z, y].astype(f32)
-        for k in range(LINE - 1):
-            total = total + zrcv[q // 2, k].astype(f32)
-        hand_over(q // 2, total, out, col)
-
-    def finish_short(q, out, col):
-        a_all(q).wait_recv()
-        total = cs[q, LINE * t + z, y].astype(f32)
-        for k in range(PLANE - 1):
-            total = total + arcv[(q - 9) // 2, k].astype(f32)
-        hand_over(len(LONG) + (q - 9) // 2, total, out, col)
-
-    def sw_all():
-        return remote(swrcv, swrcv, swsend, swrecv, partner)
-
-    def sw_keep():
-        n = 2 * ROWS
-        return pltpu.make_async_copy(swfin.at[pl.ds(pl.multiple_of(n * c, 8), n)],
-                                     sw_out.at[:, pl.ds(pl.multiple_of(HALF * c, 128), HALF)], swfsem.at[0])
-
-    def sw_give():
-        n = 2 * ROWS
-        return remote(swfin.at[pl.ds(pl.multiple_of(n * other, 8), n)],
-                      sw_out.at[:, pl.ds(pl.multiple_of(HALF * c, 128), HALF)], swfsem.at[1], swfsem.at[2], partner)
-
-    sw_all().wait_recv()
-    for a in range(2):
-        total = cs[2 * z, LINE * t + 2 * y + a].astype(f32)
-        for k in range(LINE - 1):
-            total = total + swrcv[k, a].astype(f32)
-        swfin[2 * ROWS * a:2 * ROWS * (a + 1), :] = total.reshape(2 * ROWS, HALF)
-    sw_keep().start()
-    sw_give().start()
-
-    @pl.loop(0, 4)
-    def _(i):
-        finish_long(2 * i + 1, ew_out, pl.multiple_of(4 * HALF * c + HALF * i, 128))
-    finish_short(9, tw_out, pl.multiple_of(HALF * c, 128))
-    finish_long(8, ow_out, pl.multiple_of(HALF * c, 128))
-    finish_short(11, tw_out, pl.multiple_of(2 * CH + HALF * c, 128))
-    finish_long(10, tw_out, pl.multiple_of(CH + HALF * c, 128))
+        finish(5)
+        mid(7)
+        finish(6)
+        finish(7)
 
     @pl.when(is_text)
     def _():
@@ -723,37 +782,29 @@
         for q in (N_CH - 2, N_CH - 1):
             pair_copy(q).wait_send()
 
-        @pl.loop(0, 4)
-        def _(i):
-            x_all(2 * i).wait_send()
-            x_line(2 * i + 1).wait_send()
-            y_copy(2 * i + 1).wait_send()
-        for q in (8, 10):
-            x_line(q).wait_send()
+        for q in range(N_CH):
+            x_copy(q).wait_send()
+        for q in LONG:
             y_copy(q).wait_send()
-        for q in SHORT:
-            x_all(q).wait_send()
-
-    @pl.loop(0, 4)
-    def _(i):
-        ysw_copy(i).wait_send()
-        z_all(2 * i + 1).wait_send()
-    for q in (8, 10):
+        a_pair().wait_send()
+        a_all().wait_send()
+        gp_beside().wait_send()
+        gp_line_all().wait_send()
+        gp_share_copy().wait_send()
+        sw_across().wait_send()
+    for q in WIDE:
+        y_copy(q).wait_send()
+    for q in range(N_CH):
         z_all(q).wait_send()
-    for q in SHORT:
-        a_all(q).wait_send()
-    sw_all().wait_send()
     sw_keep().wait()
-    sw_give().wait()
     lower = fin.at[:, 0:half_rows]
     pltpu.make_async_copy(lower, lower, fsem.at[0]).wait()
     remote(lower, lower, fsem.at[1], fsem.at[2], partner).wait()
 
 
-def backward(member, pooled, count, caption, scale, g1, b1, g2, b2,
-             qkv, probs, mixed, hidden, act, slope, tokens, w3, wo, we, ws):
+def backward(member, pooled, count, imgs, sums, caption, scale, g1, b1, g2, b2,
+             qkv, probs, mixed, normed, slope, n1, n2, spread, tokens, w3, wo, we, ws):
     n_tok, feat = tokens.shape
-    rows_here = caption.shape[0]
     ff = we.shape[1]
     dma = pltpu.SemaphoreType.DMA
     vm = pltpu.VMEM
@@ -761,68 +812,83 @@
     sspec = pl.BlockSpec(memory_space=pltpu.SMEM)
     anyw = pl.BlockSpec(memory_space=pl.ANY)
     shape = jax.ShapeDtypeStruct
-    longs, shorts = len(LONG), len(SHORT)
+    long, wide = len(LONG), len(WIDE)
+    apart = sums.shape[:2] + sums.shape[3:]
+    slots = member.shape[0]
     scratch = [
         vm((N_CH, PLANE, 2, ROWS, HALF), bf16), vm((2, CH, HALF), bf16), vm((N_CH, CH, HALF), bf16),
         vm((2, CH, HALF), f32),
-        vm((longs, PLANE, ROWS, HALF), bf16), vm((4, 2, 2, ROWS, HALF), bf16), vm((longs, LINE - 1, ROWS, HALF), bf16),
-        vm((shorts, PLANE - 1, ROWS, HALF), bf16), vm((LINE - 1, 2, 2, ROWS, HALF), bf16),
-        vm((longs + shorts, ROWS, HALF), f32), vm((4 * ROWS, HALF), f32),
+        vm((long, PLANE, ROWS, HALF), bf16), vm((wide, LINE, ROWS, HALF), bf16), vm((N_CH, LINE - 1, ROWS, HALF), bf16),
+        vm((N_CH, ROWS, HALF), f32), vm(apart, bf16), vm(apart, bf16), vm((2, apart[2], PLANE * 128), bf16),
+        vm((PLANE, 2, slots, feat), bf16), vm((2 * ROWS, feat), f32), vm((2 * ROWS, feat), bf16),
         vm((n_tok, feat), bf16), vm((n_tok, feat), f32), vm((n_tok, feat), f32), vm((n_tok, 1), f32),
         vm((n_tok, feat), bf16), vm((n_tok, feat), bf16),
-        vm((2, n_tok, CH), bf16), vm((2, n_tok, CH), bf16), vm((2, CH, feat), bf16), vm((2, feat, CH), bf16),
+        vm((n_tok, feat), bf16), vm((n_tok, 2 * feat), bf16), vm((2, n_tok, CH), bf16), vm((2, CH, feat), bf16), vm((2, feat, CH), bf16),
         vm((n_tok, feat), bf16), vm((n_tok, 3 * feat), bf16), vm(w3.shape, bf16), vm(wo.shape, bf16),
-        vm((2, PLANE, rows_here, feat), bf16), vm((rows_here, feat), bf16), vm((1, ff), f32), vm((8, 2 * feat), f32),
+        vm((1, ff), f32), vm((8, 2 * feat), f32),
         vm((16, feat), f32), vm((2, 2 * PLANE, 16, 128), f32), vm((2 * PLANE, 16, 128), f32), vm((PLANE, 16, 128), f32),
-        dma((24,)), dma((2,)), dma((N_CH,)), dma((N_CH,)), dma((N_CH,)), dma((longs,)), dma((longs,)),
-        dma((4,)), dma((4,)), dma((longs,)), dma((longs,)), dma((shorts,)), dma((shorts,)),
-        dma, dma, dma((3,)), dma((3,)), dma((2,)), dma((2,)), dma((2,)), dma((2,)), dma((n_tok // BLK,)),
+        dma((27,)), dma((2,)), dma((N_CH,)), dma((N_CH,)), dma((N_CH,)), dma((N_CH,)), dma((N_CH,)),
+        dma((N_CH,)), dma((N_CH,)), dma((3,)), dma((4,)), dma((6,)), dma((3,)), dma((2,)), dma((2,)),
+        dma((n_tok // BLK,)),
     ]
     return pl.pallas_call(
         bwd_kernel,
-        in_specs=[vspec] * 4 + [sspec] + [vspec] * 4 + [anyw] * 11,
+        in_specs=[vspec] * 6 + [sspec] + [vspec] * 4 + [anyw] * 13,
         out_specs=[anyw] * 5 + [vspec],
         out_shape=[shape((ROWS // 2, 3 * feat), f32), shape((ROWS // 2, feat), f32), shape((ROWS // 2, ff), f32),
                    shape((2 * ROWS, feat), f32), shape((n_tok, feat), f32), shape((16, 128), f32)],
         scratch_shapes=scratch,
         compiler_params=pltpu.CompilerParams(vmem_limit_bytes=61 << 20, collective_id=0, has_side_effects=True),
         name="bwd",
-    )(member, pooled, count, caption, scale, g1, b1, g2, b2,
-      qkv, probs, mixed, hidden, act, slope, tokens, w3, wo, we, ws)
-
-
-def hand_out_kernel(scale_by, vec, tw, ow, ew, sw, inp, loss, factor, *rest):
-    smalls, bigs = rest[:9], rest[9:]
-    bigs[4][...] = inp[...]
-
-    @pl.when(pl.program_id(0) == 0)
-    def _():
-        for src, dst in zip((tw, ow, ew, sw), bigs):
-            dst[...] = src[...]
-        width, wide = smalls[0].shape[1], smalls[8].shape[1]
-        for n in range(8):
-            smalls[n][...] = vec[n:n + 1, :width]
-        smalls[8][...] = vec[8:9, :wide]
-        loss[...] = vec[9:10, 0:1] * scale_by
-        factor[...] = vec[9:10, 1:2]
+    )(member, pooled, count, imgs, sums, caption, scale, g1, b1, g2, b2,
+      qkv, probs, mixed, normed, slope, n1, n2, spread, tokens, w3, wo, we, ws)
+
+
+def hand_out_kernel(scale_by, vec, *rest):
+    bigs, loss, factor, smalls = rest[:5], rest[5], rest[6], rest[7:16]
+    outs, held, sem_in, sem_out = rest[16:21], rest[21:26], rest[26], rest[27]
+    parts = []
+    for src, dst, buf in zip(bigs, outs, held):
+        count = max(src.shape[0] // BLK, 1)
+        rows = src.shape[0] // count
+        for n in range(count):
+            parts.append((src.at[rows * n:rows * (n + 1)], buf.at[rows * n:rows * (n + 1)],
+                          dst.at[rows * n:rows * (n + 1)]))
+    ins = [pltpu.make_async_copy(a, b, sem_in.at[n]) for n, (a, b, _) in enumerate(parts)]
+    outs = [pltpu.make_async_copy(b, c, sem_out.at[n]) for n, (_, b, c) in enumerate(parts)]
+    for move in ins:
+        move.start()
+    width, wide = smalls[0].shape[1], smalls[8].shape[1]
+    for n in range(8):
+        smalls[n][...] = vec[n:n + 1, :width]
+    smalls[8][...] = vec[8:9, :wide]
+    loss[...] = vec[9:10, 0:1] * scale_by
+    factor[...] = vec[9:10, 1:2]
+    for first, second in zip(ins, outs):
+        first.wait()
+        second.start()
+    for move in outs:
+        move.wait()
 
 
 def hand_out(vec, tw, ow, ew, sw, inp, captions):
     devices = lax.axis_size("tower") * lax.axis_size("dp")
-    feat = tw.shape[1] // 3
-    bigs = (tw, ow, ew, sw)
+    bigs = (inp, sw, ew, tw, ow)
+    feat = inp.shape[1]
     outs = ([(1, 1)] * 2 + [(1, feat // devices)] * 8 + [(1, ew.shape[1] // devices)]
             + [a.shape for a in bigs])
-    whole = lambda dims: pl.BlockSpec(dims, lambda i: (0,) * len(dims))
-    moving = pl.BlockSpec((BLK, feat), lambda i: (i, 0))
+    moves = 4 + inp.shape[0] // BLK
+    vspec = pl.BlockSpec(memory_space=pltpu.VMEM)
+    anyw = pl.BlockSpec(memory_space=pl.ANY)
     return pl.pallas_call(
         functools.partial(hand_out_kernel, 1.0 / captions),
-        grid=(inp.shape[0] // BLK,),
-        in_specs=[whole(vec.shape)] + [whole(a.shape) for a in bigs] + [moving],
-        out_specs=[whole(dims) for dims in outs] + [moving],
-        out_shape=[jax.ShapeDtypeStruct(dims, f32) for dims in outs + [inp.shape]],
+        in_specs=[vspec] + [anyw] * 5,
+        out_specs=[vspec] * 11 + [anyw] * 5,
+        out_shape=[jax.ShapeDtypeStruct(dims, f32) for dims in outs],
+        scratch_shapes=[pltpu.VMEM(a.shape, f32) for a in bigs]
+        + [pltpu.SemaphoreType.DMA((moves,)), pltpu.SemaphoreType.DMA((moves,))],
         name="hand_out",
-    )(vec, *bigs, inp)
+    )(vec, *bigs)
 
 
 def local_fast(tokens, segments, caption_image, logit_scale, first_gain, first_bias, triple_weight, query_bias,
@@ -831,17 +897,18 @@
     rows_here, length, feat = tokens.shape[1:]
     flat = tokens[0].reshape(rows_here * length, feat)
     w3, wo, we, ws = triple_weight[0], output_weight[0], expand_weight[0], shrink_weight[0]
-    qkv, probs, mixed, hidden, act, slope, member, pooled, count = forward(
+    qkv, probs, mixed, normed, sums, slope, n1, n2, spread, member, pooled, count, table = forward(
         flat, segments, first_gain, first_bias, w3, query_bias, value_bias, wo, output_bias,
         second_gain, second_bias, we, expand_bias, ws, shrink_bias)
-    tw, ow, ew, sw, inp, vec = backward(member, pooled, count, caption_image, logit_scale, first_gain, first_bias,
-                                        second_gain, second_bias, qkv, probs, mixed, hidden, act, slope, flat,
+    sums = sums.reshape(2, PLANE, 2, sums.shape[0] // (4 * PLANE), sums.shape[1])
+    tw, ow, ew, sw, inp, vec = backward(member, pooled, count, table, sums, caption_image.T, logit_scale, first_gain, first_bias,
+                                        second_gain, second_bias, qkv, probs, mixed, normed, slope, n1, n2, spread, flat,
                                         w3, wo, we, ws)
     captions = rows_here * CAPS * lax.axis_size("dp")
     outs = hand_out(vec, tw, ow, ew, sw, inp, captions)
     loss, factor = outs[0].reshape(1), outs[1].reshape(1)
     g1, b1, qb, vb, ob, g2, b2, sb, eb = (a.reshape(-1) for a in outs[2:11])
-    tw, ow, ew, sw, inp = outs[11:]
+    inp, sw, ew, tw, ow = outs[11:]
     return (loss, factor, inp.reshape(1, rows_here, length, feat), g1, b1, tw, qb, vb, ow, ob, g2, b2, ew, eb, sw, sb)
 
 

time: 149 us -> 127 us (0.85)
  Pallas kernels: 144 us -> 124 us
    pallas_call x2, Pallas kernels: 110 us -> 83.1 us  [the longest x1 78.6 us: backward(): pl.pallas_call(bwd_kernel, in_specs=[vspec] * 6 + [sspec] + [vspec] * 4 +...]
    pallas_call x1, Pallas kernels: 33.9 us -> 40.6 us  [forward(): pl.pallas_call(fwd_kernel, grid=(steps,), in_specs=[rows(feat), whole(seg...]
where the time goes in v4:
time: 127 us; the launch traced here: 125 us
  Pallas kernels  124 us (98%)
  between operations  1.49 us (1%)
    pallas_call x1, Pallas kernels, backward(): pl.pallas_call(bwd_kernel, in_specs=[vspec] * 6 + [sspec] + [vspec] * 4 +...  78.6 us
    pallas_call x1, Pallas kernels, forward(): pl.pallas_call(fwd_kernel, grid=(steps,), in_specs=[rows(feat), whole(seg...  40.6 us
    pallas_call x1, Pallas kernels, hand_out(): pl.pallas_call(functools.partial(hand_out_kernel, 1.0 / captions), in_spe...  4.47 us

profile of v4, /device:TPU:25, one launch (start us, length us, event | category | flops | bytes accessed | tf_op | source)
XLA Modules:
  0.0 125.2 jit_solution(8836044524830601104)
XLA Ops:
  1.3 40.6 %fwd.1 = (bf16[1024,2304]{1,0:T(8,128)(2,1)}, bf16[1024,1536]{1,0:T(8,128)(2,1)}, bf16[1024,768]{1,0:T(8,128)(2,1)}, f32[1024,768]{1,0:T(8,128)}, bf16[3072,128]...) custom-call(bf16[1024,768]{1,0:T(8,128)(2,1)} %bitcast.25, ...), custom_call_target="tpu_custom_call" | custom-call | tf_op jit(solution)/shard_map/fwd/pallas_call | solution.py:203
  41.9 78.6 %bwd.1 = (f32[24,2304]{1,0:T(8,128)}, f32[24,768]{1,0:T(8,128)}, f32[24,3072]{1,0:T(8,128)}, f32[96,768]{1,0:T(8,128)}, f32[1024,768]{1,0:T(8,128)}, /*index=5*/f32[16,128]{1,0:T(8,128)}) custom-call(bf16[64,1024]{1,0:T(8,128)(2,1)} %get-tuple-element.51.member, f32[64,768]{1,0:T(8,128)} %get-tuple-element.52.pooled, f32[64,128]{1,0:T(8,128)} %get-tuple-element.53.count, ...), custom_call_target="tpu_custom_call" | custom-call | tf_op jit(solution)/shard_map/bwd/pallas_call | solution.py:834
  120.6 4.5 %hand_out.1 = (f32[1,1]{1,0:T(1,128)}, f32[1,1]{1,0:T(1,128)}, f32[1,24]{1,0:T(1,128)}, f32[1,24]{1,0:T(1,128)}, f32[1,24]{1,0:T(1,128)}, /*index=5*/f32[1,24]{1...) custom-call(f32[16,128]{1,0:T(8,128)} %get-tuple-element.64.vec, ...), custom_call_target="tpu_custom_call" | custom-call | tf_op jit(solution)/shard_map/hand_out/pallas_call | solution.py:883

commit v5 on v4

--- a/solution.py
+++ b/solution.py
@@ -47,8 +47,9 @@
 
 
 def fwd_kernel(tok, seg, g1, b1, qb, vb, ob, g2, b2, eb, sb, w3h, woh, weh, wsh,
-               qkv, probs, mixed, normed_out, sums_out, slope, n1_out, n2_out, spread_out, member_out, pooled_out, count_out, table_out,
-               w3, wo, we, ws, pool_acc, count_acc, act_sum, imgs, elow, sems, gsem, esem):
+               qkv_h, probs_h, mixed_h, normed_h, sums_out, slope_h, n1_h, n2_h, spread_out, member_out, pooled_out, count_out, table_out,
+               w3, wo, we, ws, pool_acc, count_acc, act_sum, imgs, elow, out_acc,
+               qkv_b, probs_b, mixed_b, normed_b, slope_b, n1_b, n2_b, sems, gsem, esem, osem):
     i = pl.program_id(0)
     steps = pl.num_programs(0)
     rows_here, length = seg.shape
@@ -70,12 +71,34 @@
         return pltpu.make_async_remote_copy(src_ref=src, dst_ref=dst, send_sem=sem.at[0], recv_sem=sem.at[1],
                                             device_id=dev, device_id_type=MESH)
 
+    slot = lax.rem(i, 2)
+    saved = ((qkv_b, qkv_h), (probs_b, probs_h), (mixed_b, mixed_h), (normed_b, normed_h), (slope_b, slope_h),
+             (n1_b, n1_h), (n2_b, n2_h))
+    qkv, probs, mixed, normed_out, slope, n1_out, n2_out = (buf.at[slot] for buf, _ in saved)
+
+    def save(n, step):
+        buf, out = saved[n]
+        at = lax.rem(step, 2)
+        return pltpu.make_async_copy(buf.at[at], out.at[pl.ds(pl.multiple_of(step * block, block), block)],
+                                     osem.at[at, n])
+
+    def leave(*which):
+        @pl.when(is_text)
+        def _():
+            for n in which:
+                save(n, i).start()
+
+    @pl.when(is_text & (i >= 2))
+    def _():
+        for n in range(len(saved)):
+            save(n, i - 2).wait()
+
     barrier = pltpu.get_barrier_semaphore()
 
     @pl.when(i == 0)
     def _():
-        for c in copies:
-            c.start()
+        copies[0].start()
+        copies[1].start()
         for dev in facing + [partner]:
             pl.semaphore_signal(barrier, inc=1, device_id=dev, device_id_type=MESH)
         pool_acc[...] = jnp.zeros_like(pool_acc)
@@ -91,10 +114,18 @@
     norm, _ = stats(x)
     n1 = (norm * g1[...].astype(f32) + b1[...].astype(f32)).astype(bf16)
     n1_out[...] = n1
+    leave(5)
     arrive(0)
+
+    @pl.when(i == 0)
+    def _():
+        copies[2].start()
+        copies[3].start()
     qkv[:, :feat] = (mm(n1, w3[:, :feat]) + qb[...].astype(f32)).astype(bf16)
     qkv[:, feat:2 * feat] = mm(n1, w3[:, feat:2 * feat]).astype(bf16)
     qkv[:, 2 * feat:] = (mm(n1, w3[:, 2 * feat:]) + vb[...].astype(f32)).astype(bf16)
+
+    leave(0)
 
     image_seg = (lax.broadcasted_iota(jnp.int32, (1, length), 1) >= IMG_TOK).astype(jnp.int32)
     row_segs = []
@@ -127,6 +158,7 @@
             o = mm_tn(lows[h], qkv[here, 2 * feat + 128 * h:2 * feat + 128 * h + 128])
             mixed[here, 128 * h:128 * h + 128] = jnp.where(first_half, o[:128], o[128:]).astype(bf16)
 
+    leave(1, 2)
     arrive(1)
     hid = x + mm(mixed[...], wo[...]) + ob[...].astype(f32)
     norm2, spread2 = stats(hid)
@@ -134,6 +166,7 @@
     spread_out[...] = spread2
     n2 = (norm2 * g2[...].astype(f32) + b2[...].astype(f32)).astype(bf16)
     n2_out[...] = n2
+    leave(3, 6)
     slot_row = jnp.concatenate(slot_lanes, axis=1)
     hot = (lax.broadcasted_iota(jnp.int32, (slots, block), 0) == slot_row)
     member = hot.astype(f32).astype(bf16)
@@ -141,22 +174,36 @@
     placed = placed.astype(f32).astype(bf16)
     arrive(2)
     arrive(3)
-    out = hid + sb[...].astype(f32)
+    base = hid + sb[...].astype(f32)
     tile = 768
-    starts = range(0, we.shape[1], tile)
-    ahead = mm(n2, we[:, :tile])
-    for f in starts:
-        v = ahead + eb[:, f:f + tile].astype(f32)
-        if f + tile < we.shape[1]:
-            ahead = mm(n2, we[:, f + tile:f + 2 * tile])
-        v2 = v * v
-        cv = v * GELU_C
-        t = jnp.tanh(cv * (1.0 + GELU_A * v2))
-        h = 0.5 + 0.5 * t
-        a = (v * h).astype(bf16)
-        act_sum[:, f:f + tile] += mm(placed, a)
-        slope[:, f:f + tile] = (h + h * (1.0 - h) * ((2.0 * cv) * (1.0 + (3.0 * GELU_A) * v2))).astype(bf16)
-        out = out + mm(a, ws[f:f + tile, :])
+    width = we.shape[1]
+
+    def feed_forward(keep):
+        out = base
+        ahead = mm(n2, we[:, :tile])
+        for f in range(0, width, tile):
+            v = ahead + eb[:, f:f + tile].astype(f32)
+            if f + tile < width:
+                ahead = mm(n2, we[:, f + tile:f + 2 * tile])
+            v2 = v * v
+            cv = v * GELU_C
+            h = 0.5 + 0.5 * jnp.tanh(cv * (1.0 + GELU_A * v2))
+            a = (v * h).astype(bf16)
+            if keep:
+                act_sum[:, f:f + tile] += mm(placed, a)
+                slope[:, f:f + tile] = (h + h * (1.0 - h) * ((2.0 * cv) * (1.0 + (3.0 * GELU_A) * v2))).astype(bf16)
+            out = out + mm(a, ws[f:f + tile, :])
+        out_acc[...] = out
+
+    @pl.when(is_text)
+    def _():
+        feed_forward(True)
+    leave(4)
+
+    @pl.when(tower == 0)
+    def _():
+        feed_forward(False)
+    out = out_acc[...]
     member_out[...] = member
     out_hi, out_lo = low_pair(out)
     pool_acc[...] += mm(member, out_hi) + mm(member, out_lo)
@@ -167,8 +214,6 @@
         counts = jnp.maximum(count_acc[...], 1.0)
         pooled = pool_acc[...] / counts[:, :1]
         count_out[...] = counts
-        for f in range(0, we.shape[1], tile):
-            sums_out[f:f + tile, :] = act_sum[:, f:f + tile].astype(bf16).T
         pooled_out[...] = pooled
         pl.semaphore_wait(barrier, chips + 1)
 
@@ -182,10 +227,15 @@
 
         @pl.when(tower == 1)
         def _():
+            for f in range(0, width, tile):
+                sums_out[f:f + tile, :] = act_sum[:, f:f + tile].astype(bf16).T
             remote(imgs.at[core], imgs.at[core], gsem, partner).wait_recv()
             remote(imgs.at[core], imgs.at[core], esem, partner).start()
             remote(imgs.at[other], imgs.at[other], esem, partner).wait()
             table_out[...] = imgs[...]
+            for n in range(len(saved)):
+                save(n, i - 1).wait()
+                save(n, i).wait()
 
 
 def forward(tokens, segments, g1, b1, w3, qb, vb, wo, ob, g2, b2, we, eb, ws, sb):
@@ -204,9 +254,8 @@
         fwd_kernel,
         grid=(steps,),
         in_specs=[rows(feat), whole(segments)] + [whole(a) for a in smalls] + [anyw] * 4,
-        out_specs=[rows(3 * feat),
-                   rows(2 * feat),
-                   rows(feat), rows(feat), pl.BlockSpec((ff, 2 * slots), lambda i: (0, 0)), rows(ff), rows(feat), rows(feat), rows(1),
+        out_specs=[anyw] * 4 + [pl.BlockSpec((ff, 2 * slots), lambda i: (0, 0))] + [anyw] * 3 + [
+                   rows(1),
                    pl.BlockSpec((slots, block), lambda i: (0, i)),
                    pl.BlockSpec((slots, feat), lambda i: (0, 0)),
                    pl.BlockSpec((slots, 128), lambda i: (0, 0)),
@@ -226,8 +275,13 @@
                    jax.ShapeDtypeStruct(table, bf16)],
         scratch_shapes=[pltpu.VMEM(w3.shape, bf16), pltpu.VMEM(wo.shape, bf16), pltpu.VMEM(we.shape, bf16),
                         pltpu.VMEM(ws.shape, bf16), pltpu.VMEM((slots, feat), f32), pltpu.VMEM((slots, 128), f32), pltpu.VMEM((2 * slots, ff), f32),
-                        pltpu.VMEM(table, bf16), pltpu.VMEM((rows_here, feat), bf16),
-                        pltpu.SemaphoreType.DMA((4,)), pltpu.SemaphoreType.DMA((2,)), pltpu.SemaphoreType.DMA((2,))],
+                        pltpu.VMEM(table, bf16), pltpu.VMEM((rows_here, feat), bf16), pltpu.VMEM((block, feat), f32),
+                        pltpu.VMEM((2, block, 3 * feat), bf16), pltpu.VMEM((2, block, 2 * feat), bf16),
+                        pltpu.VMEM((2, block, feat), bf16), pltpu.VMEM((2, block, feat), f32),
+                        pltpu.VMEM((2, block, ff), bf16), pltpu.VMEM((2, block, feat), bf16),
+                        pltpu.VMEM((2, block, feat), bf16),
+                        pltpu.SemaphoreType.DMA((4,)), pltpu.SemaphoreType.DMA((2,)), pltpu.SemaphoreType.DMA((2,)),
+                        pltpu.SemaphoreType.DMA((2, 7))],
         compiler_params=pltpu.CompilerParams(vmem_limit_bytes=56 << 20, dimension_semantics=("arbitrary",),
                                              collective_id=1, has_side_effects=True),
         name="fwd",
@@ -241,10 +295,31 @@
 HALF = CH // 2
 ROWS = HALF // PLANE
 N_CH = 8
-WIDE = (0, 1, 3, 6)
-LONG = (2, 4, 5, 7)
+WIDE = (0, 2, 4, 7)
+LONG = (1, 3, 5)
+DEEP = (6,)
+TEXT_PLAN = {
+    ("ga", 1): (("cross",), ("leave", 0),),
+    ("ga", 2): (("leave", 1),),
+    ("ew", 2): (("mid", 0),),
+    ("ga", 3): (("leave", 2),),
+    "ow": (("mid", 1), ("leave", 3),),
+    ("attn", 0): (("mid", 2), ("leave", 4),),
+    ("attn", 5): (("share",),),
+    ("tw", 0): (("mid", 3), ("rows",), ("finish", 0),),
+    ("tw", 1): (("leave", 5),),
+    ("tw", 2): (("mid", 4), ("finish", 1),),
+    ("gn1", 0): (("leave", 6),),
+    ("gn1", 1): (("finish", 2), ("leave", 7),),
+    ("gn1", 3): (("finish", 3), ("mid", 5),),
+    "end": (("mid", 6), ("mid", 7), ("finish", 6), ("finish", 4), ("finish", 5), ("finish", 7),),
+}
+IMAGE_PLAN = (
+    ("over", 0), ("mid", 0), ("over", 2), ("over", 1), ("mid", 2), ("finish", 0), ("over", 4), ("over", 3), ("finish", 1), ("mid", 4), ("finish", 2), ("over", 7), ("over", 5), ("rows",), ("finish", 3), ("finish", 4), ("mid", 7), ("finish", 5), ("take", 6), ("finish", 7),
+)
 WIDE_AT = {q: n for n, q in enumerate(WIDE)}
-LONG_AT = {q: n for n, q in enumerate(LONG)}
+LONG_AT = {q: n for n, q in enumerate(LONG + DEEP)}
+DEEP_AT = {q: n for n, q in enumerate(DEEP)}
 
 
 def fold(x):
@@ -254,7 +329,7 @@
 def bwd_kernel(member, pooled, count, imgs, act_sums, caption, scale, g1, b1, g2, b2,
                qkv_h, probs_h, mixed_h, normed_h, slope_h, n1_h, n2_h, spread_h, tok_h, w3_h, wo_h, we_h, ws_h,
                tw_out, ow_out, ew_out, sw_out, in_out, vec_out,
-               cs, snd, prv, own, ylong, ywide, zrcv, fin, apair, asum, aall, gpall, swfin, xsw,
+               cs, snd, prv, own, ylong, ywide, zrcv, zdeep, xfin, fin, apair, asum, aall, gpall, swfin, xsw,
                gol, gn2, hid, spread2, n2b, tok, mixed, probs, slope, ws, we, ge, qkv, w3, wo,
                ebsum, attn_sum, vec, vown, vpair, vrcv,
                ld, psend, precv, xsend, xrecv, ysend, yrecv, zsend, zrecv,
@@ -308,11 +383,15 @@
     def x_line(q):
         return remote(cs.at[q, 0:LINE, y], cs.at[q, 0:LINE, y], xsend.at[q], xrecv.at[q], across)
 
+    def x_sum(q):
+        n = DEEP_AT[q]
+        return remote(xfin.at[n], xfin.at[n], xsend.at[q], xrecv.at[q], across)
+
     def x_copy(q):
-        return x_all(q) if q in WIDE else x_line(q)
+        return x_all(q) if q in WIDE else x_line(q) if q in LONG else x_sum(q)
 
     def y_copy(q):
-        if q in LONG:
+        if q not in WIDE:
             src, dst = cs.at[q, :, 1 - y], ylong.at[LONG_AT[q]]
         else:
             src, dst = cs.at[q, pl.ds(LINE * t, LINE), 1 - y], ywide.at[WIDE_AT[q]]
@@ -323,16 +402,24 @@
             to = lax.rem(z + k, LINE)
             remote(cs.at[q, LINE * t + to, y], zrcv.at[q, k - 1], zsend.at[q], zrecv.at[q],
                    at_core(t, 2 * to + y)).start()
+            if q in DEEP:
+                remote(cs.at[q, to, y], zdeep.at[DEEP_AT[q], k - 1], zsend.at[N_CH + DEEP_AT[q]],
+                       zrecv.at[N_CH + DEEP_AT[q]], at_core(t, 2 * to + y)).start()
 
     def z_all(q):
         return remote(zrcv.at[q], zrcv.at[q], zsend.at[q], zrecv.at[q], partner)
 
+    def z_deep(q):
+        n = DEEP_AT[q]
+        return remote(zdeep.at[n], zdeep.at[n], zsend.at[N_CH + n], zrecv.at[N_CH + n], partner)
+
     def mid(q):
         y_copy(q).wait_recv()
-        if q in LONG:
+        if q not in WIDE:
             for a in range(PLANE):
                 cs[q, a, y] = (cs[q, a, y].astype(f32) + ylong[LONG_AT[q], a].astype(f32)).astype(bf16)
-            x_line(q).start()
+            if q in LONG:
+                x_line(q).start()
         else:
             for a in range(LINE):
                 at = LINE * t + a
@@ -343,6 +430,9 @@
         return remote(act_sums.at[:, :, other], apair, asem.at[0], asem.at[1], partner)
 
     def a_start():
+        a_pair().wait_recv()
+        asum[...] = act_sums[:, :, c] + apair[...]
+        aall[:, :, pl.ds(pl.multiple_of(128 * p, 128), 128)] = asum[:, p]
         for k in range(1, PLANE):
             remote(asum.at[:, peer(k)], aall.at[:, :, pl.ds(pl.multiple_of(128 * p, 128), 128)],
                    asem.at[2], asem.at[3], at_core(t, peer(k))).start()
@@ -410,7 +500,20 @@
         total = cs[q, LINE * t + z, y].astype(f32)
         for k in range(LINE - 1):
             total = total + zrcv[q, k].astype(f32)
+        if q in DEEP:
+            z_deep(q).wait_recv()
+            theirs = cs[q, z, y].astype(f32)
+            for k in range(LINE - 1):
+                theirs = theirs + zdeep[DEEP_AT[q], k].astype(f32)
+            xfin[DEEP_AT[q]] = theirs.astype(bf16)
+            x_sum(q).start()
         fin[q] = total
+        keep(q).start()
+        give(q).start()
+
+    def take(q):
+        x_sum(q).wait_recv()
+        fin[q] = xfin[DEEP_AT[q]].astype(f32)
         keep(q).start()
         give(q).start()
 
@@ -483,29 +586,14 @@
                 y_copy(q).start()
             else:
                 z_start(q)
-        over(0)
-        mid(0)
-        over(1)
-        finish(0)
-        mid(1)
-        over(3)
-        finish(1)
-        over(2)
-        mid(3)
-        sw_across().wait_recv()
-        swfin[...] = xsw[...].astype(f32)
-        sw_keep().start()
-        finish(2)
-        over(4)
-        finish(3)
-        finish(4)
-        over(6)
-        over(5)
-        mid(6)
-        finish(5)
-        over(7)
-        finish(6)
-        finish(7)
+
+        def rows_over():
+            sw_across().wait_recv()
+            swfin[...] = xsw[...].astype(f32)
+            sw_keep().start()
+        acts = {"over": over, "mid": mid, "finish": finish, "take": take, "rows": rows_over}
+        for what, *of in IMAGE_PLAN:
+            acts[what](*of)
         for m in range(blocks):
             pltpu.make_async_copy(gn2.at[0:BLK], in_out.at[pl.ds(BLK * m, BLK)], outsem.at[m]).wait()
 
@@ -542,9 +630,6 @@
         hot = (lax.broadcasted_iota(jnp.int32, dots.shape, 1) == wanted).astype(f32)
         picked = jnp.sum(logits * hot, axis=1, keepdims=True)
         loss_here = jnp.sum(peak + jnp.log(total) - picked, axis=0, keepdims=True)
-        a_pair().wait_recv()
-        asum[...] = act_sums[:, :, c] + apair[...]
-        aall[:, :, pl.ds(pl.multiple_of(128 * p, 128), 128)] = asum[:, p]
         a_start()
         grad_logits = weight / total - hot
         factor_here = jnp.sum(jnp.sum(grad_logits * dots, axis=1, keepdims=True), axis=0, keepdims=True)
@@ -560,16 +645,23 @@
         for m in range(blocks):
             gol[BLK * m:BLK * (m + 1), :] = mm_tn(member[:, BLK * m:BLK * (m + 1)], gp_hi).astype(bf16)
 
+        acts = {"leave": leave, "mid": mid, "finish": finish, "cross": gp_line, "share": gp_share, "rows": shrink}
+
+        def now(place):
+            for what, *of in TEXT_PLAN.get(place, ()):
+                acts[what](*of)
+
+        def now_in(loop, index, count):
+            for n in range(count):
+                if (loop, n) in TEXT_PLAN:
+                    pl.when(index == n)(functools.partial(now, (loop, n)))
+
         @pl.loop(0, 4)
         def _(i):
             s = lax.rem(i, 2)
             for cp in tile_loads(i):
                 cp.wait()
 
-            def at(n, what, *of):
-                @pl.when(i == n)
-                def _():
-                    what(*of)
             sums = jnp.zeros((8, feat), f32)
             for m in range(blocks):
                 here = slice(BLK * m, BLK * (m + 1))
@@ -579,20 +671,17 @@
             sums = jnp.sum(sums, axis=0, keepdims=True)
             for h in range(2):
                 ebsum[:, pl.ds(pl.multiple_of(4 * HALF * h + HALF * i, 128), HALF)] = sums[:, HALF * h:HALF * (h + 1)]
-            at(1, gp_line)
-            at(1, leave, 0)
-            at(2, leave, 1)
-            at(3, leave, 2)
+            now_in("ga", i, 4)
 
             @pl.when(i == 0)
             def _():
                 n2_load.wait()
             chunk(i, n2b, ge[...])
-            at(2, mid, 0)
-            at(3, mid, 1)
+            now_in("ew", i, 4)
             for m in range(blocks):
                 here = slice(BLK * m, BLK * (m + 1))
                 gn2[here, :] += mm_nt(ge[here, :], we[s])
+            now_in("gn", i, 4)
 
             @pl.when(i < 2)
             def _():
@@ -621,14 +710,16 @@
             vec[row:row + 1, :] = jnp.sum(x, axis=0, keepdims=True)
         for n in range(4):
             vec[8 + n:9 + n, :] = ebsum[:, feat * n:feat * (n + 1)]
-        leave(3)
+        now("norm")
 
         mixed_load.wait()
         chunk(4, mixed, gol[...])
+        now("ow")
         wo_load.wait()
         for m in range(blocks):
             here = slice(BLK * m, BLK * (m + 1))
             ge[here, :] = mm_nt(gol[here, :], wo[...]).astype(bf16)
+        now("gm")
 
         qkv_load.wait()
         probs_load.wait()
@@ -663,18 +754,7 @@
                 for n, x in ((0, gq[h]), (1, gv[h])):
                     attn_sum[:, feat * n + 128 * h:feat * n + 128 * h + 128] += fold(x)
 
-            @pl.when(rp == 1)
-            def _():
-                leave(4)
-                mid(2)
-
-            @pl.when(rp == 4)
-            def _():
-                gp_share()
-
-            @pl.when(rp == 5)
-            def _():
-                mid(3)
+            now_in("attn", rp, count_t // 128)
         vec[2:3, :] = jnp.sum(attn_sum[:, :feat], axis=0, keepdims=True)
         vec[3:4, :] = jnp.sum(attn_sum[:, feat:], axis=0, keepdims=True)
 
@@ -684,16 +764,7 @@
         def _(j):
             chunk(5 + j, slope.at[1], qkv[:, pl.ds(pl.multiple_of(CH * j, 128), CH)])
 
-            @pl.when(j == 0)
-            def _():
-                shrink()
-                finish(0)
-
-            @pl.when(j == 1)
-            def _():
-                leave(5)
-        finish(1)
-        mid(4)
+            now_in("tw", j, 3)
         tok_load.wait()
         w3_load.wait()
 
@@ -701,22 +772,7 @@
             here = pl.ds(pl.multiple_of(m * BLK, BLK), BLK)
             g_in = mm_nt(qkv[here, :], w3[...])
 
-            @pl.when(m == 0)
-            def _():
-                leave(6)
-                finish(2)
-
-            @pl.when(m == 1)
-            def _():
-                leave(7)
-
-            @pl.when(m == 2)
-            def _():
-                finish(3)
-
-            @pl.when(m == 3)
-            def _():
-                mid(5)
+            now_in("gn1", m, blocks)
             norm, spread = stats(tok[here, :].astype(f32))
             g = g_in * gain1
             back = spread * (g - jnp.mean(g, axis=1, keepdims=True)
@@ -741,8 +797,7 @@
             vown[g % 2, g // 2, 8:9, :] = tail
             vown[g % 2, g // 2, 9:10, :] = scalars
         v_pair().start()
-        finish(4)
-        mid(6)
+        now("small")
         for m in range(blocks):
             here = pl.ds(BLK * m, BLK)
             pltpu.make_async_copy(gn2.at[here], in_out.at[here], outsem.at[m]).wait()
@@ -753,10 +808,7 @@
                 if tt == 0 or k:
                     remote(vown.at[c, PLANE * tt + peer(k)], vrcv.at[k], vsem.at[0], vsem.at[1],
                            at_core(tt, peer(k))).start()
-        finish(5)
-        mid(7)
-        finish(6)
-        finish(7)
+        now("end")
 
     @pl.when(is_text)
     def _():
@@ -784,8 +836,11 @@
 
         for q in range(N_CH):
             x_copy(q).wait_send()
-        for q in LONG:
+        for q in LONG + DEEP:
             y_copy(q).wait_send()
+        for q in DEEP:
+            z_deep(q).wait_send()
+            z_all(q).wait_send()
         a_pair().wait_send()
         a_all().wait_send()
         gp_beside().wait_send()
@@ -794,7 +849,7 @@
         sw_across().wait_send()
     for q in WIDE:
         y_copy(q).wait_send()
-    for q in range(N_CH):
+    for q in WIDE + LONG:
         z_all(q).wait_send()
     sw_keep().wait()
     lower = fin.at[:, 0:half_rows]
@@ -812,13 +867,14 @@
     sspec = pl.BlockSpec(memory_space=pltpu.SMEM)
     anyw = pl.BlockSpec(memory_space=pl.ANY)
     shape = jax.ShapeDtypeStruct
-    long, wide = len(LONG), len(WIDE)
+    long, wide, deep = len(LONG + DEEP), len(WIDE), len(DEEP)
     apart = sums.shape[:2] + sums.shape[3:]
     slots = member.shape[0]
     scratch = [
         vm((N_CH, PLANE, 2, ROWS, HALF), bf16), vm((2, CH, HALF), bf16), vm((N_CH, CH, HALF), bf16),
         vm((2, CH, HALF), f32),
-        vm((long, PLANE, ROWS, HALF), bf16), vm((wide, LINE, ROWS, HALF), bf16), vm((N_CH, LINE - 1, ROWS, HALF), bf16),
+        vm((max(long, 1), PLANE, ROWS, HALF), bf16), vm((max(wide, 1), LINE, ROWS, HALF), bf16), vm((N_CH, LINE - 1, ROWS, HALF), bf16),
+        vm((max(deep, 1), LINE - 1, ROWS, HALF), bf16), vm((max(deep, 1), ROWS, HALF), bf16),
         vm((N_CH, ROWS, HALF), f32), vm(apart, bf16), vm(apart, bf16), vm((2, apart[2], PLANE * 128), bf16),
         vm((PLANE, 2, slots, feat), bf16), vm((2 * ROWS, feat), f32), vm((2 * ROWS, feat), bf16),
         vm((n_tok, feat), bf16), vm((n_tok, feat), f32), vm((n_tok, feat), f32), vm((n_tok, 1), f32),
@@ -828,7 +884,7 @@
         vm((1, ff), f32), vm((8, 2 * feat), f32),
         vm((16, feat), f32), vm((2, 2 * PLANE, 16, 128), f32), vm((2 * PLANE, 16, 128), f32), vm((PLANE, 16, 128), f32),
         dma((27,)), dma((2,)), dma((N_CH,)), dma((N_CH,)), dma((N_CH,)), dma((N_CH,)), dma((N_CH,)),
-        dma((N_CH,)), dma((N_CH,)), dma((3,)), dma((4,)), dma((6,)), dma((3,)), dma((2,)), dma((2,)),
+        dma((N_CH + deep,)), dma((N_CH + deep,)), dma((3,)), dma((4,)), dma((6,)), dma((3,)), dma((2,)), dma((2,)),
         dma((n_tok // BLK,)),
     ]
     return pl.pallas_call(

time: 127 us -> 122 us (0.961); the launches traced: 125 us -> 122 us
  Pallas kernels: 124 us -> 120 us
    pallas_call x1, Pallas kernels: 40.6 us -> 36.2 us  [forward(): pl.pallas_call(fwd_kernel, grid=(steps,), in_specs=[rows(feat), whole(seg...]
where the time goes in v5:
time: 122 us
  Pallas kernels  120 us (98%)
  between operations  1.49 us (1%)
    pallas_call x1, Pallas kernels, backward(): pl.pallas_call(bwd_kernel, in_specs=[vspec] * 6 + [sspec] + [vspec] * 4 +...  79.4 us
    pallas_call x1, Pallas kernels, forward(): pl.pallas_call(fwd_kernel, grid=(steps,), in_specs=[rows(feat), whole(seg...  36.2 us
    pallas_call x1, Pallas kernels, hand_out(): pl.pallas_call(functools.partial(hand_out_kernel, 1.0 / captions), in_spe...  4.47 us

profile of v5, /device:TPU:25, one launch (start us, length us, event | category | flops | bytes accessed | tf_op | source)
XLA Modules:
  0.0 121.5 jit_solution(7720157254569901800)
XLA Ops:
  1.3 36.2 %fwd.1 = (bf16[1024,2304]{1,0:T(8,128)(2,1)}, bf16[1024,1536]{1,0:T(8,128)(2,1)}, bf16[1024,768]{1,0:T(8,128)(2,1)}, f32[1024,768]{1,0:T(8,128)}, bf16[3072,128]...) custom-call(bf16[1024,768]{1,0:T(8,128)(2,1)} %bitcast.25, ...), custom_call_target="tpu_custom_call" | custom-call | tf_op jit(solution)/shard_map/fwd/pallas_call | solution.py:253
  37.5 79.4 %bwd.1 = (f32[24,2304]{1,0:T(8,128)}, f32[24,768]{1,0:T(8,128)}, f32[24,3072]{1,0:T(8,128)}, f32[96,768]{1,0:T(8,128)}, f32[1024,768]{1,0:T(8,128)}, /*index=5*/f32[16,128]{1,0:T(8,128)}) custom-call(bf16[64,1024]{1,0:T(8,128)(2,1)} %get-tuple-element.51.member, f32[64,768]{1,0:T(8,128)} %get-tuple-element.52.pooled, f32[64,128]{1,0:T(8,128)} %get-tuple-element.53.count, ...), custom_call_target="tpu_custom_call" | custom-call | tf_op jit(solution)/shard_map/bwd/pallas_call | solution.py:890
  116.9 4.5 %hand_out.1 = (f32[1,1]{1,0:T(1,128)}, f32[1,1]{1,0:T(1,128)}, f32[1,24]{1,0:T(1,128)}, f32[1,24]{1,0:T(1,128)}, f32[1,24]{1,0:T(1,128)}, /*index=5*/f32[1,24]{1...) custom-call(f32[16,128]{1,0:T(8,128)} %get-tuple-element.64.vec, ...), custom_call_target="tpu_custom_call" | custom-call | tf_op jit(solution)/shard_map/hand_out/pallas_call | solution.py:939

commit v6 on v5

--- a/solution.py
+++ b/solution.py
@@ -48,7 +48,7 @@
 
 def fwd_kernel(tok, seg, g1, b1, qb, vb, ob, g2, b2, eb, sb, w3h, woh, weh, wsh,
                qkv_h, probs_h, mixed_h, normed_h, sums_out, slope_h, n1_h, n2_h, spread_out, member_out, pooled_out, count_out, table_out,
-               w3, wo, we, ws, pool_acc, count_acc, act_sum, imgs, elow, out_acc,
+               w3, wo, we, ws, pool_acc, count_acc, act_sum, imgs, elow,
                qkv_b, probs_b, mixed_b, normed_b, slope_b, n1_b, n2_b, sems, gsem, esem, osem):
     i = pl.program_id(0)
     steps = pl.num_programs(0)
@@ -83,10 +83,8 @@
                                      osem.at[at, n])
 
     def leave(*which):
-        @pl.when(is_text)
-        def _():
-            for n in which:
-                save(n, i).start()
+        for n in which:
+            save(n, i).start()
 
     @pl.when(is_text & (i >= 2))
     def _():
@@ -110,76 +108,94 @@
         def _():
             copies[n].wait()
 
-    x = tok[...].astype(f32)
-    norm, _ = stats(x)
-    n1 = (norm * g1[...].astype(f32) + b1[...].astype(f32)).astype(bf16)
-    n1_out[...] = n1
-    leave(5)
-    arrive(0)
-
-    @pl.when(i == 0)
-    def _():
-        copies[2].start()
-        copies[3].start()
-    qkv[:, :feat] = (mm(n1, w3[:, :feat]) + qb[...].astype(f32)).astype(bf16)
-    qkv[:, feat:2 * feat] = mm(n1, w3[:, feat:2 * feat]).astype(bf16)
-    qkv[:, 2 * feat:] = (mm(n1, w3[:, 2 * feat:]) + vb[...].astype(f32)).astype(bf16)
-
-    leave(0)
-
-    image_seg = (lax.broadcasted_iota(jnp.int32, (1, length), 1) >= IMG_TOK).astype(jnp.int32)
-    row_segs = []
-    for r in range(STEP_ROWS):
-        s = seg[pl.ds(STEP_ROWS * i + r, 1), :]
-        row_segs.append(jnp.where(is_text, s, image_seg))
-    lane = lax.broadcasted_iota(jnp.int32, (128, 128), 1)
-    first_half = lane < 64
-    slot_lanes = []
-    for pair in range(STEP_ROWS // 2):
-        base = STEP_ROWS * i + 2 * pair
-        keyed = jnp.concatenate(
-            [row_segs[2 * pair] * rows_here + base, row_segs[2 * pair + 1] * rows_here + (base + 1)], axis=1)
-        slot_lanes.append(keyed)
-        across = jnp.broadcast_to(keyed.astype(f32), (128, 128))
-        bias = jnp.where(across == across.T, 0.0, -1e30)
-        bias = jnp.concatenate([bias, bias], axis=1)
-        here = slice(pair * 128, pair * 128 + 128)
-        hps = range(HEADS // 2)
-        scores = [mm_nt(qkv[here, feat + 128 * h:feat + 128 * h + 128],
-                        split(qkv[here, 128 * h:128 * h + 128] * jnp.asarray(0.125, bf16), first_half)) + bias
-                  for h in hps]
-        lows = []
-        for h in hps:
-            e = jnp.exp(scores[h] - jnp.max(scores[h], axis=0, keepdims=True))
-            p = (e * (1.0 / jnp.sum(e, axis=0, keepdims=True))).astype(bf16)
-            probs[here, 256 * h:256 * h + 256] = p
-            lows.append(p)
-        for h in hps:
-            o = mm_tn(lows[h], qkv[here, 2 * feat + 128 * h:2 * feat + 128 * h + 128])
-            mixed[here, 128 * h:128 * h + 128] = jnp.where(first_half, o[:128], o[128:]).astype(bf16)
-
-    leave(1, 2)
-    arrive(1)
-    hid = x + mm(mixed[...], wo[...]) + ob[...].astype(f32)
-    norm2, spread2 = stats(hid)
-    normed_out[...] = norm2
-    spread_out[...] = spread2
-    n2 = (norm2 * g2[...].astype(f32) + b2[...].astype(f32)).astype(bf16)
-    n2_out[...] = n2
-    leave(3, 6)
-    slot_row = jnp.concatenate(slot_lanes, axis=1)
-    hot = (lax.broadcasted_iota(jnp.int32, (slots, block), 0) == slot_row)
-    member = hot.astype(f32).astype(bf16)
-    placed = (lax.broadcasted_iota(jnp.int32, (2 * slots, block), 0) == slot_row + slots * core)
-    placed = placed.astype(f32).astype(bf16)
-    arrive(2)
-    arrive(3)
-    base = hid + sb[...].astype(f32)
     tile = 768
     width = we.shape[1]
-
-    def feed_forward(keep):
-        out = base
+    hps = range(HEADS // 2)
+
+    def text_segments(pair):
+        base = STEP_ROWS * i + 2 * pair
+        keyed = jnp.concatenate([seg[pl.ds(base + r, 1), :] * rows_here + (base + r) for r in range(2)], axis=1)
+        across = jnp.broadcast_to(keyed.astype(f32), (128, 128))
+        return keyed, jnp.where(across == across.T, 0.0, -1e30)
+
+    def image_place(index, per_row, first_row):
+        row = jnp.zeros_like(index)
+        for r in range(1, STEP_ROWS):
+            row = row + (index >= r * per_row).astype(jnp.int32)
+        behind = (index - row * per_row >= IMG_TOK).astype(jnp.int32)
+        return behind * rows_here + row + first_row
+
+    def run(keep):
+        per_row = length if keep else -(-IMG_TOK // 8) * 8
+        both = 2 * per_row
+        count = STEP_ROWS * per_row
+        if keep:
+            x = tok[...].astype(f32)
+        else:
+            x = jnp.concatenate([tok[length * r:length * r + per_row, :].astype(f32) for r in range(STEP_ROWS)], axis=0)
+        norm, _ = stats(x)
+        n1 = (norm * g1[...].astype(f32) + b1[...].astype(f32)).astype(bf16)
+        if keep:
+            n1_out[...] = n1
+            leave(5)
+        arrive(0)
+
+        @pl.when(i == 0)
+        def _():
+            copies[2].start()
+            copies[3].start()
+        qkv[:count, :feat] = (mm(n1, w3[:, :feat]) + qb[...].astype(f32)).astype(bf16)
+        qkv[:count, feat:2 * feat] = mm(n1, w3[:, feat:2 * feat]).astype(bf16)
+        qkv[:count, 2 * feat:] = (mm(n1, w3[:, 2 * feat:]) + vb[...].astype(f32)).astype(bf16)
+        if keep:
+            leave(0)
+        first_half = lax.broadcasted_iota(jnp.int32, (both, 128), 1) < 64
+        slot_lanes = []
+        for pair in range(STEP_ROWS // 2):
+            if keep:
+                keyed, bias = text_segments(pair)
+                slot_lanes.append(keyed)
+                bias = jnp.concatenate([bias, bias], axis=1)
+            else:
+                down = lax.broadcasted_iota(jnp.int32, (both, 2 * both), 0)
+                over = lax.broadcasted_iota(jnp.int32, (both, 2 * both), 1)
+                over = jnp.where(over >= both, over - both, over)
+                bias = jnp.where(image_place(down, per_row, 0) == image_place(over, per_row, 0), 0.0, -1e30)
+            here = slice(pair * both, (pair + 1) * both)
+            scores = [mm_nt(qkv[here, feat + 128 * h:feat + 128 * h + 128],
+                            split(qkv[here, 128 * h:128 * h + 128] * jnp.asarray(0.125, bf16), first_half)) + bias
+                      for h in hps]
+            lows = []
+            for h in hps:
+                e = jnp.exp(scores[h] - jnp.max(scores[h], axis=0, keepdims=True))
+                p = (e * (1.0 / jnp.sum(e, axis=0, keepdims=True))).astype(bf16)
+                if keep:
+                    probs[here, 256 * h:256 * h + 256] = p
+                lows.append(p)
+            for h in hps:
+                o = mm_tn(lows[h], qkv[here, 2 * feat + 128 * h:2 * feat + 128 * h + 128])
+                mixed[here, 128 * h:128 * h + 128] = jnp.where(first_half, o[:both], o[both:]).astype(bf16)
+        arrive(1)
+        hid = x + mm(mixed[:count, :], wo[...]) + ob[...].astype(f32)
+        norm2, spread2 = stats(hid)
+        n2 = (norm2 * g2[...].astype(f32) + b2[...].astype(f32)).astype(bf16)
+        if keep:
+            normed_out[...] = norm2
+            spread_out[...] = spread2
+            n2_out[...] = n2
+            leave(1, 2, 3, 6)
+            slot_row = jnp.concatenate(slot_lanes, axis=1)
+        else:
+            slot_row = image_place(lax.broadcasted_iota(jnp.int32, (1, count), 1), per_row, STEP_ROWS * i)
+        hot = (lax.broadcasted_iota(jnp.int32, (slots, count), 0) == slot_row)
+        member = hot.astype(f32).astype(bf16)
+        if keep:
+            member_out[...] = member
+            placed = (lax.broadcasted_iota(jnp.int32, (2 * slots, count), 0) == slot_row + slots * core)
+            placed = placed.astype(f32).astype(bf16)
+        arrive(2)
+        arrive(3)
+        out = hid + sb[...].astype(f32)
         ahead = mm(n2, we[:, :tile])
         for f in range(0, width, tile):
             v = ahead + eb[:, f:f + tile].astype(f32)
@@ -193,21 +209,14 @@
                 act_sum[:, f:f + tile] += mm(placed, a)
                 slope[:, f:f + tile] = (h + h * (1.0 - h) * ((2.0 * cv) * (1.0 + (3.0 * GELU_A) * v2))).astype(bf16)
             out = out + mm(a, ws[f:f + tile, :])
-        out_acc[...] = out
-
-    @pl.when(is_text)
-    def _():
-        feed_forward(True)
-    leave(4)
-
-    @pl.when(tower == 0)
-    def _():
-        feed_forward(False)
-    out = out_acc[...]
-    member_out[...] = member
-    out_hi, out_lo = low_pair(out)
-    pool_acc[...] += mm(member, out_hi) + mm(member, out_lo)
-    count_acc[...] += jnp.broadcast_to(jnp.sum(hot.astype(f32), axis=1, keepdims=True), count_acc.shape)
+        if keep:
+            leave(4)
+        out_hi, out_lo = low_pair(out)
+        pool_acc[...] += mm(member, out_hi) + mm(member, out_lo)
+        count_acc[...] += jnp.broadcast_to(jnp.sum(hot.astype(f32), axis=1, keepdims=True), count_acc.shape)
+
+    pl.when(is_text)(functools.partial(run, True))
+    pl.when(tower == 0)(functools.partial(run, False))
 
     @pl.when(i == steps - 1)
     def _():
@@ -275,7 +284,7 @@
                    jax.ShapeDtypeStruct(table, bf16)],
         scratch_shapes=[pltpu.VMEM(w3.shape, bf16), pltpu.VMEM(wo.shape, bf16), pltpu.VMEM(we.shape, bf16),
                         pltpu.VMEM(ws.shape, bf16), pltpu.VMEM((slots, feat), f32), pltpu.VMEM((slots, 128), f32), pltpu.VMEM((2 * slots, ff), f32),
-                        pltpu.VMEM(table, bf16), pltpu.VMEM((rows_here, feat), bf16), pltpu.VMEM((block, feat), f32),
+                        pltpu.VMEM(table, bf16), pltpu.VMEM((rows_here, feat), bf16),
                         pltpu.VMEM((2, block, 3 * feat), bf16), pltpu.VMEM((2, block, 2 * feat), bf16),
                         pltpu.VMEM((2, block, feat), bf16), pltpu.VMEM((2, block, feat), f32),
                         pltpu.VMEM((2, block, ff), bf16), pltpu.VMEM((2, block, feat), bf16),

time: 122 us -> 120 us (0.984)
    pallas_call x1, Pallas kernels: 36.2 us -> 32.8 us  [forward(): pl.pallas_call(fwd_kernel, grid=(steps,), in_specs=[rows(feat), whole(seg...]
    pallas_call x1, Pallas kernels: 79.4 us -> 81.5 us  [backward(): pl.pallas_call(bwd_kernel, in_specs=[vspec] * 6 + [sspec] + [vspec] * 4 +...]
where the time goes in v6:
time: 120 us
  Pallas kernels  119 us (99%)
  between operations  1.47 us (1%)
    pallas_call x1, Pallas kernels, backward(): pl.pallas_call(bwd_kernel, in_specs=[vspec] * 6 + [sspec] + [vspec] * 4 +...  81.5 us
    pallas_call x1, Pallas kernels, forward(): pl.pallas_call(fwd_kernel, grid=(steps,), in_specs=[rows(feat), whole(seg...  32.8 us
    pallas_call x1, Pallas kernels, hand_out(): pl.pallas_call(functools.partial(hand_out_kernel, 1.0 / captions), in_spe...  4.47 us

profile of v6, /device:TPU:25, one launch (start us, length us, event | category | flops | bytes accessed | tf_op | source)
XLA Modules:
  0.0 120.3 jit_solution(6357024705226322350)
XLA Ops:
  1.3 32.8 %fwd.1 = (bf16[1024,2304]{1,0:T(8,128)(2,1)}, bf16[1024,1536]{1,0:T(8,128)(2,1)}, bf16[1024,768]{1,0:T(8,128)(2,1)}, f32[1024,768]{1,0:T(8,128)}, bf16[3072,128]...) custom-call(bf16[1024,768]{1,0:T(8,128)(2,1)} %bitcast.25, ...), custom_call_target="tpu_custom_call" | custom-call | tf_op jit(solution)/shard_map/fwd/pallas_call | solution.py:262
  34.1 81.5 %bwd.1 = (f32[24,2304]{1,0:T(8,128)}, f32[24,768]{1,0:T(8,128)}, f32[24,3072]{1,0:T(8,128)}, f32[96,768]{1,0:T(8,128)}, f32[1024,768]{1,0:T(8,128)}, /*index=5*/f32[16,128]{1,0:T(8,128)}) custom-call(bf16[64,1024]{1,0:T(8,128)(2,1)} %get-tuple-element.51.member, f32[64,768]{1,0:T(8,128)} %get-tuple-element.52.pooled, f32[64,128]{1,0:T(8,128)} %get-tuple-element.53.count, ...), custom_call_target="tpu_custom_call" | custom-call | tf_op jit(solution)/shard_map/bwd/pallas_call | solution.py:899
  115.6 4.5 %hand_out.1 = (f32[1,1]{1,0:T(1,128)}, f32[1,1]{1,0:T(1,128)}, f32[1,24]{1,0:T(1,128)}, f32[1,24]{1,0:T(1,128)}, f32[1,24]{1,0:T(1,128)}, /*index=5*/f32[1,24]{1...) custom-call(f32[16,128]{1,0:T(8,128)} %get-tuple-element.64.vec, ...), custom_call_target="tpu_custom_call" | custom-call | tf_op jit(solution)/shard_map/hand_out/pallas_call | solution.py:948

commit v7 on v6

--- a/solution.py
+++ b/solution.py
@@ -305,26 +305,27 @@
 ROWS = HALF // PLANE
 N_CH = 8
 WIDE = (0, 2, 4, 7)
-LONG = (1, 3, 5)
-DEEP = (6,)
+LONG = (1, 3, 6)
+DEEP = (5,)
 TEXT_PLAN = {
-    ("ga", 1): (("cross",), ("leave", 0),),
+    ("ga", 1): (("leave", 0),),
+    ("gn", 1): (("cross",),),
     ("ga", 2): (("leave", 1),),
     ("ew", 2): (("mid", 0),),
     ("ga", 3): (("leave", 2),),
     "ow": (("mid", 1), ("leave", 3),),
     ("attn", 0): (("mid", 2), ("leave", 4),),
-    ("attn", 5): (("share",),),
-    ("tw", 0): (("mid", 3), ("rows",), ("finish", 0),),
+    ("tw", 0): (("share",), ("mid", 3),),
     ("tw", 1): (("leave", 5),),
-    ("tw", 2): (("mid", 4), ("finish", 1),),
-    ("gn1", 0): (("leave", 6),),
-    ("gn1", 1): (("finish", 2), ("leave", 7),),
-    ("gn1", 3): (("finish", 3), ("mid", 5),),
-    "end": (("mid", 6), ("mid", 7), ("finish", 6), ("finish", 4), ("finish", 5), ("finish", 7),),
+    ("tw", 2): (("finish", 0), ("mid", 4), ("rows",), ("leave", 6),),
+    ("gn1", 0): (("finish", 1), ("leave", 7),),
+    ("gn1", 2): (("finish", 2),),
+    ("gn1", 3): (("mid", 5),),
+    "small": (("finish", 3),),
+    "end": (("mid", 6), ("mid", 7), ("finish", 5), ("finish", 4), ("finish", 6), ("finish", 7),),
 }
 IMAGE_PLAN = (
-    ("over", 0), ("mid", 0), ("over", 2), ("over", 1), ("mid", 2), ("finish", 0), ("over", 4), ("over", 3), ("finish", 1), ("mid", 4), ("finish", 2), ("over", 7), ("over", 5), ("rows",), ("finish", 3), ("finish", 4), ("mid", 7), ("finish", 5), ("take", 6), ("finish", 7),
+    ("over", 0), ("mid", 0), ("over", 2), ("over", 1), ("mid", 2), ("finish", 0), ("over", 4), ("over", 3), ("finish", 1), ("mid", 4), ("finish", 2), ("over", 7), ("mid", 7), ("rows",), ("finish", 3), ("finish", 4), ("over", 6), ("take", 5), ("finish", 7), ("finish", 6),
 )
 WIDE_AT = {q: n for n, q in enumerate(WIDE)}
 LONG_AT = {q: n for n, q in enumerate(LONG + DEEP)}

time: 120 us -> 119 us (level); the launches traced: 120 us -> 117 us
  Pallas kernels: 119 us -> 116 us
    pallas_call x1, Pallas kernels: 81.5 us -> 78.2 us  [backward(): pl.pallas_call(bwd_kernel, in_specs=[vspec] * 6 + [sspec] + [vspec] * 4 +...]
where the time goes in v7:
time: 119 us; the launch traced here: 117 us
  Pallas kernels  116 us (97%)
  between operations  1.47 us (1%)
    pallas_call x1, Pallas kernels, backward(): pl.pallas_call(bwd_kernel, in_specs=[vspec] * 6 + [sspec] + [vspec] * 4 +...  78.2 us
    pallas_call x1, Pallas kernels, forward(): pl.pallas_call(fwd_kernel, grid=(steps,), in_specs=[rows(feat), whole(seg...  32.8 us
    pallas_call x1, Pallas kernels, hand_out(): pl.pallas_call(functools.partial(hand_out_kernel, 1.0 / captions), in_spe...  4.47 us

profile of v7, /device:TPU:25, one launch (start us, length us, event | category | flops | bytes accessed | tf_op | source)
XLA Modules:
  0.0 117.0 jit_solution(10483824419991269258)
XLA Ops:
  1.3 32.8 %fwd.1 = (bf16[1024,2304]{1,0:T(8,128)(2,1)}, bf16[1024,1536]{1,0:T(8,128)(2,1)}, bf16[1024,768]{1,0:T(8,128)(2,1)}, f32[1024,768]{1,0:T(8,128)}, bf16[3072,128]...) custom-call(bf16[1024,768]{1,0:T(8,128)(2,1)} %bitcast.25, ...), custom_call_target="tpu_custom_call" | custom-call | tf_op jit(solution)/shard_map/fwd/pallas_call | solution.py:262
  34.1 78.2 %bwd.1 = (f32[24,2304]{1,0:T(8,128)}, f32[24,768]{1,0:T(8,128)}, f32[24,3072]{1,0:T(8,128)}, f32[96,768]{1,0:T(8,128)}, f32[1024,768]{1,0:T(8,128)}, /*index=5*/f32[16,128]{1,0:T(8,128)}) custom-call(bf16[64,1024]{1,0:T(8,128)(2,1)} %get-tuple-element.51.member, f32[64,768]{1,0:T(8,128)} %get-tuple-element.52.pooled, f32[64,128]{1,0:T(8,128)} %get-tuple-element.53.count, ...), custom_call_target="tpu_custom_call" | custom-call | tf_op jit(solution)/shard_map/bwd/pallas_call | solution.py:900
  112.4 4.5 %hand_out.1 = (f32[1,1]{1,0:T(1,128)}, f32[1,1]{1,0:T(1,128)}, f32[1,24]{1,0:T(1,128)}, f32[1,24]{1,0:T(1,128)}, f32[1,24]{1,0:T(1,128)}, /*index=5*/f32[1,24]{1...) custom-call(f32[16,128]{1,0:T(8,128)} %get-tuple-element.64.vec, ...), custom_call_target="tpu_custom_call" | custom-call | tf_op jit(solution)/shard_map/hand_out/pallas_call | solution.py:949
